TPU v7x, 512 devices: a whole 4x4x16 slice. The times are simulated.
512 devices in a mesh: seq: 128 (over x, z, core), head: 4 (over y).
Axes of the slice: x: 4, y: 4, z: 16, core: 2. Of those that a mesh axis runs over, the one named last changes fastest.
Arguments:
- query_in: bfloat16 [65536, 256], P('seq', 'head'), may hold values from -6 to 6
- key_in: bfloat16 [65536, 256], P('seq', 'head'), may hold values from -6 to 6
- value_in: bfloat16 [65536, 2048], P('seq', 'head'), may hold values from -8 to 8
- conv_query: float32 [3, 256], P(None, 'head'), may hold values from -3.5 to 3.5
- conv_key: float32 [3, 256], P(None, 'head'), may hold values from -3.5 to 3.5
- conv_value: float32 [3, 2048], P(None, 'head'), may hold values from -3.5 to 3.5
- out_proj: bfloat16 [2048, 2048], P('head'), may hold values from -0.125 to 0.125
- out_grad: bfloat16 [65536, 2048], P(('seq', 'head')), may hold values from -8 to 8
Outputs:
- mixed: bfloat16 [65536, 2048], P(('seq', 'head'))
- grad_query: float32 [65536, 256], P('seq', 'head')
- grad_key: float32 [65536, 256], P('seq', 'head')
- grad_value: float32 [65536, 2048], P('seq', 'head')
- grad_conv_query: float32 [3, 256], P(None, 'head')
- grad_conv_key: float32 [3, 256], P(None, 'head')
- grad_conv_value: float32 [3, 2048], P(None, 'head')
All inputs are finite; a program needn't handle non-finite values.
Results may differ from a plain program's by a relative error of at most 0.0049.
Values may be sent and summed in bfloat16 or wider, within the bound.
No kernel may reach another device: no remote copies, remote signals or barrier semaphores. Data moves between devices by JAX's collectives and lax.ppermute only.
A program may use at most 192 MiB of HBM per device.

v0:
```python
import math

import jax
import jax.numpy as jnp
import numpy as np
from jax import lax
from jax.sharding import PartitionSpec as P

FK = 16
VD = 128


HIGHEST = lax.Precision.HIGHEST


def from_behind(block, axis, distance):
    devices = range(lax.axis_size(axis))
    route = [(i - distance, i) for i in devices if i - distance in devices]
    return lax.ppermute(block, axis, route)


def carried_in(shard, axis, combine, identity, reverse):
    size, index = (lax.axis_size(axis), lax.axis_index(axis))
    everything = jax.tree.map(lambda part: lax.all_gather(part, axis), shard)
    start = jax.tree.map(
        lambda part, zero: jnp.broadcast_to(jnp.asarray(zero, part.dtype), part.shape),
        shard,
        identity,
    )

    def hop(k, before):
        at = size - 1 - k if reverse else k
        reached = at > index if reverse else at < index
        new = combine(before, jax.tree.map(lambda part: part[at], everything))
        return jax.tree.map(lambda a, b: jnp.where(reached, a, b), new, before)

    return lax.fori_loop(0, size, hop, start)


def pair_table(feature_dim):
    mapping = np.zeros(
        (feature_dim * feature_dim, feature_dim * (feature_dim + 1) // 2), np.float32
    )
    column = 0
    for row_index in range(feature_dim):
        for col_index in range(row_index, feature_dim):
            if row_index == col_index:
                mapping[row_index * feature_dim + col_index, column] = 1.0 / math.sqrt(
                    2.0 * feature_dim
                )
            else:
                mapping[row_index * feature_dim + col_index, column] = 1.0 / math.sqrt(feature_dim)
            column = column + 1
    return mapping


def features(inputs):
    head_count = inputs.shape[0]
    feature_dim = inputs.shape[1]
    token_count = inputs.shape[2]
    linear = inputs * feature_dim ** (-0.25)
    products = (inputs[:, :, None, :] * inputs[:, None, :, :]).reshape(
        head_count, feature_dim * feature_dim, token_count
    )
    quadratic = jnp.einsum(
        "pc,hpt->hct", jnp.asarray(pair_table(feature_dim)), products, precision=HIGHEST
    )
    constant = jnp.ones((head_count, 1, token_count), inputs.dtype)
    return jnp.concatenate([constant, linear, quadratic], axis=1)


def conv_cols(extended, weights):
    total = weights[0][:, None] * extended[:, 2:]
    total = total + weights[1][:, None] * extended[:, 1:-1]
    return total + weights[2][:, None] * extended[:, :-2]


def add_states(earlier, later):
    return jax.tree.map(jnp.add, earlier, later)


def conv_back(grad_conv, tail_cols, extended, weights, length):
    ext_grad = jnp.concatenate([grad_conv, tail_cols], axis=1)
    grad_input = (
        weights[0][:, None] * ext_grad[:, 0:length]
        + weights[1][:, None] * ext_grad[:, 1 : length + 1]
        + weights[2][:, None] * ext_grad[:, 2 : length + 2]
    )
    grad_taps = jnp.stack(
        [
            jnp.sum(grad_conv * extended[:, 2 - tap_index : 2 - tap_index + length], axis=1)
            for tap_index in range(3)
        ]
    )
    return (grad_input.T, grad_taps)


def body(query_in, key_in, value_in, conv_query, conv_key, conv_value, out_proj, out_grad):
    length = query_in.shape[0]
    head_count = conv_value.shape[1] // VD
    block_rows = min(length, 512)
    rim_rows = from_behind(
        (query_in[length - 2 :], key_in[length - 2 :], value_in[length - 2 :]), "seq", 1
    )
    ext_query = jnp.concatenate([rim_rows[0], query_in], axis=0).astype(jnp.float32).T
    ext_key = jnp.concatenate([rim_rows[1], key_in], axis=0).astype(jnp.float32).T
    ext_value = jnp.concatenate([rim_rows[2], value_in], axis=0).astype(jnp.float32).T
    query_heads = conv_cols(ext_query, conv_query).reshape(head_count, FK, length)
    key_heads = conv_cols(ext_key, conv_key).reshape(head_count, FK, length)
    value_heads = conv_cols(ext_value, conv_value).reshape(head_count, VD, length)
    phi_query, query_pull = jax.vjp(features, query_heads)
    phi_key, key_pull = jax.vjp(features, key_heads)
    causal = (
        lax.broadcasted_iota(jnp.int32, (block_rows, block_rows), 0)
        >= lax.broadcasted_iota(jnp.int32, (block_rows, block_rows), 1)
    ).astype(jnp.float32)
    row_ranges = [slice(0, block_rows)]
    key_states = [
        jnp.einsum("hfs,hvs->hfv", phi_key, value_heads, precision=HIGHEST)
        for row_range in row_ranges
    ]
    key_sums = [jnp.sum(phi_key, axis=2) for row_range in row_ranges]
    local_state = sum(key_states[1:], key_states[0])
    local_sum = sum(key_sums[1:], key_sums[0])
    zero_state = jnp.zeros_like(local_state)
    zero_sum = jnp.zeros_like(local_sum)
    similarity = jnp.einsum("hft,hfs->hts", query_heads, key_heads, precision=HIGHEST) * FK ** (
        -0.5
    )
    weights = (1.0 + similarity + 0.5 * similarity * similarity) * causal
    similarities = [similarity]
    local_weights = [weights]
    local_numer = [jnp.einsum("hts,hvs->hvt", weights, value_heads, precision=HIGHEST)]
    local_denom = jnp.sum(weights, axis=2)
    prev_state, prev_sum = carried_in(
        (local_state, local_sum), "seq", add_states, (zero_state, zero_sum), False
    )
    seen_sums = [prev_sum + sum(key_sums[:0], zero_sum)]
    denominators = [
        local_denom + jnp.einsum("hft,hf->ht", phi_query, seen_sums[0], precision=HIGHEST)
    ]
    upstream = lax.dot_general(
        lax.all_gather(out_grad, "head", axis=0, tiled=True),
        out_proj,
        (((1,), (1,)), ((), ())),
        preferred_element_type=jnp.float32,
    ).T.reshape(head_count, VD, length)
    numer_grads = [upstream / denominators[0][:, None, :]]
    query_states = [jnp.einsum("hft,hvt->hfv", phi_query, numer_grads[0], precision=HIGHEST)]
    local_grad_state = sum(query_states[1:], query_states[0])
    seen_states = [prev_state + sum(key_states[:0], zero_state)]
    position = 0
    numerator = local_numer[position] + jnp.einsum(
        "hft,hfv->hvt", phi_query, seen_states[position], precision=HIGHEST
    )
    attended_blk = numerator / denominators[position][:, None, :]
    denom_grads = [-jnp.sum(upstream * attended_blk, axis=1) / denominators[position]]
    flat_attended = attended_blk.reshape(head_count * VD, length).T.astype(jnp.bfloat16)
    mixed = lax.psum_scatter(
        jnp.dot(flat_attended, out_proj, preferred_element_type=jnp.float32),
        "head",
        scatter_dimension=0,
        tiled=True,
    ).astype(jnp.bfloat16)
    query_sums = [jnp.einsum("hft,ht->hf", phi_query, denom_grads[0], precision=HIGHEST)]
    local_grad_sum = sum(query_sums[1:], query_sums[0])
    next_state, next_sum = carried_in(
        (local_grad_state, local_grad_sum), "seq", add_states, (zero_state, zero_sum), True
    )
    position = 0
    numer_grad = numer_grads[position]
    denom_grad = denom_grads[position]
    later_state = next_state + sum(query_states[position + 1 :], zero_state)
    later_sum = next_sum + sum(query_sums[position + 1 :], zero_sum)
    phi_query_grads = (
        jnp.einsum("hvt,hfv->hft", numer_grad, seen_states[position], precision=HIGHEST)
        + denom_grad[:, None, :] * seen_sums[position][:, :, None]
    )
    phi_key_grads = (
        jnp.einsum("hvs,hfv->hfs", value_heads, later_state, precision=HIGHEST)
        + later_sum[:, :, None]
    )
    value_grads = jnp.einsum("hfs,hfv->hvs", phi_key, later_state, precision=HIGHEST) + jnp.einsum(
        "hts,hvt->hvs", local_weights[position], numer_grad, precision=HIGHEST
    )
    weight_grads = (
        jnp.einsum("hvt,hvs->hts", numer_grad, value_heads, precision=HIGHEST)
        + denom_grad[:, :, None]
    )
    similarity_grads = weight_grads * (1.0 + similarities[position]) * causal * FK ** (-0.5)
    query_direct = jnp.einsum("hts,hfs->hft", similarity_grads, key_heads, precision=HIGHEST)
    key_direct = jnp.einsum("hts,hft->hfs", similarity_grads, query_heads, precision=HIGHEST)
    grad_query_conv = (query_pull(phi_query_grads)[0] + query_direct).reshape(
        head_count * FK, length
    )
    grad_key_conv = (key_pull(phi_key_grads)[0] + key_direct).reshape(head_count * FK, length)
    grad_value_conv = value_grads.reshape(head_count * VD, length)
    tail_cols = from_behind(
        (grad_query_conv[:, :2], grad_key_conv[:, :2], grad_value_conv[:, :2]), "seq", -1
    )
    grad_query, taps_query = conv_back(grad_query_conv, tail_cols[0], ext_query, conv_query, length)
    grad_key, taps_key = conv_back(grad_key_conv, tail_cols[1], ext_key, conv_key, length)
    grad_value, taps_value = conv_back(grad_value_conv, tail_cols[2], ext_value, conv_value, length)
    grad_conv_query, grad_conv_key, grad_conv_value = lax.psum(
        (taps_query, taps_key, taps_value), "seq"
    )
    return (
        mixed,
        grad_query,
        grad_key,
        grad_value,
        grad_conv_query,
        grad_conv_key,
        grad_conv_value,
    )


def solution(mesh):
    in_specs = (
        P("seq", "head"),
        P("seq", "head"),
        P("seq", "head"),
        P(None, "head"),
        P(None, "head"),
        P(None, "head"),
        P("head", None),
        P(("seq", "head"), None),
    )
    out_specs = (
        P(("seq", "head"), None),
        P("seq", "head"),
        P("seq", "head"),
        P("seq", "head"),
        P(None, "head"),
        P(None, "head"),
        P(None, "head"),
    )
    return jax.shard_map(body, mesh=mesh, in_specs=in_specs, out_specs=out_specs, check_vma=False)
```

profile of v0, /device:TPU:1, one launch (start us, length us, event | category | flops | bytes accessed | tf_op | source)
XLA Modules:
  0.0 1457.7 jit_solution(14032197771022943189)
XLA Ops:
  8.8 4.9 collective-permute-start.2
  14.4 1.9 collective-permute-start
  19.4 2.4 convolution_bitcast_fusion.1
  22.0 1.3 multiply_add_fusion
  23.2 2.5 copy.59
  25.8 3.7 fusion.12
  30.4 3.9 collective-permute-start.1
  34.3 1.1 fusion.9
  38.7 1.7 fusion.11
  40.3 93.9 %all-gather.4 = f32[128,4,153]{2,1,0:T(4,128)} all-gather(f32[1,4,153]{2,1,0:T(4,128)S(1)} %bitcast.162), channel_id=3, replica_groups=mesh['seq'=128,'head'=4] {'seq'}, dimensions={0}, use_global_device_ids=true | all-gather | bytes 315792 | tf_op jit(solution)/shard_map/all_gather | solution.py:24
  134.6 2.3 convolution_bitcast_fusion
  136.9 6.3 fusion.15
  143.2 6.5 fusion.16
  149.7 4.0 fusion.46
  153.6 124.5 %all-gather.12.cloned.1.call-done = f32[512,153,128]{2,1,0:T(8,128)} async-done(((f32[4,153,128]{2,1,0:T(8,128)}), f32[512,153,128]{2,1,0:T(8,128)}) %all-gather.12.cloned.1.call-update) | async-done | bytes 40108048 | tf_op jit(solution)/shard_map/all_gather | solution.py:24
  278.1 227.4 %while.34 = (s32[]{:T(128)}, f32[4,153,128]{2,1,0:T(8,128)S(1)}, f32[4,153]{1,0:T(4,128)S(1)}, s32[]{:T(128)}, f32[128,4,153,128]{3,2,1,0:T(8,128)}, /*index=5*/f32[128,4,153]{2,1,0:T(4,128)}, s32[]{:T(128)}, s32[]{:T(128)}) while((s32[]{:T(128)}, f32[4,153,128]{2,1,0:T(8,128)S(1)}, f32[4,153]{1,0:T(4,128)S(1)}, s32[]{:T(128)}, ...), condition=%wide.region_2.3_spmd.clone, body=%wide.region_1.0_spmd.clone.sunk | while | flops 236848 | bytes 947491 | solution.py:37
  505.6 2.4 fusion.33
  508.0 3.4 multiply_reduce_fusion.7
  511.4 3.3 fusion.45
  516.0 3.5 fusion.43
  519.6 1.4 fusion.31
  521.0 2.5 convolution_add_fusion.1
  523.5 2.0 fusion.2
  527.4 6.2 multiply_multiply_fusion
  533.7 2.1 convolution_add_fusion.5
  535.8 2.1 collective-permute-start.3
  538.2 82.9 %all-gather.5 = f32[128,4,153]{2,1,0:T(4,128)S(1)} all-gather(f32[1,4,153]{2,1,0:T(4,128)S(1)} %bitcast.163), channel_id=5, replica_groups=mesh['seq'=128,'head'=4] {'seq'}, dimensions={0}, use_global_device_ids=true | all-gather | bytes 315792 | tf_op jit(solution)/shard_map/all_gather | solution.py:24
  622.0 2.2 convert_element_type.25
  624.2 164.2 %all-gather.14.cloned.1.call-done = f32[512,153,128]{2,1,0:T(8,128)} async-done(((f32[4,153,128]{2,1,0:T(8,128)}), f32[512,153,128]{2,1,0:T(8,128)}) %all-gather.14.cloned.1.call-update) | async-done | bytes 40108048 | tf_op jit(solution)/shard_map/all_gather | solution.py:24
  788.5 145.5 %while.35 = (s32[]{:T(128)}, f32[4,153,128]{2,1,0:T(8,128)S(1)}, f32[4,153]{1,0:T(4,128)S(1)}, s32[]{:T(128)}, f32[128,4,153,128]{3,2,1,0:T(8,128)}, /*index=5*/...) while((s32[]{:T(128)}, f32[4,153,128]{2,1,0:T(8,128)S(1)}, ...), condition=%wide.region_9.10_spmd.clone, body=%wide.region_8.9_spmd.clone.sunk | while | flops 236852 | bytes 947553 | solution.py:37
  788.5 1.1 add_select_fusion.10
  793.1 1.1 add_select_fusion.10
  794.2 1.1 add_select_fusion.10
  797.6 1.1 add_select_fusion.10
  798.7 1.1 add_select_fusion.10
  799.9 1.1 add_select_fusion.10
  803.3 1.1 add_select_fusion.10
  804.4 1.1 add_select_fusion.10
  805.6 1.1 add_select_fusion.10
  809.0 1.1 add_select_fusion.10
  810.1 1.1 add_select_fusion.10
  814.7 1.1 add_select_fusion.10
  815.8 1.1 add_select_fusion.10
  819.2 1.1 add_select_fusion.10
  820.3 1.1 add_select_fusion.10
  821.5 1.1 add_select_fusion.10
  824.9 1.1 add_select_fusion.10
  826.0 1.1 add_select_fusion.10
  827.2 1.1 add_select_fusion.10
  830.6 1.1 add_select_fusion.10
  831.7 1.1 add_select_fusion.10
  836.2 1.1 add_select_fusion.10
  934.0 1.3 fusion.10
  935.5 8.1 convolution_add_fusion.2
  943.6 1.6 copy.43
  945.3 2.6 collective-permute-start.5
  947.9 1.2 convolution_add_fusion
  949.1 2.1 fusion.1
  952.1 1.3 copy-done.3
  953.4 3.6 convolution_add_fusion.4
  957.3 1.9 collective-permute-start.4
  959.3 3.3 collective-permute-done.4
  963.4 1.6 multiply_reduce_fusion.6
  965.1 485.7 %all-reduce = (f32[3,64]{1,0:T(4,128)}, f32[3,64]{1,0:T(4,128)}, f32[3,512]{1,0:T(4,128)}) all-reduce(f32[3,64]{1,0:T(4,128)S(1)} %get-tuple-element.377, f32[3,64]{1,0:T(4,128)S(1)} %get-tuple-element.378, f32[3,512]{1,0:T(4,128)S(1)} %pad_maximum_fusion.7), channel_id=1, replica_groups=mesh['seq'=128,'head'=4] {'seq'}, use_global_device_ids=true, to_apply=%region_15.16 | all-reduce | flops 1920 | bytes 15360 | tf_op jit(solution)/shard_map/psum | solution.py:204
  (634 shorter events, 360.6 us)
Async XLA Ops:
  7.2 142.5 %copy-start = (bf16[512,2048]{1,0:T(8,128)(2,1)S(1)}, bf16[512,2048]{1,0:T(8,128)(2,1)}, u32[]{:S(2)}) copy-start(bf16[512,2048]{1,0:T(8,128)(2,1)} %param.20) | copy-start | bytes 6291460
  7.2 12.2 copy-start.26
  7.2 142.5 %all-gather.10.cloned.1.call-start = ((), (), s32[]{:S(2)}) async-start(), calls=%async_computation.2 | async-start | bytes 2621440 | tf_op jit(solution)/shard_map/all_gather | solution.py:143
  7.9 270.2 %all-gather.12.cloned.1.call-start = ((), (), s32[]{:S(2)}) async-start(), calls=%async_computation.3 | async-start | bytes 42270720 | tf_op jit(solution)/shard_map/all_gather | solution.py:24
  8.8 9.2 collective-permute-start.2
  14.4 7.4 collective-permute-start
  17.9 3.8 copy-start.37
  17.9 3.8 copy-start.39
  17.9 3.8 copy-start.41
  18.9 2.9 copy-start.10
  19.1 2.7 copy-start.14
  19.1 6.7 copy-start.30
  19.4 2.4 copy-start.35
  29.6 592.5 %reduce-scatter.2.cloned.1.call-start = ((), (), s32[]{:S(2)}) async-start(), calls=%async_computation.1 | async-start | bytes 5242880 | tf_op jit(solution)/shard_map/reduce_scatter | solution.py:159
  30.4 5.9 collective-permute-start.1
  36.2 1.0 copy-start.43
  36.2 98.3 %copy-start.45 = (f32[64]{0:T(128)}, f32[64]{0:T(128)S(1)}, u32[]{:S(2)}) copy-start(f32[64]{0:T(128)S(1)} %get-tuple-element.372) | copy-start | bytes 772
  36.2 98.3 %copy-start.47 = (f32[64]{0:T(128)}, f32[64]{0:T(128)S(1)}, u32[]{:S(2)}) copy-start(f32[64]{0:T(128)S(1)} %get-tuple-element.373) | copy-start | bytes 772
  37.2 0.7 copy-start.12
  38.7 98.2 %copy-start.18 = (f32[64,512]{1,0:T(8,128)}, f32[64,512]{1,0:T(8,128)S(1)}, u32[]{:S(2)}) copy-start(f32[64,512]{1,0:T(8,128)S(1)} %get-tuple-element.359) | copy-start | bytes 393220
  38.7 95.9 %copy-start.27 = (f32[256,136,1]{0,1,2:T(8,128)S(1)}, f32[256,136,1]{0,1,2:T(8,128)}, u32[]{:S(2)}) copy-start(f32[256,136,1]{0,1,2:T(8,128)} %constant.90) | copy-start | bytes 417796
  134.6 2.4 copy-start.15
  134.6 2.4 copy-start.23
  136.9 6.3 copy-start.5
  505.6 5.8 copy-start.8
  514.8 1.2 copy-start.32
  514.8 1.2 copy-start.36
  514.8 273.7 %all-gather.14.cloned.1.call-start = ((), (), s32[]{:S(2)}) async-start(), calls=%async_computation.4 | async-start | bytes 42270720 | tf_op jit(solution)/shard_map/all_gather | solution.py:24
  516.0 5.0 copy-start.9
  520.9 2.5 copy-start.28
  523.5 2.1 copy-start.19
  525.5 1.2 copy-start.6
  525.6 1.5 copy-start.24
  525.6 1.9 copy-start.33
  527.4 6.2 copy-start.16
  533.6 2.2 copy-start.2
  533.7 4.3 copy-start.13
  533.7 87.5 %copy-start.44 = (f32[64]{0:T(128)S(1)}, f32[64]{0:T(128)}, u32[]{:S(2)}) copy-start(f32[64]{0:T(128)} %copy-done.43) | copy-start | bytes 772
  533.7 87.5 %copy-start.46 = (f32[64]{0:T(128)S(1)}, f32[64]{0:T(128)}, u32[]{:S(2)}) copy-start(f32[64]{0:T(128)} %copy-done.45) | copy-start | bytes 772
  533.7 87.5 %copy-start.48 = (f32[64]{0:T(128)S(1)}, f32[64]{0:T(128)}, u32[]{:S(2)}) copy-start(f32[64]{0:T(128)} %copy-done.47) | copy-start | bytes 772
  535.8 85.3 %collective-permute-start.3 = (f32[64,2]{1,0:T(8,128)S(1)}, f32[64,2]{1,0:T(8,128)S(1)}, u32[]{:S(2)}, u32[]{:S(2)}) collective-permute-start(f32[64,2]{1,0:T(8,128)S(1)} %slice.147), channel_id=1, source_target_pairs={{4,0},{8,4},{12,8},{16,12},{20,16},{24,20},{28,24},{32,28},{36,32}... | collective-permute-start | bytes 1544 | tf_op jit(solution)/shard_map/ppermute | solution.py:19
  622.0 311.9 %copy-start.4 = (f32[4,136,512]{2,1,0:T(8,128)S(1)}, f32[4,136,512]{2,1,0:T(8,128)}, u32[]{:S(2)}) copy-start(f32[4,136,512]{2,1,0:T(8,128)} %convolution_bitcast_fusion.1) | copy-start | bytes 3342340
  788.5 145.5 %copy-start.31 = (f32[4,16,512]{2,1,0:T(8,128)S(1)}, f32[4,16,512]{2,1,0:T(8,128)}, u32[]{:S(2)}) copy-start(f32[4,16,512]{2,1,0:T(8,128)} %copy-done.30) | copy-start | bytes 393220
  934.0 1.4 copy-start.25
  934.0 1.5 copy-start.34
  943.6 4.3 copy-start.7
  945.3 2.6 copy-start.21
  945.3 3.8 copy-start.29
  945.3 18.1 %collective-permute-start.5 = (f32[512,2]{0,1:T(2,128)S(1)}, f32[512,2]{0,1:T(2,128)S(1)}, u32[]{:S(2)}, u32[]{:S(2)}) collective-permute-start(f32[512,2]{0,1:T(2,128)S(1)} %slice.153), channel_id=1, source_target_pairs={{4,0},{8,4},{12,8},{16,12},{20,16},{24,20},{28,24},{32,28},{36,32}... | collective-permute-start | bytes 12296 | tf_op jit(solution)/shard_map/ppermute | solution.py:19
  949.1 2.1 copy-start.17
  951.2 2.2 copy-start.3
  951.2 2.2 copy-start.20
  953.4 3.6 copy-start.11
  953.4 9.2 copy-start.38
  953.4 9.2 copy-start.40
  953.4 9.2 copy-start.42
  953.4 10.0 copy-start.22
  957.3 5.2 collective-permute-start.4
  962.6 488.2 %copy-start.1 = (bf16[512,2048]{1,0:T(8,128)(2,1)S(1)}, bf16[512,2048]{1,0:T(8,128)(2,1)}, u32[]{:S(2)}) copy-start(bf16[512,2048]{1,0:T(8,128)(2,1)} %param.20) | copy-start | bytes 6291460
Sparse Core Ops, SparseCore 0:
  10.1 43.5 all-gather.9
  57.4 220.6 all-gather.11
  514.9 50.3 reduce-scatter.1
  568.3 220.1 all-gather.13
where the time goes:
time: 1480 us; the launch traced here: 1460 us
  blocking collectives  663 us (45%)
  other arithmetic  383 us (26%)
  waiting for transfers between devices  293 us (20%)
  matrix products  68.3 us (5%)
  starting transfers between devices  17.7 us (1%)
  between operations  15 us (1%)
    psum x1, blocking collectives, body(): lax.psum((taps_query, taps_key, taps_value), 'seq')  486 us
    select_n x512, other arithmetic, hop(): return jax.tree.map(lambda a, b: jnp.where(reached, a, b), new, before)  368 us
    all_gather x2, waiting for transfers between devices, carried_in(): everything = jax.tree.map(lambda part: lax.all_gather(part, axis), shard)  289 us
    all_gather x2, blocking collectives, carried_in(): everything = jax.tree.map(lambda part: lax.all_gather(part, axis), shard)  177 us
  transfers between devices with their start and end apart: 10, of which 3 were waited for; matrix products, arithmetic and copies ran while one was open for 5% of the time, Pallas kernels for 0%

commit v1 on v0

v1 whole, which is shorter than its diff:
```python
import jax
import jax.numpy as jnp
import numpy as np
from jax import lax
from jax.experimental import pallas as pl
from jax.experimental.pallas import tpu as pltpu
from jax.sharding import Mesh, PartitionSpec as P

FK = 16
VD = 128
FEAT = 153
ROWS = 160
WIDE = 256
SUMS = FEAT

SEQ = ("x", "z", "core")
HIGHEST = lax.Precision.HIGHEST
F32 = jnp.float32
BF16 = jnp.bfloat16


def tables():
    places = np.full((8, WIDE), -1, np.int32)
    factors = np.zeros((8, WIDE), np.float32)
    factors[0, 0] = 1.0
    factors[0, 1 : FK + 1] = 0.25
    places[0, 1 : FK + 1] = np.arange(FK)
    factors[1, 0] = 1.0
    factors[2, : FK + 1] = 1.0
    column = FK + 1
    for i in range(FK):
        for j in range(i, FK):
            places[0, column], places[1, column] = i, j
            factors[0, column] = 1.0 / 32.0 if i == j else 1.0 / 16.0
            column += 1
    return places, factors


def mm(a, b, ca, cb):
    return lax.dot_general(a, b, (((ca,), (cb,)), ((), ())), preferred_element_type=F32)


def halves(x):
    high = x.astype(BF16)
    return high, (x - high.astype(F32)).astype(BF16)


def fold(pair):
    return pair[:, :VD] + pair[:, VD:]


def selectors(places, head):
    row = lax.broadcasted_iota(jnp.int32, (WIDE, WIDE), 0)
    own = (((row >> 4) & 3) == head) & (row < 192)
    channel = row & 15
    first = jnp.where(own & (channel == places[0:1, :]), 1.0, 0.0).astype(BF16)
    second = jnp.where(own & (channel == places[1:2, :]), 1.0, 0.0).astype(BF16)
    return first, second


def head_lanes(head, width):
    lane = lax.broadcasted_iota(jnp.int32, (1, width), 1)
    return jnp.where(((lane >> 4) & 3) == head, 1.0, 0.0)


def expand(pieces, select, factors):
    return (
        mm(pieces, select[0], 1, 0) + factors[1:2, :],
        mm(pieces, select[1], 1, 0) + factors[2:3, :],
    )


def pull(grad_first, grad_second, select):
    return mm(grad_first.astype(BF16), select[0][:64, :], 1, 1) + mm(
        grad_second.astype(BF16), select[1][:64, :], 1, 1
    )


def pack(state, total):
    row = lax.broadcasted_iota(jnp.int32, (ROWS, VD), 0)
    state = jnp.where(row == SUMS, total[:, :VD], state[:ROWS, :])
    return jnp.where(row == SUMS + 1, total[:, VD:], state)


def unpack(packed):
    total = jnp.concatenate([packed[SUMS : SUMS + 1, :], packed[SUMS + 1 : SUMS + 2, :]], axis=1)
    return jnp.concatenate([packed, jnp.zeros((WIDE - ROWS, VD), F32)], axis=0), total


def similar(query_pieces, key_pieces, head):
    mine = (query_pieces.astype(F32) * head_lanes(head, WIDE)).astype(BF16)
    return mm(mine, key_pieces, 1, 1) * 0.25


def direct(high, low):
    return high[:, :64] + high[:, 64:128] + low[:, :64]


def causal_mask(length):
    return lax.broadcasted_iota(jnp.int32, (length, length), 0) >= lax.broadcasted_iota(
        jnp.int32, (length, length), 1
    )


def extend(scratch, rows, rim):
    length = rows.shape[0]
    scratch[0:8, :] = jnp.concatenate([jnp.zeros((6, rows.shape[1]), F32), rim], axis=0)
    scratch[8 : length + 8, :] = rows.astype(F32)


def convolve(scratch, taps, length):
    total = taps[0:1, :] * scratch[8 : length + 8, :]
    total = total + taps[1:2, :] * scratch[7 : length + 7, :]
    return total + taps[2:3, :] * scratch[6 : length + 6, :]


def first_kernel(
    q_in, k_in, v_in, rim_qk, rim_v, taps_q, taps_k, taps_v, places, factors,
    q4, k4, k5, vb, state, narrow, broad,
):
    head = pl.program_id(0)
    length = q_in.shape[0]

    @pl.when(head == 0)
    def _():
        rim = rim_qk[...].astype(F32)
        for source, taps, edge, target in (
            (q_in, taps_q, rim[:, :64], q4),
            (k_in, taps_k, rim[:, 64:], k4),
        ):
            extend(narrow, source[...], edge)
            x = convolve(narrow, taps[...], length)
            high = x.astype(BF16).astype(F32)
            rest = x - high
            mid = rest.astype(BF16).astype(F32)
            low = rest - mid
            target[:, :128] = jnp.concatenate([high, mid], axis=1).astype(BF16)
            target[:, 128:] = jnp.concatenate([low, high], axis=1).astype(BF16)
            if target is k4:
                k5[:, :128] = jnp.concatenate([high, high], axis=1).astype(BF16)
                k5[:, 128:] = jnp.concatenate([high, mid], axis=1).astype(BF16)

    extend(broad, v_in[...], rim_v[...].astype(F32))
    value = jnp.concatenate(halves(convolve(broad, taps_v[...], length)), axis=1)
    vb[...] = value
    first, second = expand(k4[...], selectors(places[...], head), factors[...])
    phi = (first * second).astype(BF16)
    state[...] = pack(
        fold(mm(phi, value, 0, 0)), jnp.sum(phi.astype(F32), axis=0, keepdims=True)
    )


def local_kernel(q4, k5, vb, numer, denom):
    head = pl.program_id(0)
    a = similar(q4[...], k5[...], head)
    length = a.shape[0]
    weight = jnp.where(causal_mask(length), 1.0 + a + 0.5 * a * a, 0.0)
    high, low = halves(weight)
    value = vb[...]
    numer[...] = fold(mm(high, value, 1, 0)) + mm(low, value[:, :VD], 1, 0)
    denom[...] = jnp.broadcast_to(jnp.sum(weight, axis=1, keepdims=True), (length, VD))


def middle_kernel(q4, before, numer, denom, up, places, factors, att, ng, dg, state):
    head = pl.program_id(0)
    scale = factors[...]
    first, second = expand(q4[...], selectors(places[...], head), scale)
    phi = first * second * scale[0:1, :]
    high, low = halves(phi)
    seen, total = unpack(before[...])
    seen_high, seen_low = halves(seen)
    inter = mm(high, seen_high, 1, 0) + mm(high, seen_low, 1, 0) + mm(low, seen_high, 1, 0)
    inverse = 1.0 / (denom[...] + jnp.sum(phi * total, axis=1, keepdims=True))
    out = (numer[...] + inter) * inverse
    att[...] = out.astype(BF16)
    upstream = up[...]
    numer_grad = upstream * inverse
    denom_grad = -jnp.sum(numer_grad * out, axis=1, keepdims=True)
    ng[...] = numer_grad
    dg[...] = jnp.broadcast_to(denom_grad, dg.shape)
    state[...] = pack(
        mm(high, numer_grad.astype(BF16), 0, 0),
        jnp.sum(high.astype(F32) * denom_grad, axis=0, keepdims=True),
    )


def inner_kernel(q4, k4, k5, vb, before, ng, dg, places, factors, gq, kd, gv):
    head = pl.program_id(0)
    scale = factors[...]
    query, value = q4[...], vb[...]
    a = similar(query, k5[...], head)
    mask = causal_mask(a.shape[0])
    numer_grad = ng[...]
    denom_grad = dg[:, 0:1]
    high, low = halves(numer_grad)
    both = jnp.concatenate([high, low], axis=1)
    value_high, value_low = value[:, :VD], value[:, VD:]
    weight_grad = (
        mm(both, jnp.concatenate([value_high, value_high], axis=1), 1, 1)
        + mm(high, value_low, 1, 1)
        + denom_grad
    )
    sim_high, sim_low = halves(jnp.where(mask, weight_grad * (0.25 + 0.25 * a), 0.0))
    weight = jnp.where(mask, 1.0 + a + 0.5 * a * a, 0.0).astype(BF16)
    gv[...] = mm(weight, high, 0, 0)
    lanes = head_lanes(head, 64)
    key = k4[...]
    query_direct = direct(mm(sim_high, key, 1, 0), mm(sim_low, key, 1, 0)) * lanes
    key_direct = direct(mm(sim_high, query, 0, 0), mm(sim_low, query, 0, 0)) * lanes
    select = selectors(places[...], head)
    first, second = expand(query, select, scale)
    seen, total = unpack(before[...])
    seen_high, seen_low = halves(seen)
    phi_grad = (
        mm(both, jnp.concatenate([seen_high, seen_high], axis=1), 1, 1)
        + mm(high, seen_low, 1, 1)
        + denom_grad * total
    ) * scale[0:1, :]
    query_grad = query_direct + pull(phi_grad * second, phi_grad * first, select)

    @pl.when(head == 0)
    def _():
        gq[...] = query_grad
        kd[...] = key_direct

    @pl.when(head > 0)
    def _():
        gq[...] += query_grad
        kd[...] += key_direct


def conv_back(scratch, grad, taps, length):
    scratch[0:length, :] = grad
    scratch[length : length + 8, :] = jnp.zeros((8, grad.shape[1]), F32)
    return (
        taps[0:1, :] * grad
        + taps[1:2, :] * scratch[1 : length + 1, :]
        + taps[2:3, :] * scratch[2 : length + 2, :]
    )


def edges(scratch, grad, length):
    sums = [
        jnp.sum(grad * scratch[8 - tap : length + 8 - tap, :], axis=0, keepdims=True)
        for tap in range(3)
    ]
    return jnp.concatenate(sums + [sums[0], grad[0:4, :]], axis=0)


def last_kernel(
    q_in, k_in, v_in, rim_qk, rim_v, taps_q, taps_k, taps_v, places, factors,
    k4, vb, after, gq, kd, gv_in, grad_q, grad_k, grad_v, edge_qk, edge_v, narrow, broad, gk,
):
    head = pl.program_id(0)
    length = q_in.shape[0]
    later, total = unpack(after[...])
    later_high, later_low = halves(later)
    value = vb[...]
    value_high = value[:, :VD]
    select = selectors(places[...], head)
    first, second = expand(k4[...], select, factors[...])
    phi_grad = (
        mm(
            jnp.concatenate([value_high, value_high], axis=1),
            jnp.concatenate([later_high, later_low], axis=1),
            1,
            1,
        )
        + mm(value[:, VD:], later_high, 1, 1)
        + total
    )
    key_grad = pull(phi_grad * second, phi_grad * first, select)

    @pl.when(head == 0)
    def _():
        gk[...] = kd[...] + key_grad

    @pl.when(head > 0)
    def _():
        gk[...] += key_grad

    value_grad = gv_in[...] + mm((first * second).astype(BF16), later_high, 1, 0)
    grad_v[...] = conv_back(broad, value_grad, taps_v[...], length)
    extend(broad, v_in[...], rim_v[...].astype(F32))
    edge_v[...] = edges(broad, value_grad, length)

    @pl.when(head == pl.num_programs(0) - 1)
    def _():
        rim = rim_qk[...].astype(F32)
        found = []
        for source, taps, edge, grad, target in (
            (q_in, taps_q, rim[:, :64], gq[...], grad_q),
            (k_in, taps_k, rim[:, 64:], gk[...], grad_k),
        ):
            target[...] = conv_back(narrow, grad, taps[...], length)
            extend(narrow, source[...], edge)
            found.append(edges(narrow, grad, length))
        edge_qk[...] = jnp.concatenate(found, axis=1)


def rim_kernel(tail, taps_q, taps_k, taps_v, q_in, k_in, v_in, grad_q, grad_k, grad_v):
    tails = tail[...]
    for start, taps, source, target in (
        (0, taps_q, q_in, grad_q),
        (64, taps_k, k_in, grad_k),
        (128, taps_v, v_in, grad_v),
    ):
        width = taps.shape[1]
        row = lax.broadcasted_iota(jnp.int32, (8, width), 0)
        one, two = tails[0:1, start : start + width], tails[1:2, start : start + width]
        weights = taps[...]
        extra = jnp.where(row == 6, weights[2:3, :] * one, 0.0)
        extra = extra + jnp.where(row == 7, weights[1:2, :] * one + weights[2:3, :] * two, 0.0)
        target[...] = source[...] + extra


def from_behind(block, axis, distance):
    devices = range(lax.axis_size(axis))
    route = [(i - distance, i) for i in devices if i - distance in devices]
    return lax.ppermute(block, axis, route)


def carried_in(packed, reverse):
    ranks = lax.axis_size(SEQ)
    everyone = lax.all_to_all(packed.reshape(ranks, -1), SEQ, 0, 0, tiled=True)
    rows = lax.broadcasted_iota(jnp.int32, (ranks, ranks), 0)
    cols = lax.broadcasted_iota(jnp.int32, (ranks, ranks), 1)
    reached = (cols > rows) if reverse else (cols < rows)
    sums = jnp.dot(reached.astype(F32), everyone, precision=HIGHEST)
    return lax.all_to_all(sums, SEQ, 0, 0, tiled=True).reshape(packed.shape)


def turned(block, axis, distance):
    size = lax.axis_size(axis)
    return lax.ppermute(block, axis, [(i, (i + distance) % size) for i in range(size)])


def gathered(block, axis):
    size, index, rows = lax.axis_size(axis), lax.axis_index(axis), block.shape[0]
    whole = jnp.zeros((size * rows,) + block.shape[1:], block.dtype)
    for distance in range(size):
        part = turned(block, axis, distance) if distance else block
        source = (index - distance) % size
        whole = lax.dynamic_update_slice_in_dim(whole, part, source * rows, 0)
    return whole


def scattered(whole, axis):
    size, index = lax.axis_size(axis), lax.axis_index(axis)
    rows = whole.shape[0] // size
    total = lax.dynamic_slice_in_dim(whole, index * rows, rows, 0)
    for distance in range(1, size):
        target = (index + distance) % size
        part = lax.dynamic_slice_in_dim(whole, target * rows, rows, 0)
        total = total + turned(part, axis, distance)
    return total


def to_all(block, axis):
    copies = jnp.broadcast_to(block[None], (lax.axis_size(axis),) + block.shape)
    return lax.all_to_all(copies, axis, 0, 0, tiled=True)


def body(query_in, key_in, value_in, conv_query, conv_key, conv_value, out_proj, out_grad):
    length, keys = query_in.shape
    heads = conv_value.shape[1] // VD
    assert keys == heads * FK == 64
    places, factors = (jnp.asarray(t) for t in tables())

    def whole(*shape):
        return pl.BlockSpec(shape, lambda h: (0,) * len(shape))

    def per_head(rows):
        return pl.BlockSpec((rows, VD), lambda h: (0, h))

    pairs = pl.BlockSpec((length, 2 * VD), lambda h: (0, h))
    packs = pl.BlockSpec((ROWS, VD), lambda h: (h, 0))
    table = whole(8, WIDE)
    pieces = whole(length, WIDE)
    narrow = whole(length, keys)

    def arr(rows, cols, dtype=F32):
        return jax.ShapeDtypeStruct((rows, cols), dtype)

    def call(kernel, name, ins, outs, shapes, flops, scratch=()):
        return pl.pallas_call(
            kernel,
            name=name,
            grid=(heads,),
            in_specs=ins,
            out_specs=outs,
            out_shape=shapes,
            scratch_shapes=list(scratch),
            cost_estimate=pl.CostEstimate(
                flops=flops, bytes_accessed=4 << 20, transcendentals=0
            ),
        )

    values = heads * VD
    rim = from_behind(
        jnp.concatenate([x[length - 2 :] for x in (query_in, key_in, value_in)], axis=1), SEQ, 1
    )
    rim_qk, rim_v = rim[:, : 2 * keys], rim[:, 2 * keys :]
    conv_ins = [
        narrow, narrow, per_head(length), whole(2, 2 * keys), per_head(2),
        whole(3, keys), whole(3, keys), per_head(3), table, table,
    ]
    conv_args = (
        query_in, key_in, value_in, rim_qk, rim_v,
        conv_query, conv_key, conv_value, places, factors,
    )
    buffers = [pltpu.VMEM((length + 8, keys), F32), pltpu.VMEM((length + 8, VD), F32)]
    q4, k4, k5, vb, local_state = call(
        first_kernel, "first", conv_ins,
        [pieces, pieces, pieces, pairs, packs],
        [arr(length, WIDE, BF16)] * 3 + [arr(length, 2 * values, BF16), arr(heads * ROWS, VD)],
        2 << 30, buffers,
    )(*conv_args)
    cotangent = gathered(out_grad, "head")
    upstream = lax.dot_general(
        cotangent, out_proj, (((1,), (1,)), ((), ())), preferred_element_type=F32
    )
    numer, denom = call(
        local_kernel, "local", [pieces, pieces, pairs],
        [per_head(length)] * 2, [arr(length, values)] * 2, 4 << 30,
    )(q4, k5, vb)
    before = carried_in(local_state, False)
    att, ng, dg, grad_state = call(
        middle_kernel, "middle",
        [pieces, packs] + [per_head(length)] * 3 + [table, table],
        [per_head(length)] * 3 + [packs],
        [arr(length, values, BF16), arr(length, values), arr(length, values)]
        + [arr(heads * ROWS, VD)],
        4 << 30,
    )(q4, before, numer, denom, upstream, places, factors)
    after = carried_in(grad_state, True)
    gq, kd, gv = call(
        inner_kernel, "inner",
        [pieces] * 3 + [pairs, packs] + [per_head(length)] * 2 + [table, table],
        [narrow, narrow, per_head(length)],
        [arr(length, keys)] * 2 + [arr(length, values)],
        8 << 30,
    )(q4, k4, k5, vb, before, ng, dg, places, factors)
    partial = jnp.dot(att, out_proj, preferred_element_type=F32)
    mixed = scattered(partial, "head").astype(BF16)
    grad_query, grad_key, grad_value, edge_qk, edge_v = call(
        last_kernel, "last",
        conv_ins + [pieces, pairs, packs, narrow, narrow, per_head(length)],
        [narrow, narrow, per_head(length), whole(8, 2 * keys), per_head(8)],
        [arr(length, keys)] * 2 + [arr(length, values), arr(8, 2 * keys), arr(8, values)],
        4 << 30, buffers + [pltpu.VMEM((length, keys), F32)],
    )(*conv_args, k4, vb, after, gq, kd, gv)
    edge = jnp.concatenate([edge_qk, edge_v], axis=1)
    tail = from_behind(edge[4:6], SEQ, -1)
    taps = lax.psum(edge[:3], "core")
    taps = jnp.sum(to_all(taps, "z").reshape(lax.axis_size("z"), 3, -1), axis=0)
    taps = lax.psum(taps, "x")
    last = length // 8 - 1
    rims = [pl.BlockSpec((8, n), lambda i: (last, 0)) for n in (keys, keys, values)]
    grad_query, grad_key, grad_value = pl.pallas_call(
        rim_kernel,
        name="rims",
        grid=(1,),
        in_specs=[whole(2, 2 * keys + values), whole(3, keys), whole(3, keys), whole(3, values)]
        + rims,
        out_specs=rims,
        out_shape=[arr(length, keys)] * 2 + [arr(length, values)],
        input_output_aliases={4: 0, 5: 1, 6: 2},
    )(tail, conv_query, conv_key, conv_value, grad_query, grad_key, grad_value)
    return (
        mixed,
        grad_query,
        grad_key,
        grad_value,
        taps[:, :keys],
        taps[:, keys : 2 * keys],
        taps[:, 2 * keys :],
    )


def refined(mesh):
    ranks, groups = mesh.devices.shape
    shape = (4, 16, 2, groups) if ranks == 128 else (1, ranks // 2, 2, groups)
    return Mesh(mesh.devices.reshape(shape), SEQ + ("head",))


def solution(mesh):
    mesh = refined(mesh)
    in_specs = (
        P(SEQ, "head"),
        P(SEQ, "head"),
        P(SEQ, "head"),
        P(None, "head"),
        P(None, "head"),
        P(None, "head"),
        P("head", None),
        P(SEQ + ("head",), None),
    )
    out_specs = (
        P(SEQ + ("head",), None),
        P(SEQ, "head"),
        P(SEQ, "head"),
        P(SEQ, "head"),
        P(None, "head"),
        P(None, "head"),
        P(None, "head"),
    )
    return jax.shard_map(body, mesh=mesh, in_specs=in_specs, out_specs=out_specs, check_vma=False)
```

time: 1480 us -> 231 us (0.16)
  the two profiles are of different devices: /device:TPU:1 before, /device:TPU:32 now
where the time goes in v1:
time: 231 us; the launch traced here: 230 us
  starting transfers between devices  77.6 us (34%)
  waiting for transfers between devices  60.6 us (26%)
  Pallas kernels  35.9 us (16%)
  local copies, waits for them, and re-layouts  25 us (11%)
  blocking collectives  21 us (9%)
  matrix products  5.72 us (2%)
  other arithmetic  3.02 us (1%)
    all_to_all x2, waiting for transfers between devices, carried_in(): everyone = lax.all_to_all(packed.reshape(ranks, -1), SEQ, 0, 0, tiled=True)  38.5 us
    all_to_all x2, starting transfers between devices, carried_in(): everyone = lax.all_to_all(packed.reshape(ranks, -1), SEQ, 0, 0, tiled=True)  26.8 us
    ppermute x6, starting transfers between devices, turned(): lax.ppermute(block, axis, [(i, (i + distance) % size) for i in range(size)])  21.9 us
    psum x1, blocking collectives, body(): taps = lax.psum(taps, 'x')  17.4 us
    all_to_all x2, starting transfers between devices, carried_in(): return lax.all_to_all(sums, SEQ, 0, 0, tiled=True).reshape(packed.shape)  13 us
    all_to_all x2, waiting for transfers between devices, carried_in(): return lax.all_to_all(sums, SEQ, 0, 0, tiled=True).reshape(packed.shape)  12.5 us
    all_to_all x1, starting transfers between devices, to_all(): return lax.all_to_all(copies, axis, 0, 0, tiled=True)  12.1 us
    pallas_call x1, Pallas kernels, body(): call(inner_kernel, 'inner', [pieces] * 3 + [pairs, packs] + [per_head(len...  10.9 us
  transfers between devices with their start and end apart: 13, of which 6 were waited for; matrix products, arithmetic and copies ran while one was open for 10% of the time, Pallas kernels for 11%

profile of v1, /device:TPU:32, one launch (start us, length us, event | category | flops | bytes accessed | tf_op | source)
XLA Modules:
  0.0 229.9 jit_solution(2914329643852750311)
XLA Ops:
  0.6 0.0 copy-start
  0.6 0.9 slice.32
  1.5 1.0 copy.54.q_in
  2.5 0.0 copy-start.6
  2.5 1.0 copy.55.k_in
  3.5 0.0 copy-start.7
  3.5 0.1 pad_maximum_fusion
  3.6 1.9 collective-permute-start
  5.5 3.0 %collective-permute-done = bf16[2,640]{1,0:T(2,128)(2,1)S(1)} collective-permute-done((bf16[2,640]{1,0:T(2,128)(2,1)S(1)}, bf16[2,640]{1,0:T(2,128)(2,1)S(1)}, u32[]{:S(2)}, u32[]{:S(2)}) %collective-permute-start) | collective-permute-done | bytes 2592 | tf_op jit(solution)/shard_map/ppermute | solution.py:320
  8.5 0.5 slice.42.rim_qk
  9.0 0.6 slice.43.rim_v
  9.6 5.1 %first.1 = (bf16[512,256]{1,0:T(8,128)(2,1)}, bf16[512,256]{1,0:T(8,128)(2,1)}, bf16[512,256]{1,0:T(8,128)(2,1)}, bf16[512,1024]{1,0:T(8,128)(2,1)}, f32[640,128]{1,0:T(8,128)}) custom-call(bf16[512,64]{1,0:T(8,128)(2,1)} %copy-done.6, bf16[512,64]{1,0:T(8,128)(2,1)} %copy-done.7, bf16[512,512]{1,0:T(8,128)(2,1)} %v_in.3, bf16[2,128]{1,0:T(2,128)(2,1)} %slice.42.rim_qk, ...), custom_call_target="tpu_custom_call" | custom-call | flops 2147483648 | bytes 4194304 | tf_op jit(solution)/shard_map/first/pallas_call | solution.py:413
  14.7 20.2 %all-to-all-start = ((f32[128,1,640]{2,1,0:T(1,128)}), f32[128,1,640]{2,1,0:T(1,128)S(1)}, u32[]{:S(2)}, u32[]{:S(2)}) async-start(f32[128,1,640]{2,1,0:T(1,128)} %bitcast.20), calls=%async_computation | async-start | bytes 655360 | tf_op jit(solution)/shard_map/all_to_all | solution.py:325
  35.0 3.5 %collective-permute-start.1 = (bf16[128,2048]{1,0:T(8,128)(2,1)S(1)}, bf16[128,2048]{1,0:T(8,128)(2,1)}, u32[]{:S(2)}, u32[]{:S(2)}) collective-permute-start(bf16[128,2048]{1,0:T(8,128)(2,1)S(1)} %copy-done.2), channel_id=1, source_target_pairs={{0,1},{1,2},{2,3},{3,0},{4,5},{5,6},{6,7},{7,4},{8,9},{9,10},{10,1... | collective-permute-start | bytes 1572872 | tf_op jit(solution)/shard_map/ppermute | solution.py:335
  38.4 3.6 %collective-permute-start.3 = (bf16[128,2048]{1,0:T(8,128)(2,1)S(1)}, bf16[128,2048]{1,0:T(8,128)(2,1)S(1)}, u32[]{:S(2)}, u32[]{:S(2)}) collective-permute-start(bf16[128,2048]{1,0:T(8,128)(2,1)S(1)} %copy-done.2), channel_id=1, source_target_pairs={{0,3},{1,0},{2,1},{3,2},{4,7},{5,4},{6,5},{7,6},{8,11},{9,8},{10,9... | collective-permute-start | bytes 1572872 | tf_op jit(solution)/shard_map/ppermute | solution.py:335
  42.0 3.9 %collective-permute-start.2 = (bf16[128,2048]{1,0:T(8,128)(2,1)S(1)}, bf16[128,2048]{1,0:T(8,128)(2,1)}, u32[]{:S(2)}, u32[]{:S(2)}) collective-permute-start(bf16[128,2048]{1,0:T(8,128)(2,1)S(1)} %copy-done.2), channel_id=1, source_target_pairs={{0,2},{1,3},{2,0},{3,1},{4,6},{5,7},{6,4},{7,5},{8,10},{9,11},{10,... | collective-permute-start | bytes 1572872 | tf_op jit(solution)/shard_map/ppermute | solution.py:335
  46.0 1.6 broadcast_in_dim.4
  47.6 0.8 constant_dynamic-update-slice_fusion.5
  48.4 12.5 %all-to-all-done = f32[128,1,640]{2,1,0:T(1,128)S(1)} async-done(((f32[128,1,640]{2,1,0:T(1,128)}), f32[128,1,640]{2,1,0:T(1,128)S(1)}, u32[]{:S(2)}, u32[]{:S(2)}) %all-to-all-start) | async-done | bytes 327712 | tf_op jit(solution)/shard_map/all_to_all | solution.py:325
  60.9 0.3 convolution_bitcast_fusion.1
  61.2 1.1 copy.57
  62.3 6.4 %all-to-all-start.1 = ((f32[128,1,640]{2,1,0:T(1,128)}), f32[128,1,640]{2,1,0:T(1,128)S(1)}, u32[]{:S(2)}, u32[]{:S(2)}) async-start(f32[128,1,640]{2,1,0:T(1,128)} %copy.57), calls=%async_computation.1 | async-start | bytes 655360 | tf_op jit(solution)/shard_map/all_to_all | solution.py:330
  68.7 5.0 %local.1 = (f32[512,512]{1,0:T(8,128)}, f32[512,512]{1,0:T(8,128)}) custom-call(bf16[512,256]{1,0:T(8,128)(2,1)} %get-tuple-element.29.q4, bf16[512,256]{1,0:T(8,128)(2,1)} %get-tuple-element.31.k5, bf16[512,1024]{1,0:T(8,128)(2,1)} %get-tuple-element.32.vb), custom_call_target="tpu_custom_call" | custom-call | flops 4294967296 | bytes 4194304 | tf_op jit(solution)/shard_map/local/pallas_call | solution.py:423
  73.8 0.0 collective-permute-done.1
  73.8 1.9 constant_dynamic-update-slice_fusion.4
  75.7 1.9 constant_dynamic-update-slice_fusion.3
  77.6 0.0 collective-permute-done.3
  77.6 0.8 constant_dynamic-update-slice_fusion.2
  78.4 3.8 %fusion.5.up = f32[512,512]{1,0:T(8,128)} fusion(bf16[512,2048]{1,0:T(8,128)(2,1)} %constant_dynamic-update-slice_fusion.2, bf16[512,2048]{1,0:T(8,128)(2,1)S(1)} %copy-done), kind=kOutput, calls=%fused_computation.20 | convolution fusion | flops 1073741824 | bytes 5242880 | tf_op jit(solution)/shard_map/dot_general | solution.py:420
  82.2 12.5 %all-to-all-done.1 = f32[128,1,640]{2,1,0:T(1,128)S(1)} async-done(((f32[128,1,640]{2,1,0:T(1,128)}), f32[128,1,640]{2,1,0:T(1,128)S(1)}, u32[]{:S(2)}, u32[]{:S(2)}) %all-to-all-start.1) | async-done | bytes 327712 | tf_op jit(solution)/shard_map/all_to_all | solution.py:330
  94.8 0.7 copy-done.4
  95.5 5.5 %middle.1 = (bf16[512,512]{1,0:T(8,128)(2,1)}, f32[512,512]{1,0:T(8,128)}, f32[512,512]{1,0:T(8,128)}, f32[640,128]{1,0:T(8,128)}) custom-call(bf16[512,256]{1,0:T(8,128)(2,1)} %get-tuple-element.29.q4, f32[640,128]{1,0:T(8,128)} %bitcast.18, f32[512,512]{1,0:T(8,128)} %get-tuple-element.33.numer, f32[512,512]{1,0:T(8,128)} %get-tuple-element.34.denom, ...), custom_call_target="tpu_custom_call" | custom-call | flops 4294967296 | bytes 4194304 | tf_op jit(solution)/shard_map/middle/pallas_call | solution.py:428
  101.0 6.6 %all-to-all-start.2 = ((f32[128,1,640]{2,1,0:T(1,128)}), f32[128,1,640]{2,1,0:T(1,128)S(1)}, u32[]{:S(2)}, u32[]{:S(2)}) async-start(f32[128,1,640]{2,1,0:T(1,128)} %bitcast.21), calls=%async_computation.2 | async-start | bytes 655360 | tf_op jit(solution)/shard_map/all_to_all | solution.py:325
  107.7 26.0 %all-to-all-done.2 = f32[128,1,640]{2,1,0:T(1,128)S(1)} async-done(((f32[128,1,640]{2,1,0:T(1,128)}), f32[128,1,640]{2,1,0:T(1,128)S(1)}, u32[]{:S(2)}, u32[]{:S(2)}) %all-to-all-start.2) | async-done | bytes 327712 | tf_op jit(solution)/shard_map/all_to_all | solution.py:325
  133.7 0.3 convolution_bitcast_fusion
  134.0 1.1 copy.59
  135.1 6.5 %all-to-all-start.3 = ((f32[128,1,640]{2,1,0:T(1,128)}), f32[128,1,640]{2,1,0:T(1,128)S(1)}, u32[]{:S(2)}, u32[]{:S(2)}) async-start(f32[128,1,640]{2,1,0:T(1,128)} %copy.59), calls=%async_computation.3 | async-start | bytes 655360 | tf_op jit(solution)/shard_map/all_to_all | solution.py:330
  141.6 1.3 fusion.6
  142.9 1.9 constant_dynamic-slice_fusion.2
  144.8 1.1 copy-done.1
  145.9 3.5 %collective-permute-start.4 = (f32[128,2048]{1,0:T(8,128)}, f32[128,2048]{1,0:T(8,128)S(1)}, u32[]{:S(2)}, u32[]{:S(2)}) collective-permute-start(f32[128,2048]{1,0:T(8,128)} %get-tuple-element.79), channel_id=1, source_target_pairs={{0,1},{1,2},{2,3},{3,0},{4,5},{5,6},{6,7},{7,4},{8,9},{9,10},{10,1... | collective-permute-start | bytes 3145736 | tf_op jit(solution)/shard_map/ppermute | solution.py:335
  149.4 3.6 %collective-permute-start.6 = (f32[128,2048]{1,0:T(8,128)}, f32[128,2048]{1,0:T(8,128)}, u32[]{:S(2)}, u32[]{:S(2)}) collective-permute-start(f32[128,2048]{1,0:T(8,128)} %get-tuple-element.80), channel_id=1, source_target_pairs={{0,3},{1,0},{2,1},{3,2},{4,7},{5,4},{6,5},{7,6},{8,11},{9,8},{10,9... | collective-permute-start | bytes 3145736 | tf_op jit(solution)/shard_map/ppermute | solution.py:335
  152.9 3.9 %collective-permute-start.5 = (f32[128,2048]{1,0:T(8,128)}, f32[128,2048]{1,0:T(8,128)}, u32[]{:S(2)}, u32[]{:S(2)}) collective-permute-start(f32[128,2048]{1,0:T(8,128)} %get-tuple-element.81), channel_id=1, source_target_pairs={{0,2},{1,3},{2,0},{3,1},{4,6},{5,7},{6,4},{7,5},{8,10},{9,11},{10,... | collective-permute-start | bytes 3145736 | tf_op jit(solution)/shard_map/ppermute | solution.py:335
  156.8 10.9 %inner.1 = (f32[512,64]{1,0:T(8,128)}, f32[512,64]{1,0:T(8,128)}, f32[512,512]{1,0:T(8,128)}) custom-call(bf16[512,256]{1,0:T(8,128)(2,1)} %get-tuple-element.29.q4, bf16[512,256]{1,0:T(8,128)(2,1)} %get-tuple-element.36.k4, bf16[512,256]{1,0:T(8,128)(2,1)} %get-tuple-element.31.k5, bf16[512,1024]{1,0:T(8,128)(2,1)} %get-tuple-element.32.vb, ...), custom_call_target="tpu_custom_call" | custom-call | flops 8589934592 | bytes 4194304 | tf_op jit(solution)/shard_map/inner/pallas_call | solution.py:437
  167.7 0.0 copy-start.5
  167.7 0.7 copy-done.5
  168.4 7.9 %last.1 = (f32[512,64]{1,0:T(8,128)}, f32[512,64]{1,0:T(8,128)}, f32[512,512]{1,0:T(8,128)}, f32[8,128]{1,0:T(8,128)}, f32[8,512]{1,0:T(8,128)}) custom-call(bf16[512,64]{1,0:T(8,128)(2,1)} %copy-done.6, bf16[512,64]{1,0:T(8,128)(2,1)} %copy-done.7, bf16[512,512]{1,0:T(8,128)(2,1)} %v_in.3, bf16[2,128]{1,0:T(2,128)(2,1)} %slice.42.rim_qk, ...), custom_call_target="tpu_custom_call" | custom-call | flops 4294967296 | bytes 4194304 | tf_op jit(solution)/shard_map/last/pallas_call | solution.py:446
  176.3 0.7 constant_dynamic-update-slice_fusion.1
  177.0 0.7 constant_dynamic-update-slice_fusion
  177.7 1.9 collective-permute-start.7
  179.7 3.6 %psum.14 = f32[3,640]{1,0:T(4,128)S(1)} all-reduce(f32[3,640]{1,0:T(4,128)S(1)} %slice.45), channel_id=1, replica_groups=mesh['x'=4,'z'=16,'core'=2,'head'=4] {'core'}, use_global_device_ids=true, to_apply=%region_0.1 | all-reduce | flops 1920 | bytes 15360 | tf_op jit(solution)/shard_map/psum | solution.py:455
  183.3 0.7 broadcast_in_dim.10
  184.0 12.1 %all-to-all-start.4 = ((f32[16,3,640]{2,1,0:T(4,128)}), f32[16,3,640]{2,1,0:T(4,128)S(1)}, u32[]{:S(2)}, u32[]{:S(2)}) async-start(f32[16,3,640]{2,1,0:T(4,128)} %broadcast_in_dim.10), calls=%async_computation.4 | async-start | bytes 327680 | tf_op jit(solution)/shard_map/all_to_all | solution.py:361
  196.1 0.0 collective-permute-done.4
  196.1 2.0 collective-permute-done.5
  198.2 2.9 %add_convert_fusion = bf16[128,2048]{1,0:T(8,128)(2,1)} fusion(f32[128,2048]{1,0:T(8,128)} %collective-permute-done.6, f32[128,2048]{1,0:T(8,128)} %collective-permute-done.5, f32[128,2048]{1,0:T(8,128)S(1)} %collective-permute-done.4, f32[512,2048]{1,0:T(8,128)} %copy-done.1, s32[]{:T(128)S(6)} %select_n.63), kind=kLoop, calls=%fused_computation.2 | loop fusion | flops 1048576 | bytes 4718596 | tf_op jit(solution)/shard_map/convert_element_type | solution.py:445
  201.1 0.6 copy-done.8
  201.7 1.5 rims.1
  203.2 1.7 copy.63
  204.9 1.7 copy.64
  206.6 4.6 %all-to-all-done.4 = f32[16,3,640]{2,1,0:T(4,128)S(1)} async-done(((f32[16,3,640]{2,1,0:T(4,128)}), f32[16,3,640]{2,1,0:T(4,128)S(1)}, u32[]{:S(2)}, u32[]{:S(2)}) %all-to-all-start.4) | async-done | bytes 122912 | tf_op jit(solution)/shard_map/all_to_all | solution.py:361
  211.3 17.4 %psum.15 = f32[3,640]{1,0:T(4,128)S(1)} all-reduce(f32[3,640]{1,0:T(4,128)S(1)} %reduce_sum.9), channel_id=1, replica_groups=mesh['x'=4,'z'=16,'core'=2,'head'=4] {'x'}, use_global_device_ids=true, to_apply=%region_2.3 | all-reduce | flops 1920 | bytes 15360 | tf_op jit(solution)/shard_map/psum | solution.py:457
  228.7 0.6 fusion.4
  229.3 0.6 slice.48
  (19 shorter events, 0.1 us)
Async XLA Ops:
  0.6 77.8 %copy-start = (bf16[512,2048]{1,0:T(8,128)(2,1)S(1)}, bf16[512,2048]{1,0:T(8,128)(2,1)}, u32[]{:S(2)}) copy-start(bf16[512,2048]{1,0:T(8,128)(2,1)} %param.16) | copy-start | bytes 6291460
  2.5 7.1 %copy-start.6 = (bf16[512,64]{1,0:T(8,128)(2,1)}, bf16[512,64]{1,0:T(8,128)(2,1)S(1)}, u32[]{:S(2)}) copy-start(bf16[512,64]{1,0:T(8,128)(2,1)S(1)} %copy.54.q_in) | copy-start | bytes 196612
  3.5 6.1 %copy-start.7 = (bf16[512,64]{1,0:T(8,128)(2,1)}, bf16[512,64]{1,0:T(8,128)(2,1)S(1)}, u32[]{:S(2)}) copy-start(bf16[512,64]{1,0:T(8,128)(2,1)S(1)} %copy.55.k_in) | copy-start | bytes 196612
  3.6 4.9 %collective-permute-start = (bf16[2,640]{1,0:T(2,128)(2,1)S(1)}, bf16[2,640]{1,0:T(2,128)(2,1)S(1)}, u32[]{:S(2)}, u32[]{:S(2)}) collective-permute-start(bf16[2,640]{1,0:T(2,128)(2,1)S(1)} %pad_maximum_fusion), channel_id=1, source_target_pairs={{0,4},{4,8},{8,12},{12,16},{16,20},{20,24},{24,28},{28,32},{32,36}... | collective-permute-start | bytes 7688 | tf_op jit(solution)/shard_map/ppermute | solution.py:320
  9.6 25.3 %copy-start.2 = (bf16[128,2048]{1,0:T(8,128)(2,1)S(1)}, bf16[128,2048]{1,0:T(8,128)(2,1)}, u32[]{:S(2)}) copy-start(bf16[128,2048]{1,0:T(8,128)(2,1)} %param.17) | copy-start | bytes 1572868
  14.7 46.2 %all-to-all-start = ((f32[128,1,640]{2,1,0:T(1,128)}), f32[128,1,640]{2,1,0:T(1,128)S(1)}, u32[]{:S(2)}, u32[]{:S(2)}) async-start(f32[128,1,640]{2,1,0:T(1,128)} %bitcast.20), calls=%async_computation | async-start | bytes 655360 | tf_op jit(solution)/shard_map/all_to_all | solution.py:325
  35.0 38.8 %collective-permute-start.1 = (bf16[128,2048]{1,0:T(8,128)(2,1)S(1)}, bf16[128,2048]{1,0:T(8,128)(2,1)}, u32[]{:S(2)}, u32[]{:S(2)}) collective-permute-start(bf16[128,2048]{1,0:T(8,128)(2,1)S(1)} %copy-done.2), channel_id=1, source_target_pairs={{0,1},{1,2},{2,3},{3,0},{4,5},{5,6},{6,7},{7,4},{8,9},{9,10},{10,1... | collective-permute-start | bytes 1572872 | tf_op jit(solution)/shard_map/ppermute | solution.py:335
  38.4 39.1 %collective-permute-start.3 = (bf16[128,2048]{1,0:T(8,128)(2,1)S(1)}, bf16[128,2048]{1,0:T(8,128)(2,1)S(1)}, u32[]{:S(2)}, u32[]{:S(2)}) collective-permute-start(bf16[128,2048]{1,0:T(8,128)(2,1)S(1)} %copy-done.2), channel_id=1, source_target_pairs={{0,3},{1,0},{2,1},{3,2},{4,7},{5,4},{6,5},{7,6},{8,11},{9,8},{10,9... | collective-permute-start | bytes 1572872 | tf_op jit(solution)/shard_map/ppermute | solution.py:335
  42.0 33.6 %collective-permute-start.2 = (bf16[128,2048]{1,0:T(8,128)(2,1)S(1)}, bf16[128,2048]{1,0:T(8,128)(2,1)}, u32[]{:S(2)}, u32[]{:S(2)}) collective-permute-start(bf16[128,2048]{1,0:T(8,128)(2,1)S(1)} %copy-done.2), channel_id=1, source_target_pairs={{0,2},{1,3},{2,0},{3,1},{4,6},{5,7},{6,4},{7,5},{8,10},{9,11},{10,... | collective-permute-start | bytes 1572872 | tf_op jit(solution)/shard_map/ppermute | solution.py:335
  62.3 32.5 %all-to-all-start.1 = ((f32[128,1,640]{2,1,0:T(1,128)}), f32[128,1,640]{2,1,0:T(1,128)S(1)}, u32[]{:S(2)}, u32[]{:S(2)}) async-start(f32[128,1,640]{2,1,0:T(1,128)} %copy.57), calls=%async_computation.1 | async-start | bytes 655360 | tf_op jit(solution)/shard_map/all_to_all | solution.py:330
  94.8 0.7 copy-start.4
  101.0 40.6 %copy-start.3 = (bf16[512,512]{1,0:T(8,128)(2,1)S(1)}, bf16[512,512]{1,0:T(8,128)(2,1)}, u32[]{:S(2)}) copy-start(bf16[512,512]{1,0:T(8,128)(2,1)} %get-tuple-element.35) | copy-start | bytes 1572868
  101.0 32.6 %all-to-all-start.2 = ((f32[128,1,640]{2,1,0:T(1,128)}), f32[128,1,640]{2,1,0:T(1,128)S(1)}, u32[]{:S(2)}, u32[]{:S(2)}) async-start(f32[128,1,640]{2,1,0:T(1,128)} %bitcast.21), calls=%async_computation.2 | async-start | bytes 655360 | tf_op jit(solution)/shard_map/all_to_all | solution.py:325
  135.1 32.6 %all-to-all-start.3 = ((f32[128,1,640]{2,1,0:T(1,128)}), f32[128,1,640]{2,1,0:T(1,128)S(1)}, u32[]{:S(2)}, u32[]{:S(2)}) async-start(f32[128,1,640]{2,1,0:T(1,128)} %copy.59), calls=%async_computation.3 | async-start | bytes 655360 | tf_op jit(solution)/shard_map/all_to_all | solution.py:330
  142.9 3.0 %copy-start.1 = (f32[512,2048]{1,0:T(8,128)}, f32[512,2048]{1,0:T(8,128)S(1)}, u32[]{:S(2)}) copy-start(f32[512,2048]{1,0:T(8,128)S(1)} %fusion.6) | copy-start | bytes 12582916
  145.9 50.2 %collective-permute-start.4 = (f32[128,2048]{1,0:T(8,128)}, f32[128,2048]{1,0:T(8,128)S(1)}, u32[]{:S(2)}, u32[]{:S(2)}) collective-permute-start(f32[128,2048]{1,0:T(8,128)} %get-tuple-element.79), channel_id=1, source_target_pairs={{0,1},{1,2},{2,3},{3,0},{4,5},{5,6},{6,7},{7,4},{8,9},{9,10},{10,1... | collective-permute-start | bytes 3145736 | tf_op jit(solution)/shard_map/ppermute | solution.py:335
  149.4 46.8 %collective-permute-start.6 = (f32[128,2048]{1,0:T(8,128)}, f32[128,2048]{1,0:T(8,128)}, u32[]{:S(2)}, u32[]{:S(2)}) collective-permute-start(f32[128,2048]{1,0:T(8,128)} %get-tuple-element.80), channel_id=1, source_target_pairs={{0,3},{1,0},{2,1},{3,2},{4,7},{5,4},{6,5},{7,6},{8,11},{9,8},{10,9... | collective-permute-start | bytes 3145736 | tf_op jit(solution)/shard_map/ppermute | solution.py:335
  152.9 45.2 %collective-permute-start.5 = (f32[128,2048]{1,0:T(8,128)}, f32[128,2048]{1,0:T(8,128)}, u32[]{:S(2)}, u32[]{:S(2)}) collective-permute-start(f32[128,2048]{1,0:T(8,128)} %get-tuple-element.81), channel_id=1, source_target_pairs={{0,2},{1,3},{2,0},{3,1},{4,6},{5,7},{6,4},{7,5},{8,10},{9,11},{10,... | collective-permute-start | bytes 3145736 | tf_op jit(solution)/shard_map/ppermute | solution.py:335
  167.7 0.7 copy-start.5
  177.7 23.4 %collective-permute-start.7 = (f32[2,640]{1,0:T(2,128)S(1)}, f32[2,640]{1,0:T(2,128)S(1)}, u32[]{:S(2)}, u32[]{:S(2)}) collective-permute-start(f32[2,640]{1,0:T(2,128)S(1)} %slice.44), channel_id=1, source_target_pairs={{4,0},{8,4},{12,8},{16,12},{20,16},{24,20},{28,24},{32,28},{36,32}... | collective-permute-start | bytes 15368 | tf_op jit(solution)/shard_map/ppermute | solution.py:320
  184.0 27.2 %all-to-all-start.4 = ((f32[16,3,640]{2,1,0:T(4,128)}), f32[16,3,640]{2,1,0:T(4,128)S(1)}, u32[]{:S(2)}, u32[]{:S(2)}) async-start(f32[16,3,640]{2,1,0:T(4,128)} %broadcast_in_dim.10), calls=%async_computation.4 | async-start | bytes 327680 | tf_op jit(solution)/shard_map/all_to_all | solution.py:361
  201.1 0.6 copy-start.8

commit v2 on v1

--- a/solution.py
+++ b/solution.py
@@ -119,7 +119,7 @@
     q4, k4, k5, vb, state, narrow, broad,
 ):
     head = pl.program_id(0)
-    length = q_in.shape[0]
+    length = q_in.shape[1]
 
     @pl.when(head == 0)
     def _():
@@ -128,7 +128,7 @@
             (q_in, taps_q, rim[:, :64], q4),
             (k_in, taps_k, rim[:, 64:], k4),
         ):
-            extend(narrow, source[...], edge)
+            extend(narrow, source[...].astype(F32).T, edge)
             x = convolve(narrow, taps[...], length)
             high = x.astype(BF16).astype(F32)
             rest = x - high
@@ -239,20 +239,22 @@
     )
 
 
-def edges(scratch, grad, length):
-    sums = [
-        jnp.sum(grad * scratch[8 - tap : length + 8 - tap, :], axis=0, keepdims=True)
-        for tap in range(3)
-    ]
-    return jnp.concatenate(sums + [sums[0], grad[0:4, :]], axis=0)
+def tap_sums(scratch, grad, length):
+    return jnp.concatenate(
+        [
+            jnp.sum(grad * scratch[8 - tap : length + 8 - tap, :], axis=0, keepdims=True)
+            for tap in range(3)
+        ],
+        axis=0,
+    )
 
 
 def last_kernel(
     q_in, k_in, v_in, rim_qk, rim_v, taps_q, taps_k, taps_v, places, factors,
-    k4, vb, after, gq, kd, gv_in, grad_q, grad_k, grad_v, edge_qk, edge_v, narrow, broad, gk,
+    k4, vb, after, gq, kd, gv_in, grad_q, grad_k, grad_v, taps_out, heads_first, narrow, broad, gk,
 ):
     head = pl.program_id(0)
-    length = q_in.shape[0]
+    length = q_in.shape[1]
     later, total = unpack(after[...])
     later_high, later_low = halves(later)
     value = vb[...]
@@ -282,7 +284,14 @@
     value_grad = gv_in[...] + mm((first * second).astype(BF16), later_high, 1, 0)
     grad_v[...] = conv_back(broad, value_grad, taps_v[...], length)
     extend(broad, v_in[...], rim_v[...].astype(F32))
-    edge_v[...] = edges(broad, value_grad, length)
+    sums = tap_sums(broad, value_grad, length)
+    heads = heads_first.shape[1] // VD - 1
+    for index in range(heads):
+
+        @pl.when(head == index)
+        def _(index=index):
+            taps_out[3 * index : 3 * index + 3, :] = sums
+            heads_first[:, (index + 1) * VD : (index + 2) * VD] = value_grad[0:2, :]
 
     @pl.when(head == pl.num_programs(0) - 1)
     def _():
@@ -292,10 +301,12 @@
             (q_in, taps_q, rim[:, :64], gq[...], grad_q),
             (k_in, taps_k, rim[:, 64:], gk[...], grad_k),
         ):
-            target[...] = conv_back(narrow, grad, taps[...], length)
-            extend(narrow, source[...], edge)
-            found.append(edges(narrow, grad, length))
-        edge_qk[...] = jnp.concatenate(found, axis=1)
+            target[...] = conv_back(narrow, grad, taps[...], length).T
+            extend(narrow, source[...].astype(F32).T, edge)
+            found.append(tap_sums(narrow, grad, length))
+        taps_out[3 * heads : 3 * heads + 3, :] = jnp.concatenate(found, axis=1)
+        taps_out[3 * heads + 3 :, :] = jnp.zeros((13 - 3 * heads, VD), F32)
+        heads_first[:, :VD] = jnp.concatenate([gq[0:2, :], gk[0:2, :]], axis=1)
 
 
 def rim_kernel(tail, taps_q, taps_k, taps_v, q_in, k_in, v_in, grad_q, grad_k, grad_v):
@@ -311,6 +322,8 @@
         weights = taps[...]
         extra = jnp.where(row == 6, weights[2:3, :] * one, 0.0)
         extra = extra + jnp.where(row == 7, weights[1:2, :] * one + weights[2:3, :] * two, 0.0)
+        if start < 128:
+            extra = jnp.concatenate([jnp.zeros((120, width), F32), extra], axis=0).T
         target[...] = source[...] + extra
 
 
@@ -320,14 +333,16 @@
     return lax.ppermute(block, axis, route)
 
 
-def carried_in(packed, reverse):
+def carried_in(packed, reverse, ahead=()):
     ranks = lax.axis_size(SEQ)
     everyone = lax.all_to_all(packed.reshape(ranks, -1), SEQ, 0, 0, tiled=True)
     rows = lax.broadcasted_iota(jnp.int32, (ranks, ranks), 0)
     cols = lax.broadcasted_iota(jnp.int32, (ranks, ranks), 1)
     reached = (cols > rows) if reverse else (cols < rows)
     sums = jnp.dot(reached.astype(F32), everyone, precision=HIGHEST)
-    return lax.all_to_all(sums, SEQ, 0, 0, tiled=True).reshape(packed.shape)
+    if ahead:
+        sums, ahead = lax.optimization_barrier((sums, ahead))
+    return lax.all_to_all(sums, SEQ, 0, 0, tiled=True).reshape(packed.shape), ahead
 
 
 def turned(block, axis, distance):
@@ -400,13 +415,15 @@
     rim = from_behind(
         jnp.concatenate([x[length - 2 :] for x in (query_in, key_in, value_in)], axis=1), SEQ, 1
     )
-    rim_qk, rim_v = rim[:, : 2 * keys], rim[:, 2 * keys :]
+    query_cols, key_cols = query_in.T, key_in.T
+    upright = whole(keys, length)
     conv_ins = [
-        narrow, narrow, per_head(length), whole(2, 2 * keys), per_head(2),
+        upright, upright, per_head(length), whole(2, 2 * keys),
+        pl.BlockSpec((2, VD), lambda h: (0, h + 1)),
         whole(3, keys), whole(3, keys), per_head(3), table, table,
     ]
     conv_args = (
-        query_in, key_in, value_in, rim_qk, rim_v,
+        query_cols, key_cols, value_in, rim, rim,
         conv_query, conv_key, conv_value, places, factors,
     )
     buffers = [pltpu.VMEM((length + 8, keys), F32), pltpu.VMEM((length + 8, VD), F32)]
@@ -424,7 +441,7 @@
         local_kernel, "local", [pieces, pieces, pairs],
         [per_head(length)] * 2, [arr(length, values)] * 2, 4 << 30,
     )(q4, k5, vb)
-    before = carried_in(local_state, False)
+    before, _ = carried_in(local_state, False)
     att, ng, dg, grad_state = call(
         middle_kernel, "middle",
         [pieces, packs] + [per_head(length)] * 3 + [table, table],
@@ -433,7 +450,6 @@
         + [arr(heads * ROWS, VD)],
         4 << 30,
     )(q4, before, numer, denom, upstream, places, factors)
-    after = carried_in(grad_state, True)
     gq, kd, gv = call(
         inner_kernel, "inner",
         [pieces] * 3 + [pairs, packs] + [per_head(length)] * 2 + [table, table],
@@ -441,22 +457,26 @@
         [arr(length, keys)] * 2 + [arr(length, values)],
         8 << 30,
     )(q4, k4, k5, vb, before, ng, dg, places, factors)
+    after, (gq, kd, gv) = carried_in(grad_state, True, (gq, kd, gv))
     partial = jnp.dot(att, out_proj, preferred_element_type=F32)
     mixed = scattered(partial, "head").astype(BF16)
-    grad_query, grad_key, grad_value, edge_qk, edge_v = call(
+    grad_query, grad_key, grad_value, taps, first_rows = call(
         last_kernel, "last",
         conv_ins + [pieces, pairs, packs, narrow, narrow, per_head(length)],
-        [narrow, narrow, per_head(length), whole(8, 2 * keys), per_head(8)],
-        [arr(length, keys)] * 2 + [arr(length, values), arr(8, 2 * keys), arr(8, values)],
+        [upright, upright, per_head(length), whole(16, VD), whole(2, 2 * keys + values)],
+        [arr(keys, length)] * 2
+        + [arr(length, values), arr(16, VD), arr(2, 2 * keys + values)],
         4 << 30, buffers + [pltpu.VMEM((length, keys), F32)],
     )(*conv_args, k4, vb, after, gq, kd, gv)
-    edge = jnp.concatenate([edge_qk, edge_v], axis=1)
-    tail = from_behind(edge[4:6], SEQ, -1)
-    taps = lax.psum(edge[:3], "core")
-    taps = jnp.sum(to_all(taps, "z").reshape(lax.axis_size("z"), 3, -1), axis=0)
-    taps = lax.psum(taps, "x")
-    last = length // 8 - 1
-    rims = [pl.BlockSpec((8, n), lambda i: (last, 0)) for n in (keys, keys, values)]
+    tail = from_behind(first_rows, SEQ, -1)
+    for axis in ("z", ("x", "core")):
+        everyone = to_all(taps, axis).reshape((lax.axis_size(axis),) + taps.shape)
+        taps = jnp.sum(everyone, axis=0)
+    rims = [
+        pl.BlockSpec((keys, VD), lambda i: (0, length // VD - 1)),
+        pl.BlockSpec((keys, VD), lambda i: (0, length // VD - 1)),
+        pl.BlockSpec((8, values), lambda i: (length // 8 - 1, 0)),
+    ]
     grad_query, grad_key, grad_value = pl.pallas_call(
         rim_kernel,
         name="rims",
@@ -464,17 +484,19 @@
         in_specs=[whole(2, 2 * keys + values), whole(3, keys), whole(3, keys), whole(3, values)]
         + rims,
         out_specs=rims,
-        out_shape=[arr(length, keys)] * 2 + [arr(length, values)],
+        out_shape=[arr(keys, length)] * 2 + [arr(length, values)],
         input_output_aliases={4: 0, 5: 1, 6: 2},
     )(tail, conv_query, conv_key, conv_value, grad_query, grad_key, grad_value)
+    value_taps = taps[: 3 * heads].reshape(heads, 3, VD).transpose(1, 0, 2).reshape(3, values)
+    other_taps = taps[3 * heads : 3 * heads + 3]
     return (
         mixed,
-        grad_query,
-        grad_key,
+        grad_query.T,
+        grad_key.T,
         grad_value,
-        taps[:, :keys],
-        taps[:, keys : 2 * keys],
-        taps[:, 2 * keys :],
+        other_taps[:, :keys],
+        other_taps[:, keys:],
+        value_taps,
     )
 
 

time: 231 us -> 208 us (0.900)
  the two profiles are of different devices: /device:TPU:32 before, /device:TPU:1 now
where the time goes in v2:
time: 208 us; the launch traced here: 207 us
  starting transfers between devices  78.2 us (38%)
  waiting for transfers between devices  62.5 us (30%)
  Pallas kernels  35.8 us (17%)
  local copies, waits for them, and re-layouts  20.7 us (10%)
  matrix products  5.74 us (3%)
  other arithmetic  3.02 us (1%)
    all_to_all x2, waiting for transfers between devices, carried_in(): everyone = lax.all_to_all(packed.reshape(ranks, -1), SEQ, 0, 0, tiled=True)  27.3 us
    all_to_all x2, starting transfers between devices, carried_in(): everyone = lax.all_to_all(packed.reshape(ranks, -1), SEQ, 0, 0, tiled=True)  24.7 us
    all_to_all x2, waiting for transfers between devices, carried_in(): lax.all_to_all(sums, SEQ, 0, 0, tiled=True).reshape(packed.shape)  23 us
    ppermute x6, starting transfers between devices, turned(): lax.ppermute(block, axis, [(i, (i + distance) % size) for i in range(size)])  20.2 us
    all_to_all x2, starting transfers between devices, carried_in(): lax.all_to_all(sums, SEQ, 0, 0, tiled=True).reshape(packed.shape)  14 us
    pallas_call x1, Pallas kernels, body(): call(inner_kernel, 'inner', [pieces] * 3 + [pairs, packs] + [per_head(len...  10.8 us
    all_to_all x2, starting transfers between devices, to_all(): return lax.all_to_all(copies, axis, 0, 0, tiled=True)  10.7 us
    ppermute x2, starting transfers between devices, from_behind(): return lax.ppermute(block, axis, route)  8.56 us
  transfers between devices with their start and end apart: 14, of which 6 were waited for; matrix products, arithmetic and copies ran while one was open for 10% of the time, Pallas kernels for 12%

profile of v2, /device:TPU:1, one launch (start us, length us, event | category | flops | bytes accessed | tf_op | source)
XLA Modules:
  0.0 206.9 jit_solution(8168453025002746541)
XLA Ops:
  0.6 0.0 copy-start
  0.6 0.9 slice.23
  1.5 0.8 slice.21
  2.3 0.1 copy.39
  2.4 0.8 slice.22
  3.2 0.1 copy.40
  3.3 0.1 pad_maximum_fusion
  3.4 4.9 %collective-permute-start = (bf16[2,640]{1,0:T(2,128)(2,1)S(1)}, bf16[2,640]{1,0:T(2,128)(2,1)S(1)}, u32[]{:S(2)}, u32[]{:S(2)}) collective-permute-start(bf16[2,640]{1,0:T(2,128)(2,1)S(1)} %pad_maximum_fusion), channel_id=1, source_target_pairs={{0,4},{4,8},{8,12},{12,16},{16,20},{20,24},{24,28},{28,32},{32,36}... | collective-permute-start | bytes 7688 | tf_op jit(solution)/shard_map/ppermute | solution.py:333
  8.3 3.8 %collective-permute-done.rim_qk.rim_v = bf16[2,640]{1,0:T(2,128)(2,1)S(1)} collective-permute-done((bf16[2,640]{1,0:T(2,128)(2,1)S(1)}, bf16[2,640]{1,0:T(2,128)(2,1)S(1)}, u32[]{:S(2)}, u32[]{:S(2)}) %collective-permute-start) | collective-permute-done | bytes 2592 | tf_op jit(solution)/shard_map/ppermute | solution.py:333
  12.1 0.6 copy-done.7
  12.7 5.1 %first.1 = (bf16[512,256]{1,0:T(8,128)(2,1)}, bf16[512,256]{1,0:T(8,128)(2,1)}, bf16[512,256]{1,0:T(8,128)(2,1)}, bf16[512,1024]{1,0:T(8,128)(2,1)}, f32[640,128]{1,0:T(8,128)}) custom-call(bf16[64,512]{1,0:T(8,128)(2,1)} %bitcast.35, bf16[64,512]{1,0:T(8,128)(2,1)} %bitcast.37, bf16[512,512]{1,0:T(8,128)(2,1)} %v_in.3, bf16[2,640]{1,0:T(2,128)(2,1)} %copy-done.7, ...), custom_call_target="tpu_custom_call" | custom-call | flops 2147483648 | bytes 4194304 | tf_op jit(solution)/shard_map/first/pallas_call | solution.py:430
  17.8 17.7 %all-to-all-start = ((f32[128,1,640]{2,1,0:T(1,128)}), f32[128,1,640]{2,1,0:T(1,128)S(1)}, u32[]{:S(2)}, u32[]{:S(2)}) async-start(f32[128,1,640]{2,1,0:T(1,128)} %bitcast.26), calls=%async_computation | async-start | bytes 655360 | tf_op jit(solution)/shard_map/all_to_all | solution.py:338
  35.5 0.0 copy-done.2
  35.6 3.2 %collective-permute-start.1 = (bf16[128,2048]{1,0:T(8,128)(2,1)S(1)}, bf16[128,2048]{1,0:T(8,128)(2,1)}, u32[]{:S(2)}, u32[]{:S(2)}) collective-permute-start(bf16[128,2048]{1,0:T(8,128)(2,1)S(1)} %copy-done.2), channel_id=1, source_target_pairs={{0,1},{1,2},{2,3},{3,0},{4,5},{5,6},{6,7},{7,4},{8,9},{9,10},{10,1... | collective-permute-start | bytes 1572872 | tf_op jit(solution)/shard_map/ppermute | solution.py:350
  38.8 3.4 %collective-permute-start.3 = (bf16[128,2048]{1,0:T(8,128)(2,1)S(1)}, bf16[128,2048]{1,0:T(8,128)(2,1)S(1)}, u32[]{:S(2)}, u32[]{:S(2)}) collective-permute-start(bf16[128,2048]{1,0:T(8,128)(2,1)S(1)} %copy-done.2), channel_id=1, source_target_pairs={{0,3},{1,0},{2,1},{3,2},{4,7},{5,4},{6,5},{7,6},{8,11},{9,8},{10,9... | collective-permute-start | bytes 1572872 | tf_op jit(solution)/shard_map/ppermute | solution.py:350
  42.1 3.5 %collective-permute-start.2 = (bf16[128,2048]{1,0:T(8,128)(2,1)S(1)}, bf16[128,2048]{1,0:T(8,128)(2,1)}, u32[]{:S(2)}, u32[]{:S(2)}) collective-permute-start(bf16[128,2048]{1,0:T(8,128)(2,1)S(1)} %copy-done.2), channel_id=1, source_target_pairs={{0,2},{1,3},{2,0},{3,1},{4,6},{5,7},{6,4},{7,5},{8,10},{9,11},{10,... | collective-permute-start | bytes 1572872 | tf_op jit(solution)/shard_map/ppermute | solution.py:350
  45.8 1.6 broadcast_in_dim.6
  47.4 0.9 constant_dynamic-update-slice_fusion.3
  48.2 12.7 %all-to-all-done = f32[128,1,640]{2,1,0:T(1,128)S(1)} async-done(((f32[128,1,640]{2,1,0:T(1,128)}), f32[128,1,640]{2,1,0:T(1,128)S(1)}, u32[]{:S(2)}, u32[]{:S(2)}) %all-to-all-start) | async-done | bytes 327712 | tf_op jit(solution)/shard_map/all_to_all | solution.py:338
  60.9 0.3 convolution_bitcast_fusion
  61.2 1.1 copy.34
  62.3 7.0 %all-to-all-start.1 = ((f32[128,1,640]{2,1,0:T(1,128)}), f32[128,1,640]{2,1,0:T(1,128)S(1)}, u32[]{:S(2)}, u32[]{:S(2)}) async-start(f32[128,1,640]{2,1,0:T(1,128)} %copy.34), calls=%async_computation.1 | async-start | bytes 655360 | tf_op jit(solution)/shard_map/all_to_all | solution.py:345
  69.3 5.1 %local.1 = (f32[512,512]{1,0:T(8,128)}, f32[512,512]{1,0:T(8,128)}) custom-call(bf16[512,256]{1,0:T(8,128)(2,1)} %get-tuple-element.33.q4, bf16[512,256]{1,0:T(8,128)(2,1)} %get-tuple-element.35.k5, bf16[512,1024]{1,0:T(8,128)(2,1)} %get-tuple-element.36.vb), custom_call_target="tpu_custom_call" | custom-call | flops 4294967296 | bytes 4194304 | tf_op jit(solution)/shard_map/local/pallas_call | solution.py:440
  74.4 0.0 collective-permute-done.1
  74.4 1.9 constant_dynamic-update-slice_fusion.2
  76.2 0.0 collective-permute-done.2
  76.3 1.9 constant_dynamic-update-slice_fusion.1
  78.2 0.0 collective-permute-done.3
  78.2 0.8 constant_dynamic-update-slice_fusion
  79.0 3.8 %fusion.6.up = f32[512,512]{1,0:T(8,128)} fusion(bf16[512,2048]{1,0:T(8,128)(2,1)} %constant_dynamic-update-slice_fusion, bf16[512,2048]{1,0:T(8,128)(2,1)S(1)} %copy-done), kind=kOutput, calls=%fused_computation.18 | convolution fusion | flops 1073741824 | bytes 5242880 | tf_op jit(solution)/shard_map/dot_general | solution.py:437
  82.9 11.9 %all-to-all-done.1 = f32[128,1,640]{2,1,0:T(1,128)S(1)} async-done(((f32[128,1,640]{2,1,0:T(1,128)}), f32[128,1,640]{2,1,0:T(1,128)S(1)}, u32[]{:S(2)}, u32[]{:S(2)}) %all-to-all-start.1) | async-done | bytes 327712 | tf_op jit(solution)/shard_map/all_to_all | solution.py:345
  94.8 0.7 copy-done.5
  95.5 5.5 %middle.1 = (bf16[512,512]{1,0:T(8,128)(2,1)}, f32[512,512]{1,0:T(8,128)}, f32[512,512]{1,0:T(8,128)}, f32[640,128]{1,0:T(8,128)}) custom-call(bf16[512,256]{1,0:T(8,128)(2,1)} %get-tuple-element.33.q4, f32[640,128]{1,0:T(8,128)} %bitcast.28, f32[512,512]{1,0:T(8,128)} %get-tuple-element.37.numer, f32[512,512]{1,0:T(8,128)} %get-tuple-element.38.denom, ...), custom_call_target="tpu_custom_call" | custom-call | flops 4294967296 | bytes 4194304 | tf_op jit(solution)/shard_map/middle/pallas_call | solution.py:445
  101.0 7.0 %all-to-all-start.2 = ((f32[128,1,640]{2,1,0:T(1,128)}), f32[128,1,640]{2,1,0:T(1,128)S(1)}, u32[]{:S(2)}, u32[]{:S(2)}) async-start(f32[128,1,640]{2,1,0:T(1,128)} %bitcast.30), calls=%async_computation.2 | async-start | bytes 655360 | tf_op jit(solution)/shard_map/all_to_all | solution.py:338
  108.0 10.8 %inner.1 = (f32[512,64]{1,0:T(8,128)}, f32[512,64]{1,0:T(8,128)}, f32[512,512]{1,0:T(8,128)}) custom-call(bf16[512,256]{1,0:T(8,128)(2,1)} %get-tuple-element.33.q4, bf16[512,256]{1,0:T(8,128)(2,1)} %get-tuple-element.40.k4, bf16[512,256]{1,0:T(8,128)(2,1)} %get-tuple-element.35.k5, bf16[512,1024]{1,0:T(8,128)(2,1)} %get-tuple-element.36.vb, ...), custom_call_target="tpu_custom_call" | custom-call | flops 8589934592 | bytes 4194304 | tf_op jit(solution)/shard_map/inner/pallas_call | solution.py:453
  118.9 14.6 %all-to-all-done.2 = f32[128,1,640]{2,1,0:T(1,128)S(1)} async-done(((f32[128,1,640]{2,1,0:T(1,128)}), f32[128,1,640]{2,1,0:T(1,128)S(1)}, u32[]{:S(2)}, u32[]{:S(2)}) %all-to-all-start.2) | async-done | bytes 327712 | tf_op jit(solution)/shard_map/all_to_all | solution.py:338
  133.5 0.3 fusion
  133.8 1.1 copy.36
  134.9 7.0 %all-to-all-start.3 = ((f32[128,1,640]{2,1,0:T(1,128)}), f32[128,1,640]{2,1,0:T(1,128)S(1)}, u32[]{:S(2)}, u32[]{:S(2)}) async-start(f32[128,1,640]{2,1,0:T(1,128)} %copy.36), calls=%async_computation.3 | async-start | bytes 655360 | tf_op jit(solution)/shard_map/all_to_all | solution.py:345
  142.0 1.3 fusion.7
  143.2 1.8 constant_dynamic-slice_fusion.2
  145.0 1.1 copy-done.1
  146.2 3.2 %collective-permute-start.4 = (f32[128,2048]{1,0:T(8,128)}, f32[128,2048]{1,0:T(8,128)S(1)}, u32[]{:S(2)}, u32[]{:S(2)}) collective-permute-start(f32[128,2048]{1,0:T(8,128)} %get-tuple-element.59), channel_id=1, source_target_pairs={{0,1},{1,2},{2,3},{3,0},{4,5},{5,6},{6,7},{7,4},{8,9},{9,10},{10,1... | collective-permute-start | bytes 3145736 | tf_op jit(solution)/shard_map/ppermute | solution.py:350
  149.4 3.4 %collective-permute-start.6 = (f32[128,2048]{1,0:T(8,128)}, f32[128,2048]{1,0:T(8,128)}, u32[]{:S(2)}, u32[]{:S(2)}) collective-permute-start(f32[128,2048]{1,0:T(8,128)} %get-tuple-element.60), channel_id=1, source_target_pairs={{0,3},{1,0},{2,1},{3,2},{4,7},{5,4},{6,5},{7,6},{8,11},{9,8},{10,9... | collective-permute-start | bytes 3145736 | tf_op jit(solution)/shard_map/ppermute | solution.py:350
  152.8 3.5 %collective-permute-start.5 = (f32[128,2048]{1,0:T(8,128)}, f32[128,2048]{1,0:T(8,128)}, u32[]{:S(2)}, u32[]{:S(2)}) collective-permute-start(f32[128,2048]{1,0:T(8,128)} %get-tuple-element.61), channel_id=1, source_target_pairs={{0,2},{1,3},{2,0},{3,1},{4,6},{5,7},{6,4},{7,5},{8,10},{9,11},{10,... | collective-permute-start | bytes 3145736 | tf_op jit(solution)/shard_map/ppermute | solution.py:350
  156.3 11.1 %all-to-all-done.3 = f32[128,1,640]{2,1,0:T(1,128)S(1)} async-done(((f32[128,1,640]{2,1,0:T(1,128)}), f32[128,1,640]{2,1,0:T(1,128)S(1)}, u32[]{:S(2)}, u32[]{:S(2)}) %all-to-all-start.3) | async-done | bytes 327712 | tf_op jit(solution)/shard_map/all_to_all | solution.py:345
  167.4 0.7 copy-done.4
  168.1 7.7 %last.1 = (f32[64,512]{1,0:T(8,128)}, f32[64,512]{1,0:T(8,128)}, f32[512,512]{1,0:T(8,128)}, f32[16,128]{1,0:T(8,128)}, f32[2,640]{1,0:T(2,128)}) custom-call(bf16[64,512]{1,0:T(8,128)(2,1)} %bitcast.36, bf16[64,512]{1,0:T(8,128)(2,1)} %bitcast.38, bf16[512,512]{1,0:T(8,128)(2,1)} %v_in.3, bf16[2,640]{1,0:T(2,128)(2,1)} %copy-done.7, ...), custom_call_target="tpu_custom_call" | custom-call | flops 4294967296 | bytes 4194304 | tf_op jit(solution)/shard_map/last/pallas_call | solution.py:463
  175.8 1.4 broadcast_in_dim.7
  177.2 3.6 %all-to-all-start.4 = ((f32[16,16,128]{2,1,0:T(8,128)}), f32[16,16,128]{2,1,0:T(8,128)S(1)}, u32[]{:S(2)}, u32[]{:S(2)}) async-start(f32[16,16,128]{2,1,0:T(8,128)} %broadcast_in_dim.7), calls=%async_computation.4 | async-start | bytes 262144 | tf_op jit(solution)/shard_map/all_to_all | solution.py:376
  180.8 3.6 %collective-permute-start.7 = (f32[2,640]{1,0:T(2,128)}, f32[2,640]{1,0:T(2,128)S(1)}, u32[]{:S(2)}, u32[]{:S(2)}) collective-permute-start(f32[2,640]{1,0:T(2,128)} %get-tuple-element.51), channel_id=1, source_target_pairs={{4,0},{8,4},{12,8},{16,12},{20,16},{24,20},{28,24},{32,28},{36,32}... | collective-permute-start | bytes 15368 | tf_op jit(solution)/shard_map/ppermute | solution.py:333
  184.5 8.3 %all-to-all-done.4 = f32[16,16,128]{2,1,0:T(8,128)S(1)} async-done(((f32[16,16,128]{2,1,0:T(8,128)}), f32[16,16,128]{2,1,0:T(8,128)S(1)}, u32[]{:S(2)}, u32[]{:S(2)}) %all-to-all-start.4) | async-done | bytes 131104 | tf_op jit(solution)/shard_map/all_to_all | solution.py:376
  192.8 0.6 broadcast_in_dim.8
  193.5 7.1 %all-to-all-start.5 = ((f32[8,16,128]{2,1,0:T(8,128)}), f32[8,16,128]{2,1,0:T(8,128)S(1)}, u32[]{:S(2)}, u32[]{:S(2)}) async-start(f32[8,16,128]{2,1,0:T(8,128)} %broadcast_in_dim.8), calls=%async_computation.5 | async-start | bytes 131072 | tf_op jit(solution)/shard_map/all_to_all | solution.py:376
  200.6 0.0 collective-permute-done.4
  200.6 0.0 collective-permute-done.6
  200.6 0.0 collective-permute-done.5
  200.6 2.9 %add_convert_fusion = bf16[128,2048]{1,0:T(8,128)(2,1)} fusion(f32[128,2048]{1,0:T(8,128)} %collective-permute-done.6, f32[128,2048]{1,0:T(8,128)} %collective-permute-done.5, f32[128,2048]{1,0:T(8,128)S(1)} %collective-permute-done.4, f32[512,2048]{1,0:T(8,128)} %copy-done.1, s32[]{:T(128)S(6)} %select_n.63), kind=kLoop, calls=%fused_computation.1 | loop fusion | flops 1048576 | bytes 4718596 | tf_op jit(solution)/shard_map/convert_element_type | solution.py:462
  203.5 0.0 collective-permute-done.7.tail
  203.5 0.6 copy-done.6
  204.1 1.6 rims.1
  205.7 0.0 all-to-all-done.5
  205.7 0.7 fusion.5
  206.3 0.6 reshape.44
  (11 shorter events, 0.0 us)
Async XLA Ops:
  0.6 78.4 %copy-start = (bf16[512,2048]{1,0:T(8,128)(2,1)S(1)}, bf16[512,2048]{1,0:T(8,128)(2,1)}, u32[]{:S(2)}) copy-start(bf16[512,2048]{1,0:T(8,128)(2,1)} %param.16) | copy-start | bytes 6291460
  3.4 8.8 %collective-permute-start = (bf16[2,640]{1,0:T(2,128)(2,1)S(1)}, bf16[2,640]{1,0:T(2,128)(2,1)S(1)}, u32[]{:S(2)}, u32[]{:S(2)}) collective-permute-start(bf16[2,640]{1,0:T(2,128)(2,1)S(1)} %pad_maximum_fusion), channel_id=1, source_target_pairs={{0,4},{4,8},{8,12},{12,16},{16,20},{20,24},{24,28},{28,32},{32,36}... | collective-permute-start | bytes 7688 | tf_op jit(solution)/shard_map/ppermute | solution.py:333
  12.1 0.6 copy-start.7
  12.7 22.8 %copy-start.2 = (bf16[128,2048]{1,0:T(8,128)(2,1)S(1)}, bf16[128,2048]{1,0:T(8,128)(2,1)}, u32[]{:S(2)}) copy-start(bf16[128,2048]{1,0:T(8,128)(2,1)} %param.17) | copy-start | bytes 1572868
  17.8 43.1 %all-to-all-start = ((f32[128,1,640]{2,1,0:T(1,128)}), f32[128,1,640]{2,1,0:T(1,128)S(1)}, u32[]{:S(2)}, u32[]{:S(2)}) async-start(f32[128,1,640]{2,1,0:T(1,128)} %bitcast.26), calls=%async_computation | async-start | bytes 655360 | tf_op jit(solution)/shard_map/all_to_all | solution.py:338
  35.6 38.8 %collective-permute-start.1 = (bf16[128,2048]{1,0:T(8,128)(2,1)S(1)}, bf16[128,2048]{1,0:T(8,128)(2,1)}, u32[]{:S(2)}, u32[]{:S(2)}) collective-permute-start(bf16[128,2048]{1,0:T(8,128)(2,1)S(1)} %copy-done.2), channel_id=1, source_target_pairs={{0,1},{1,2},{2,3},{3,0},{4,5},{5,6},{6,7},{7,4},{8,9},{9,10},{10,1... | collective-permute-start | bytes 1572872 | tf_op jit(solution)/shard_map/ppermute | solution.py:350
  38.8 39.4 %collective-permute-start.3 = (bf16[128,2048]{1,0:T(8,128)(2,1)S(1)}, bf16[128,2048]{1,0:T(8,128)(2,1)S(1)}, u32[]{:S(2)}, u32[]{:S(2)}) collective-permute-start(bf16[128,2048]{1,0:T(8,128)(2,1)S(1)} %copy-done.2), channel_id=1, source_target_pairs={{0,3},{1,0},{2,1},{3,2},{4,7},{5,4},{6,5},{7,6},{8,11},{9,8},{10,9... | collective-permute-start | bytes 1572872 | tf_op jit(solution)/shard_map/ppermute | solution.py:350
  42.1 34.1 %collective-permute-start.2 = (bf16[128,2048]{1,0:T(8,128)(2,1)S(1)}, bf16[128,2048]{1,0:T(8,128)(2,1)}, u32[]{:S(2)}, u32[]{:S(2)}) collective-permute-start(bf16[128,2048]{1,0:T(8,128)(2,1)S(1)} %copy-done.2), channel_id=1, source_target_pairs={{0,2},{1,3},{2,0},{3,1},{4,6},{5,7},{6,4},{7,5},{8,10},{9,11},{10,... | collective-permute-start | bytes 1572872 | tf_op jit(solution)/shard_map/ppermute | solution.py:350
  62.3 32.5 %all-to-all-start.1 = ((f32[128,1,640]{2,1,0:T(1,128)}), f32[128,1,640]{2,1,0:T(1,128)S(1)}, u32[]{:S(2)}, u32[]{:S(2)}) async-start(f32[128,1,640]{2,1,0:T(1,128)} %copy.34), calls=%async_computation.1 | async-start | bytes 655360 | tf_op jit(solution)/shard_map/all_to_all | solution.py:345
  94.8 0.7 copy-start.5
  101.0 32.5 %all-to-all-start.2 = ((f32[128,1,640]{2,1,0:T(1,128)}), f32[128,1,640]{2,1,0:T(1,128)S(1)}, u32[]{:S(2)}, u32[]{:S(2)}) async-start(f32[128,1,640]{2,1,0:T(1,128)} %bitcast.30), calls=%async_computation.2 | async-start | bytes 655360 | tf_op jit(solution)/shard_map/all_to_all | solution.py:338
  118.9 23.1 %copy-start.3 = (bf16[512,512]{1,0:T(8,128)(2,1)S(1)}, bf16[512,512]{1,0:T(8,128)(2,1)}, u32[]{:S(2)}) copy-start(bf16[512,512]{1,0:T(8,128)(2,1)} %get-tuple-element.39) | copy-start | bytes 1572868
  134.9 32.5 %all-to-all-start.3 = ((f32[128,1,640]{2,1,0:T(1,128)}), f32[128,1,640]{2,1,0:T(1,128)S(1)}, u32[]{:S(2)}, u32[]{:S(2)}) async-start(f32[128,1,640]{2,1,0:T(1,128)} %copy.36), calls=%async_computation.3 | async-start | bytes 655360 | tf_op jit(solution)/shard_map/all_to_all | solution.py:345
  143.2 3.0 %copy-start.1 = (f32[512,2048]{1,0:T(8,128)}, f32[512,2048]{1,0:T(8,128)S(1)}, u32[]{:S(2)}) copy-start(f32[512,2048]{1,0:T(8,128)S(1)} %fusion.7) | copy-start | bytes 12582916
  146.2 54.4 %collective-permute-start.4 = (f32[128,2048]{1,0:T(8,128)}, f32[128,2048]{1,0:T(8,128)S(1)}, u32[]{:S(2)}, u32[]{:S(2)}) collective-permute-start(f32[128,2048]{1,0:T(8,128)} %get-tuple-element.59), channel_id=1, source_target_pairs={{0,1},{1,2},{2,3},{3,0},{4,5},{5,6},{6,7},{7,4},{8,9},{9,10},{10,1... | collective-permute-start | bytes 3145736 | tf_op jit(solution)/shard_map/ppermute | solution.py:350
  149.4 51.2 %collective-permute-start.6 = (f32[128,2048]{1,0:T(8,128)}, f32[128,2048]{1,0:T(8,128)}, u32[]{:S(2)}, u32[]{:S(2)}) collective-permute-start(f32[128,2048]{1,0:T(8,128)} %get-tuple-element.60), channel_id=1, source_target_pairs={{0,3},{1,0},{2,1},{3,2},{4,7},{5,4},{6,5},{7,6},{8,11},{9,8},{10,9... | collective-permute-start | bytes 3145736 | tf_op jit(solution)/shard_map/ppermute | solution.py:350
  152.8 47.8 %collective-permute-start.5 = (f32[128,2048]{1,0:T(8,128)}, f32[128,2048]{1,0:T(8,128)}, u32[]{:S(2)}, u32[]{:S(2)}) collective-permute-start(f32[128,2048]{1,0:T(8,128)} %get-tuple-element.61), channel_id=1, source_target_pairs={{0,2},{1,3},{2,0},{3,1},{4,6},{5,7},{6,4},{7,5},{8,10},{9,11},{10,... | collective-permute-start | bytes 3145736 | tf_op jit(solution)/shard_map/ppermute | solution.py:350
  167.4 0.7 copy-start.4
  177.2 15.6 %all-to-all-start.4 = ((f32[16,16,128]{2,1,0:T(8,128)}), f32[16,16,128]{2,1,0:T(8,128)S(1)}, u32[]{:S(2)}, u32[]{:S(2)}) async-start(f32[16,16,128]{2,1,0:T(8,128)} %broadcast_in_dim.7), calls=%async_computation.4 | async-start | bytes 262144 | tf_op jit(solution)/shard_map/all_to_all | solution.py:376
  180.8 22.7 %collective-permute-start.7 = (f32[2,640]{1,0:T(2,128)}, f32[2,640]{1,0:T(2,128)S(1)}, u32[]{:S(2)}, u32[]{:S(2)}) collective-permute-start(f32[2,640]{1,0:T(2,128)} %get-tuple-element.51), channel_id=1, source_target_pairs={{4,0},{8,4},{12,8},{16,12},{20,16},{24,20},{28,24},{32,28},{36,32}... | collective-permute-start | bytes 15368 | tf_op jit(solution)/shard_map/ppermute | solution.py:333
  193.5 12.2 %all-to-all-start.5 = ((f32[8,16,128]{2,1,0:T(8,128)}), f32[8,16,128]{2,1,0:T(8,128)S(1)}, u32[]{:S(2)}, u32[]{:S(2)}) async-start(f32[8,16,128]{2,1,0:T(8,128)} %broadcast_in_dim.8), calls=%async_computation.5 | async-start | bytes 131072 | tf_op jit(solution)/shard_map/all_to_all | solution.py:376
  203.5 0.6 copy-start.6

commit v3 on v2

--- a/solution.py
+++ b/solution.py
@@ -104,7 +104,7 @@
 
 def extend(scratch, rows, rim):
     length = rows.shape[0]
-    scratch[0:8, :] = jnp.concatenate([jnp.zeros((6, rows.shape[1]), F32), rim], axis=0)
+    scratch[0:8, :] = rim
     scratch[8 : length + 8, :] = rows.astype(F32)
 
 
@@ -114,38 +114,74 @@
     return total + taps[2:3, :] * scratch[6 : length + 6, :]
 
 
+def rim_rows(q_in, k_in, v_in, out):
+    pair = jnp.concatenate([q_in[...].astype(F32), k_in[...].astype(F32)], axis=0).T
+    out[:, :VD] = pair[-16:, :].astype(BF16)
+    out[:, VD:] = v_in[...]
+
+
+def split_query(x, target):
+    high = x.astype(BF16).astype(F32)
+    rest = x - high
+    mid = rest.astype(BF16).astype(F32)
+    target[:, :128] = jnp.concatenate([high, mid], axis=1).astype(BF16)
+    target[:, 128:] = jnp.concatenate([rest - mid, high], axis=1).astype(BF16)
+    return high, mid
+
+
+def split_key(x, target, similar_target):
+    high, mid = split_query(x, target)
+    similar_target[:, :128] = jnp.concatenate([high, high], axis=1).astype(BF16)
+    similar_target[:, 128:] = jnp.concatenate([high, mid], axis=1).astype(BF16)
+
+
 def first_kernel(
-    q_in, k_in, v_in, rim_qk, rim_v, taps_q, taps_k, taps_v, places, factors,
+    q_in, k_in, v_in, taps_q, taps_k, taps_v, places, factors,
     q4, k4, k5, vb, state, narrow, broad,
 ):
     head = pl.program_id(0)
     length = q_in.shape[1]
+    none = jnp.zeros((8, 1), F32)
 
     @pl.when(head == 0)
     def _():
-        rim = rim_qk[...].astype(F32)
-        for source, taps, edge, target in (
-            (q_in, taps_q, rim[:, :64], q4),
-            (k_in, taps_k, rim[:, 64:], k4),
-        ):
-            extend(narrow, source[...].astype(F32).T, edge)
-            x = convolve(narrow, taps[...], length)
-            high = x.astype(BF16).astype(F32)
-            rest = x - high
-            mid = rest.astype(BF16).astype(F32)
-            low = rest - mid
-            target[:, :128] = jnp.concatenate([high, mid], axis=1).astype(BF16)
-            target[:, 128:] = jnp.concatenate([low, high], axis=1).astype(BF16)
-            if target is k4:
-                k5[:, :128] = jnp.concatenate([high, high], axis=1).astype(BF16)
-                k5[:, 128:] = jnp.concatenate([high, mid], axis=1).astype(BF16)
-
-    extend(broad, v_in[...], rim_v[...].astype(F32))
+        extend(narrow, q_in[...].astype(F32).T, jnp.broadcast_to(none, (8, 64)))
+        split_query(convolve(narrow, taps_q[...], length), q4)
+        extend(narrow, k_in[...].astype(F32).T, jnp.broadcast_to(none, (8, 64)))
+        split_key(convolve(narrow, taps_k[...], length), k4, k5)
+
+    extend(broad, v_in[...], jnp.broadcast_to(none, (8, VD)))
     value = jnp.concatenate(halves(convolve(broad, taps_v[...], length)), axis=1)
     vb[...] = value
     first, second = expand(k4[...], selectors(places[...], head), factors[...])
-    phi = (first * second).astype(BF16)
+    known = lax.broadcasted_iota(jnp.int32, (length, WIDE), 0) >= 2
+    phi = jnp.where(known, first * second, 0.0).astype(BF16)
     state[...] = pack(
+        fold(mm(phi, value, 0, 0)), jnp.sum(phi.astype(F32), axis=0, keepdims=True)
+    )
+
+
+def mend_kernel(
+    q_in, k_in, v_in, rim_qk, rim_v, taps_q, taps_k, taps_v, places, factors,
+    q4_in, k4_in, k5_in, vb_in, state_in, q4, k4, k5, vb, state, narrow, broad,
+):
+    head = pl.program_id(0)
+
+    @pl.when(head == 0)
+    def _():
+        rim = rim_qk[8:, :].astype(F32)
+        extend(narrow, q_in[...].astype(F32).T[:16, :], rim[:, :64])
+        split_query(convolve(narrow, taps_q[...], 16), q4)
+        extend(narrow, k_in[...].astype(F32).T[:16, :], rim[:, 64:])
+        split_key(convolve(narrow, taps_k[...], 16), k4, k5)
+
+    extend(broad, v_in[...], rim_v[8:, :].astype(F32))
+    value = jnp.concatenate(halves(convolve(broad, taps_v[...], 16)), axis=1)
+    vb[...] = value
+    first, second = expand(k4[...], selectors(places[...], head), factors[...])
+    missing = lax.broadcasted_iota(jnp.int32, (16, WIDE), 0) < 2
+    phi = jnp.where(missing, first * second, 0.0).astype(BF16)
+    state[...] = state_in[...] + pack(
         fold(mm(phi, value, 0, 0)), jnp.sum(phi.astype(F32), axis=0, keepdims=True)
     )
 
@@ -283,7 +319,7 @@
 
     value_grad = gv_in[...] + mm((first * second).astype(BF16), later_high, 1, 0)
     grad_v[...] = conv_back(broad, value_grad, taps_v[...], length)
-    extend(broad, v_in[...], rim_v[...].astype(F32))
+    extend(broad, v_in[...], rim_v[8:, :].astype(F32))
     sums = tap_sums(broad, value_grad, length)
     heads = heads_first.shape[1] // VD - 1
     for index in range(heads):
@@ -295,7 +331,7 @@
 
     @pl.when(head == pl.num_programs(0) - 1)
     def _():
-        rim = rim_qk[...].astype(F32)
+        rim = rim_qk[8:, :].astype(F32)
         found = []
         for source, taps, edge, grad, target in (
             (q_in, taps_q, rim[:, :64], gq[...], grad_q),
@@ -376,6 +412,11 @@
     return lax.all_to_all(copies, axis, 0, 0, tiled=True)
 
 
+def total_over(block, axis):
+    everyone = to_all(block, axis).reshape((lax.axis_size(axis),) + block.shape)
+    return jnp.sum(everyone, axis=0)
+
+
 def body(query_in, key_in, value_in, conv_query, conv_key, conv_value, out_proj, out_grad):
     length, keys = query_in.shape
     heads = conv_value.shape[1] // VD
@@ -412,27 +453,50 @@
         )
 
     values = heads * VD
-    rim = from_behind(
-        jnp.concatenate([x[length - 2 :] for x in (query_in, key_in, value_in)], axis=1), SEQ, 1
-    )
     query_cols, key_cols = query_in.T, key_in.T
     upright = whole(keys, length)
-    conv_ins = [
-        upright, upright, per_head(length), whole(2, 2 * keys),
-        pl.BlockSpec((2, VD), lambda h: (0, h + 1)),
-        whole(3, keys), whole(3, keys), per_head(3), table, table,
+    final = [
+        pl.BlockSpec((keys, VD), lambda i: (0, length // VD - 1)),
+        pl.BlockSpec((keys, VD), lambda i: (0, length // VD - 1)),
+        pl.BlockSpec((16, values), lambda i: (length // 16 - 1, 0)),
     ]
-    conv_args = (
-        query_cols, key_cols, value_in, rim, rim,
-        conv_query, conv_key, conv_value, places, factors,
-    )
+    rim = pl.pallas_call(
+        rim_rows,
+        name="edge",
+        grid=(1,),
+        in_specs=final,
+        out_specs=whole(16, 2 * keys + values),
+        out_shape=arr(16, 2 * keys + values, BF16),
+    )(query_cols, key_cols, value_in)
+    rim = from_behind(rim, SEQ, 1)
+    weights = [whole(3, keys), whole(3, keys), per_head(3), table, table]
+    weight_args = (conv_query, conv_key, conv_value, places, factors)
+    inputs = (query_cols, key_cols, value_in)
+    input_specs = [upright, upright, per_head(length)]
+    rim_specs = [whole(16, 2 * keys), pl.BlockSpec((16, VD), lambda h: (0, h + 1))]
+    conv_ins = input_specs + rim_specs + weights
+    conv_args = inputs + (rim, rim) + weight_args
     buffers = [pltpu.VMEM((length + 8, keys), F32), pltpu.VMEM((length + 8, VD), F32)]
-    q4, k4, k5, vb, local_state = call(
-        first_kernel, "first", conv_ins,
-        [pieces, pieces, pieces, pairs, packs],
-        [arr(length, WIDE, BF16)] * 3 + [arr(length, 2 * values, BF16), arr(heads * ROWS, VD)],
-        2 << 30, buffers,
-    )(*conv_args)
+    pairs_of = [pieces, pieces, pieces, pairs, packs]
+    shapes_of = [arr(length, WIDE, BF16)] * 3 + [
+        arr(length, 2 * values, BF16), arr(heads * ROWS, VD),
+    ]
+    begun = call(
+        first_kernel, "first", input_specs + weights, pairs_of, shapes_of, 2 << 30, buffers
+    )(*inputs, *weight_args)
+    top = whole(16, WIDE)
+    corner = whole(keys, VD)
+    untouched = pl.BlockSpec(memory_space=pl.ANY)
+    q4, k4, k5, vb, local_state = pl.pallas_call(
+        mend_kernel,
+        name="mend",
+        grid=(heads,),
+        in_specs=[corner, corner, per_head(16)] + rim_specs + weights + [untouched] * 4 + [packs],
+        out_specs=[top, top, top, pl.BlockSpec((16, 2 * VD), lambda h: (0, h)), packs],
+        out_shape=shapes_of,
+        scratch_shapes=[pltpu.VMEM((24, keys), F32), pltpu.VMEM((24, VD), F32)],
+        input_output_aliases={10: 0, 11: 1, 12: 2, 13: 3, 14: 4},
+    )(*conv_args, *begun)
     cotangent = gathered(out_grad, "head")
     upstream = lax.dot_general(
         cotangent, out_proj, (((1,), (1,)), ((), ())), preferred_element_type=F32
@@ -469,9 +533,7 @@
         4 << 30, buffers + [pltpu.VMEM((length, keys), F32)],
     )(*conv_args, k4, vb, after, gq, kd, gv)
     tail = from_behind(first_rows, SEQ, -1)
-    for axis in ("z", ("x", "core")):
-        everyone = to_all(taps, axis).reshape((lax.axis_size(axis),) + taps.shape)
-        taps = jnp.sum(everyone, axis=0)
+    taps = total_over(taps, "z")
     rims = [
         pl.BlockSpec((keys, VD), lambda i: (0, length // VD - 1)),
         pl.BlockSpec((keys, VD), lambda i: (0, length // VD - 1)),
@@ -487,6 +549,10 @@
         out_shape=[arr(keys, length)] * 2 + [arr(length, values)],
         input_output_aliases={4: 0, 5: 1, 6: 2},
     )(tail, conv_query, conv_key, conv_value, grad_query, grad_key, grad_value)
+    taps, mixed, grad_query, grad_key, grad_value = lax.optimization_barrier(
+        (taps, mixed, grad_query, grad_key, grad_value)
+    )
+    taps = total_over(taps, ("x", "core"))
     value_taps = taps[: 3 * heads].reshape(heads, 3, VD).transpose(1, 0, 2).reshape(3, values)
     other_taps = taps[3 * heads : 3 * heads + 3]
     return (

time: 208 us -> 216 us (1.038)
  blocking collectives: 0 us -> 11.4 us
  starting transfers between devices: 78.2 us -> 71.5 us
  Pallas kernels: 35.8 us -> 41.4 us
  local copies, waits for them, and re-layouts: 20.7 us -> 17.5 us
    ppermute x6, waiting for transfers between devices: 0.02 us -> 12.6 us  [turned(): lax.ppermute(block, axis, [(i, (i + distance) % size) for i in range(size)])]
    all_to_all x0 -> x1, blocking collectives: none -> 11.4 us  [to_all(): return lax.all_to_all(copies, axis, 0, 0, tiled=True)]
    all_to_all x2 -> x1, waiting for transfers between devices: 8.33 us -> 0.01 us  [to_all(): return lax.all_to_all(copies, axis, 0, 0, tiled=True)]
    all_to_all x2 -> x1, starting transfers between devices: 10.7 us -> 3.51 us  [to_all(): return lax.all_to_all(copies, axis, 0, 0, tiled=True)]
    pallas_call x1 -> x3, Pallas kernels: 5.09 us -> 10.7 us  [the longest x1 4.99 us: body(): call(first_kernel, 'first', input_specs + weights, pairs_of, shapes_of, 2...]
    ppermute x2, waiting for transfers between devices: 3.84 us -> 0.01 us  [from_behind(): return lax.ppermute(block, axis, route)]
    slice x3 -> x0, local copies, waits for them, and re-layouts: 2.45 us -> none  [body(): x[length - 2:]]
  transfers between devices with their start and end apart: 14 -> 13, of which waited for: 6 -> 5; matrix products, arithmetic and copies ran while one was open for 10% -> 9% of each run, Pallas kernels for 12% -> 14%
where the time goes in v3:
time: 216 us; the launch traced here: 214 us
  starting transfers between devices  71.5 us (33%)
  waiting for transfers between devices  62.9 us (29%)
  Pallas kernels  41.4 us (19%)
  local copies, waits for them, and re-layouts  17.5 us (8%)
  blocking collectives  11.4 us (5%)
  matrix products  5.77 us (3%)
  other arithmetic  2.93 us (1%)
    all_to_all x2, waiting for transfers between devices, carried_in(): everyone = lax.all_to_all(packed.reshape(ranks, -1), SEQ, 0, 0, tiled=True)  27.3 us
    all_to_all x2, starting transfers between devices, carried_in(): everyone = lax.all_to_all(packed.reshape(ranks, -1), SEQ, 0, 0, tiled=True)  25.1 us
    all_to_all x2, waiting for transfers between devices, carried_in(): lax.all_to_all(sums, SEQ, 0, 0, tiled=True).reshape(packed.shape)  23 us
    ppermute x6, starting transfers between devices, turned(): lax.ppermute(block, axis, [(i, (i + distance) % size) for i in range(size)])  20.2 us
    all_to_all x2, starting transfers between devices, carried_in(): lax.all_to_all(sums, SEQ, 0, 0, tiled=True).reshape(packed.shape)  14 us
    ppermute x6, waiting for transfers between devices, turned(): lax.ppermute(block, axis, [(i, (i + distance) % size) for i in range(size)])  12.6 us
    all_to_all x1, blocking collectives, to_all(): return lax.all_to_all(copies, axis, 0, 0, tiled=True)  11.4 us
    pallas_call x1, Pallas kernels, body(): call(inner_kernel, 'inner', [pieces] * 3 + [pairs, packs] + [per_head(len...  10.8 us
  transfers between devices with their start and end apart: 13, of which 5 were waited for; matrix products, arithmetic and copies ran while one was open for 9% of the time, Pallas kernels for 14%

profile of v3, /device:TPU:1, one launch (start us, length us, event | category | flops | bytes accessed | tf_op | source)
XLA Modules:
  0.0 214.2 jit_solution(7357172603389721440)
XLA Ops:
  0.6 0.0 copy-start
  0.6 1.6 edge.1
  2.3 4.9 %collective-permute-start = (bf16[16,640]{1,0:T(8,128)(2,1)}, bf16[16,640]{1,0:T(8,128)(2,1)S(1)}, u32[]{:S(2)}, u32[]{:S(2)}) collective-permute-start(bf16[16,640]{1,0:T(8,128)(2,1)} %edge.1), channel_id=1, source_target_pairs={{0,4},{4,8},{8,12},{12,16},{16,20},{20,24},{24,28},{28,32},{32,36}... | collective-permute-start | bytes 61448 | tf_op jit(solution)/shard_map/ppermute | solution.py:369
  7.2 5.0 %first.1 = (bf16[512,256]{1,0:T(8,128)(2,1)}, bf16[512,256]{1,0:T(8,128)(2,1)}, bf16[512,256]{1,0:T(8,128)(2,1)}, bf16[512,1024]{1,0:T(8,128)(2,1)}, f32[640,128]{1,0:T(8,128)}) custom-call(bf16[64,512]{1,0:T(8,128)(2,1)} %bitcast.32, bf16[64,512]{1,0:T(8,128)(2,1)} %bitcast.36, bf16[512,512]{1,0:T(8,128)(2,1)} %v_in.7, f32[3,64]{1,0:T(4,128)} %taps_q.7, ...), custom_call_target="tpu_custom_call" | custom-call | flops 2147483648 | bytes 4194304 | tf_op jit(solution)/shard_map/first/pallas_call | solution.py:484
  12.2 0.0 copy-start.2
  12.2 0.0 collective-permute-done.rim_qk.rim_v
  12.2 0.0 copy-start.6
  12.2 0.6 copy-done.6
  12.8 4.1 %mend.1 = (bf16[512,256]{1,0:T(8,128)(2,1)}, bf16[512,256]{1,0:T(8,128)(2,1)}, bf16[512,256]{1,0:T(8,128)(2,1)}, bf16[512,1024]{1,0:T(8,128)(2,1)}, f32[640,128]{1,0:T(8,128)}) custom-call(bf16[64,512]{1,0:T(8,128)(2,1)} %bitcast.33, bf16[64,512]{1,0:T(8,128)(2,1)} %bitcast.37, ...), custom_call_target="tpu_custom_call", output_to_operand_aliasing={{0}: (10, {}), {1}: (11, {}), {2}: (12, {}), {3}: (13, {}),... | custom-call | tf_op jit(solution)/shard_map/mend/pallas_call | solution.py:490
  16.9 18.1 %all-to-all-start = ((f32[128,1,640]{2,1,0:T(1,128)}), f32[128,1,640]{2,1,0:T(1,128)S(1)}, u32[]{:S(2)}, u32[]{:S(2)}) async-start(f32[128,1,640]{2,1,0:T(1,128)} %bitcast.26), calls=%async_computation | async-start | bytes 655360 | tf_op jit(solution)/shard_map/all_to_all | solution.py:374
  35.0 0.0 copy-done.2
  35.0 3.2 %collective-permute-start.1 = (bf16[128,2048]{1,0:T(8,128)(2,1)S(1)}, bf16[128,2048]{1,0:T(8,128)(2,1)}, u32[]{:S(2)}, u32[]{:S(2)}) collective-permute-start(bf16[128,2048]{1,0:T(8,128)(2,1)S(1)} %copy-done.2), channel_id=1, source_target_pairs={{0,1},{1,2},{2,3},{3,0},{4,5},{5,6},{6,7},{7,4},{8,9},{9,10},{10,1... | collective-permute-start | bytes 1572872 | tf_op jit(solution)/shard_map/ppermute | solution.py:386
  38.2 3.4 %collective-permute-start.3 = (bf16[128,2048]{1,0:T(8,128)(2,1)S(1)}, bf16[128,2048]{1,0:T(8,128)(2,1)S(1)}, u32[]{:S(2)}, u32[]{:S(2)}) collective-permute-start(bf16[128,2048]{1,0:T(8,128)(2,1)S(1)} %copy-done.2), channel_id=1, source_target_pairs={{0,3},{1,0},{2,1},{3,2},{4,7},{5,4},{6,5},{7,6},{8,11},{9,8},{10,9... | collective-permute-start | bytes 1572872 | tf_op jit(solution)/shard_map/ppermute | solution.py:386
  41.6 3.5 %collective-permute-start.2 = (bf16[128,2048]{1,0:T(8,128)(2,1)S(1)}, bf16[128,2048]{1,0:T(8,128)(2,1)}, u32[]{:S(2)}, u32[]{:S(2)}) collective-permute-start(bf16[128,2048]{1,0:T(8,128)(2,1)S(1)} %copy-done.2), channel_id=1, source_target_pairs={{0,2},{1,3},{2,0},{3,1},{4,6},{5,7},{6,4},{7,5},{8,10},{9,11},{10,... | collective-permute-start | bytes 1572872 | tf_op jit(solution)/shard_map/ppermute | solution.py:386
  45.2 1.6 broadcast_in_dim.6
  46.8 0.8 constant_dynamic-update-slice_fusion.3
  47.7 12.7 %all-to-all-done = f32[128,1,640]{2,1,0:T(1,128)S(1)} async-done(((f32[128,1,640]{2,1,0:T(1,128)}), f32[128,1,640]{2,1,0:T(1,128)S(1)}, u32[]{:S(2)}, u32[]{:S(2)}) %all-to-all-start) | async-done | bytes 327712 | tf_op jit(solution)/shard_map/all_to_all | solution.py:374
  60.4 0.3 convolution_bitcast_fusion
  60.7 1.1 copy.31
  61.8 7.0 %all-to-all-start.1 = ((f32[128,1,640]{2,1,0:T(1,128)}), f32[128,1,640]{2,1,0:T(1,128)S(1)}, u32[]{:S(2)}, u32[]{:S(2)}) async-start(f32[128,1,640]{2,1,0:T(1,128)} %copy.31), calls=%async_computation.1 | async-start | bytes 655360 | tf_op jit(solution)/shard_map/all_to_all | solution.py:381
  68.8 5.0 %local.1 = (f32[512,512]{1,0:T(8,128)}, f32[512,512]{1,0:T(8,128)}) custom-call(bf16[512,256]{1,0:T(8,128)(2,1)} %get-tuple-element.50.q4, bf16[512,256]{1,0:T(8,128)(2,1)} %get-tuple-element.52.k5, bf16[512,1024]{1,0:T(8,128)(2,1)} %get-tuple-element.49.vb), custom_call_target="tpu_custom_call" | custom-call | flops 4294967296 | bytes 4194304 | tf_op jit(solution)/shard_map/local/pallas_call | solution.py:504
  73.8 0.0 collective-permute-done.1
  73.8 1.9 constant_dynamic-update-slice_fusion.2
  75.7 0.0 collective-permute-done.2
  75.7 1.9 constant_dynamic-update-slice_fusion.1
  77.6 0.0 collective-permute-done.3
  77.6 0.8 constant_dynamic-update-slice_fusion
  78.5 0.0 copy-done
  78.5 3.9 %fusion.6.up = f32[512,512]{1,0:T(8,128)} fusion(bf16[512,2048]{1,0:T(8,128)(2,1)} %constant_dynamic-update-slice_fusion, bf16[512,2048]{1,0:T(8,128)(2,1)S(1)} %copy-done), kind=kOutput, calls=%fused_computation.17 | convolution fusion | flops 1073741824 | bytes 5242880 | tf_op jit(solution)/shard_map/dot_general | solution.py:501
  82.3 11.9 %all-to-all-done.1 = f32[128,1,640]{2,1,0:T(1,128)S(1)} async-done(((f32[128,1,640]{2,1,0:T(1,128)}), f32[128,1,640]{2,1,0:T(1,128)S(1)}, u32[]{:S(2)}, u32[]{:S(2)}) %all-to-all-start.1) | async-done | bytes 327712 | tf_op jit(solution)/shard_map/all_to_all | solution.py:381
  94.2 0.0 copy-start.4
  94.2 0.7 copy-done.4
  95.0 5.5 %middle.1 = (bf16[512,512]{1,0:T(8,128)(2,1)}, f32[512,512]{1,0:T(8,128)}, f32[512,512]{1,0:T(8,128)}, f32[640,128]{1,0:T(8,128)}) custom-call(bf16[512,256]{1,0:T(8,128)(2,1)} %get-tuple-element.50.q4, f32[640,128]{1,0:T(8,128)} %bitcast.27, f32[512,512]{1,0:T(8,128)} %get-tuple-element.53.numer, f32[512,512]{1,0:T(8,128)} %get-tuple-element.54.denom, ...), custom_call_target="tpu_custom_call" | custom-call | flops 4294967296 | bytes 4194304 | tf_op jit(solution)/shard_map/middle/pallas_call | solution.py:509
  100.5 7.0 %all-to-all-start.2 = ((f32[128,1,640]{2,1,0:T(1,128)}), f32[128,1,640]{2,1,0:T(1,128)S(1)}, u32[]{:S(2)}, u32[]{:S(2)}) async-start(f32[128,1,640]{2,1,0:T(1,128)} %bitcast.29), calls=%async_computation.2 | async-start | bytes 655360 | tf_op jit(solution)/shard_map/all_to_all | solution.py:374
  107.5 10.8 %inner.1 = (f32[512,64]{1,0:T(8,128)}, f32[512,64]{1,0:T(8,128)}, f32[512,512]{1,0:T(8,128)}) custom-call(bf16[512,256]{1,0:T(8,128)(2,1)} %get-tuple-element.50.q4, bf16[512,256]{1,0:T(8,128)(2,1)} %get-tuple-element.48.k4, bf16[512,256]{1,0:T(8,128)(2,1)} %get-tuple-element.52.k5, bf16[512,1024]{1,0:T(8,128)(2,1)} %get-tuple-element.49.vb, ...), custom_call_target="tpu_custom_call" | custom-call | flops 8589934592 | bytes 4194304 | tf_op jit(solution)/shard_map/inner/pallas_call | solution.py:517
  118.4 14.6 %all-to-all-done.2 = f32[128,1,640]{2,1,0:T(1,128)S(1)} async-done(((f32[128,1,640]{2,1,0:T(1,128)}), f32[128,1,640]{2,1,0:T(1,128)S(1)}, u32[]{:S(2)}, u32[]{:S(2)}) %all-to-all-start.2) | async-done | bytes 327712 | tf_op jit(solution)/shard_map/all_to_all | solution.py:374
  133.0 0.3 fusion
  133.3 1.1 copy.33
  134.4 7.0 %all-to-all-start.3 = ((f32[128,1,640]{2,1,0:T(1,128)}), f32[128,1,640]{2,1,0:T(1,128)S(1)}, u32[]{:S(2)}, u32[]{:S(2)}) async-start(f32[128,1,640]{2,1,0:T(1,128)} %copy.33), calls=%async_computation.3 | async-start | bytes 655360 | tf_op jit(solution)/shard_map/all_to_all | solution.py:381
  141.4 0.0 copy-done.3
  141.4 1.3 fusion.7
  142.6 0.0 copy-start.1
  142.6 1.9 constant_dynamic-slice_fusion.2
  144.5 1.1 copy-done.1
  145.7 3.2 %collective-permute-start.4 = (f32[128,2048]{1,0:T(8,128)}, f32[128,2048]{1,0:T(8,128)S(1)}, u32[]{:S(2)}, u32[]{:S(2)}) collective-permute-start(f32[128,2048]{1,0:T(8,128)} %get-tuple-element.79), channel_id=1, source_target_pairs={{0,1},{1,2},{2,3},{3,0},{4,5},{5,6},{6,7},{7,4},{8,9},{9,10},{10,1... | collective-permute-start | bytes 3145736 | tf_op jit(solution)/shard_map/ppermute | solution.py:386
  148.9 3.4 %collective-permute-start.6 = (f32[128,2048]{1,0:T(8,128)}, f32[128,2048]{1,0:T(8,128)}, u32[]{:S(2)}, u32[]{:S(2)}) collective-permute-start(f32[128,2048]{1,0:T(8,128)} %get-tuple-element.80), channel_id=1, source_target_pairs={{0,3},{1,0},{2,1},{3,2},{4,7},{5,4},{6,5},{7,6},{8,11},{9,8},{10,9... | collective-permute-start | bytes 3145736 | tf_op jit(solution)/shard_map/ppermute | solution.py:386
  152.2 3.5 %collective-permute-start.5 = (f32[128,2048]{1,0:T(8,128)}, f32[128,2048]{1,0:T(8,128)}, u32[]{:S(2)}, u32[]{:S(2)}) collective-permute-start(f32[128,2048]{1,0:T(8,128)} %get-tuple-element.81), channel_id=1, source_target_pairs={{0,2},{1,3},{2,0},{3,1},{4,6},{5,7},{6,4},{7,5},{8,10},{9,11},{10,... | collective-permute-start | bytes 3145736 | tf_op jit(solution)/shard_map/ppermute | solution.py:386
  155.8 11.1 %all-to-all-done.3 = f32[128,1,640]{2,1,0:T(1,128)S(1)} async-done(((f32[128,1,640]{2,1,0:T(1,128)}), f32[128,1,640]{2,1,0:T(1,128)S(1)}, u32[]{:S(2)}, u32[]{:S(2)}) %all-to-all-start.3) | async-done | bytes 327712 | tf_op jit(solution)/shard_map/all_to_all | solution.py:381
  166.8 0.7 copy-done.5
  167.6 7.7 %last.1 = (f32[64,512]{1,0:T(8,128)}, f32[64,512]{1,0:T(8,128)}, f32[512,512]{1,0:T(8,128)}, f32[16,128]{1,0:T(8,128)}, f32[2,640]{1,0:T(2,128)}) custom-call(bf16[64,512]{1,0:T(8,128)(2,1)} %bitcast.34, bf16[64,512]{1,0:T(8,128)(2,1)} %bitcast.38, bf16[512,512]{1,0:T(8,128)(2,1)} %v_in.7, bf16[16,640]{1,0:T(8,128)(2,1)} %copy-done.6, ...), custom_call_target="tpu_custom_call" | custom-call | flops 4294967296 | bytes 4194304 | tf_op jit(solution)/shard_map/last/pallas_call | solution.py:527
  175.3 3.7 %collective-permute-start.7 = (f32[2,640]{1,0:T(2,128)}, f32[2,640]{1,0:T(2,128)S(1)}, u32[]{:S(2)}, u32[]{:S(2)}) collective-permute-start(f32[2,640]{1,0:T(2,128)} %get-tuple-element.67), channel_id=1, source_target_pairs={{4,0},{8,4},{12,8},{16,12},{20,16},{24,20},{28,24},{32,28},{36,32}... | collective-permute-start | bytes 15368 | tf_op jit(solution)/shard_map/ppermute | solution.py:369
  179.0 1.4 broadcast_in_dim.7
  180.4 3.5 %all-to-all-start.4 = ((f32[16,16,128]{2,1,0:T(8,128)}), f32[16,16,128]{2,1,0:T(8,128)S(1)}, u32[]{:S(2)}, u32[]{:S(2)}) async-start(f32[16,16,128]{2,1,0:T(8,128)} %broadcast_in_dim.7), calls=%async_computation.4 | async-start | bytes 262144 | tf_op jit(solution)/shard_map/all_to_all | solution.py:412
  183.9 0.0 collective-permute-done.4
  183.9 0.0 collective-permute-done.6
  184.0 12.5 %collective-permute-done.5 = f32[128,2048]{1,0:T(8,128)} collective-permute-done((f32[128,2048]{1,0:T(8,128)}, f32[128,2048]{1,0:T(8,128)}, u32[]{:S(2)}, u32[]{:S(2)}) %collective-permute-start.5) | collective-permute-done | bytes 1048608 | tf_op jit(solution)/shard_map/ppermute | solution.py:386
  196.5 2.9 %add_convert_fusion = bf16[128,2048]{1,0:T(8,128)(2,1)} fusion(f32[128,2048]{1,0:T(8,128)} %collective-permute-done.6, f32[128,2048]{1,0:T(8,128)} %collective-permute-done.5, f32[128,2048]{1,0:T(8,128)S(1)} %collective-permute-done.4, f32[512,2048]{1,0:T(8,128)} %copy-done.1, s32[]{:T(128)S(6)} %select_n.63), kind=kLoop, calls=%fused_computation.1 | loop fusion | flops 1048576 | bytes 4718596 | tf_op jit(solution)/shard_map/convert_element_type | solution.py:526
  199.4 0.0 collective-permute-done.7.tail
  199.4 0.6 copy-done.7
  200.0 1.6 rims.1
  201.6 0.0 all-to-all-done.4
  201.6 11.4 %all_to_all.52 = f32[8,16,128]{2,1,0:T(8,128)S(1)} all-to-all(f32[8,16,128]{2,1,0:T(8,128)S(1)} %broadcast_in_dim.8), channel_id=1, replica_groups=mesh['x'=4,'z'=16,'core'=2,'head'=4] {'x','core'}, dimensions={0} | all-to-all | bytes 131072 | tf_op jit(solution)/shard_map/all_to_all | solution.py:412
  213.0 0.7 fusion.5
  213.6 0.6 reshape.44
  (6 shorter events, 0.0 us)
Async XLA Ops:
  0.6 77.8 %copy-start = (bf16[512,2048]{1,0:T(8,128)(2,1)S(1)}, bf16[512,2048]{1,0:T(8,128)(2,1)}, u32[]{:S(2)}) copy-start(bf16[512,2048]{1,0:T(8,128)(2,1)} %param.16) | copy-start | bytes 6291460
  2.3 9.9 %collective-permute-start = (bf16[16,640]{1,0:T(8,128)(2,1)}, bf16[16,640]{1,0:T(8,128)(2,1)S(1)}, u32[]{:S(2)}, u32[]{:S(2)}) collective-permute-start(bf16[16,640]{1,0:T(8,128)(2,1)} %edge.1), channel_id=1, source_target_pairs={{0,4},{4,8},{8,12},{12,16},{16,20},{20,24},{24,28},{28,32},{32,36}... | collective-permute-start | bytes 61448 | tf_op jit(solution)/shard_map/ppermute | solution.py:369
  12.2 22.8 %copy-start.2 = (bf16[128,2048]{1,0:T(8,128)(2,1)S(1)}, bf16[128,2048]{1,0:T(8,128)(2,1)}, u32[]{:S(2)}) copy-start(bf16[128,2048]{1,0:T(8,128)(2,1)} %param.17) | copy-start | bytes 1572868
  12.2 0.6 copy-start.6
  16.9 43.5 %all-to-all-start = ((f32[128,1,640]{2,1,0:T(1,128)}), f32[128,1,640]{2,1,0:T(1,128)S(1)}, u32[]{:S(2)}, u32[]{:S(2)}) async-start(f32[128,1,640]{2,1,0:T(1,128)} %bitcast.26), calls=%async_computation | async-start | bytes 655360 | tf_op jit(solution)/shard_map/all_to_all | solution.py:374
  35.0 38.8 %collective-permute-start.1 = (bf16[128,2048]{1,0:T(8,128)(2,1)S(1)}, bf16[128,2048]{1,0:T(8,128)(2,1)}, u32[]{:S(2)}, u32[]{:S(2)}) collective-permute-start(bf16[128,2048]{1,0:T(8,128)(2,1)S(1)} %copy-done.2), channel_id=1, source_target_pairs={{0,1},{1,2},{2,3},{3,0},{4,5},{5,6},{6,7},{7,4},{8,9},{9,10},{10,1... | collective-permute-start | bytes 1572872 | tf_op jit(solution)/shard_map/ppermute | solution.py:386
  38.2 39.4 %collective-permute-start.3 = (bf16[128,2048]{1,0:T(8,128)(2,1)S(1)}, bf16[128,2048]{1,0:T(8,128)(2,1)S(1)}, u32[]{:S(2)}, u32[]{:S(2)}) collective-permute-start(bf16[128,2048]{1,0:T(8,128)(2,1)S(1)} %copy-done.2), channel_id=1, source_target_pairs={{0,3},{1,0},{2,1},{3,2},{4,7},{5,4},{6,5},{7,6},{8,11},{9,8},{10,9... | collective-permute-start | bytes 1572872 | tf_op jit(solution)/shard_map/ppermute | solution.py:386
  41.6 34.1 %collective-permute-start.2 = (bf16[128,2048]{1,0:T(8,128)(2,1)S(1)}, bf16[128,2048]{1,0:T(8,128)(2,1)}, u32[]{:S(2)}, u32[]{:S(2)}) collective-permute-start(bf16[128,2048]{1,0:T(8,128)(2,1)S(1)} %copy-done.2), channel_id=1, source_target_pairs={{0,2},{1,3},{2,0},{3,1},{4,6},{5,7},{6,4},{7,5},{8,10},{9,11},{10,... | collective-permute-start | bytes 1572872 | tf_op jit(solution)/shard_map/ppermute | solution.py:386
  61.8 32.5 %all-to-all-start.1 = ((f32[128,1,640]{2,1,0:T(1,128)}), f32[128,1,640]{2,1,0:T(1,128)S(1)}, u32[]{:S(2)}, u32[]{:S(2)}) async-start(f32[128,1,640]{2,1,0:T(1,128)} %copy.31), calls=%async_computation.1 | async-start | bytes 655360 | tf_op jit(solution)/shard_map/all_to_all | solution.py:381
  94.2 0.7 copy-start.4
  100.5 32.5 %all-to-all-start.2 = ((f32[128,1,640]{2,1,0:T(1,128)}), f32[128,1,640]{2,1,0:T(1,128)S(1)}, u32[]{:S(2)}, u32[]{:S(2)}) async-start(f32[128,1,640]{2,1,0:T(1,128)} %bitcast.29), calls=%async_computation.2 | async-start | bytes 655360 | tf_op jit(solution)/shard_map/all_to_all | solution.py:374
  118.3 23.0 %copy-start.3 = (bf16[512,512]{1,0:T(8,128)(2,1)S(1)}, bf16[512,512]{1,0:T(8,128)(2,1)}, u32[]{:S(2)}) copy-start(bf16[512,512]{1,0:T(8,128)(2,1)} %get-tuple-element.66) | copy-start | bytes 1572868
  134.4 32.5 %all-to-all-start.3 = ((f32[128,1,640]{2,1,0:T(1,128)}), f32[128,1,640]{2,1,0:T(1,128)S(1)}, u32[]{:S(2)}, u32[]{:S(2)}) async-start(f32[128,1,640]{2,1,0:T(1,128)} %copy.33), calls=%async_computation.3 | async-start | bytes 655360 | tf_op jit(solution)/shard_map/all_to_all | solution.py:381
  142.6 3.0 %copy-start.1 = (f32[512,2048]{1,0:T(8,128)}, f32[512,2048]{1,0:T(8,128)S(1)}, u32[]{:S(2)}) copy-start(f32[512,2048]{1,0:T(8,128)S(1)} %fusion.7) | copy-start | bytes 12582916
  145.7 38.3 %collective-permute-start.4 = (f32[128,2048]{1,0:T(8,128)}, f32[128,2048]{1,0:T(8,128)S(1)}, u32[]{:S(2)}, u32[]{:S(2)}) collective-permute-start(f32[128,2048]{1,0:T(8,128)} %get-tuple-element.79), channel_id=1, source_target_pairs={{0,1},{1,2},{2,3},{3,0},{4,5},{5,6},{6,7},{7,4},{8,9},{9,10},{10,1... | collective-permute-start | bytes 3145736 | tf_op jit(solution)/shard_map/ppermute | solution.py:386
  148.9 35.1 %collective-permute-start.6 = (f32[128,2048]{1,0:T(8,128)}, f32[128,2048]{1,0:T(8,128)}, u32[]{:S(2)}, u32[]{:S(2)}) collective-permute-start(f32[128,2048]{1,0:T(8,128)} %get-tuple-element.80), channel_id=1, source_target_pairs={{0,3},{1,0},{2,1},{3,2},{4,7},{5,4},{6,5},{7,6},{8,11},{9,8},{10,9... | collective-permute-start | bytes 3145736 | tf_op jit(solution)/shard_map/ppermute | solution.py:386
  152.2 44.3 %collective-permute-start.5 = (f32[128,2048]{1,0:T(8,128)}, f32[128,2048]{1,0:T(8,128)}, u32[]{:S(2)}, u32[]{:S(2)}) collective-permute-start(f32[128,2048]{1,0:T(8,128)} %get-tuple-element.81), channel_id=1, source_target_pairs={{0,2},{1,3},{2,0},{3,1},{4,6},{5,7},{6,4},{7,5},{8,10},{9,11},{10,... | collective-permute-start | bytes 3145736 | tf_op jit(solution)/shard_map/ppermute | solution.py:386
  166.8 0.7 copy-start.5
  175.3 24.1 %collective-permute-start.7 = (f32[2,640]{1,0:T(2,128)}, f32[2,640]{1,0:T(2,128)S(1)}, u32[]{:S(2)}, u32[]{:S(2)}) collective-permute-start(f32[2,640]{1,0:T(2,128)} %get-tuple-element.67), channel_id=1, source_target_pairs={{4,0},{8,4},{12,8},{16,12},{20,16},{24,20},{28,24},{32,28},{36,32}... | collective-permute-start | bytes 15368 | tf_op jit(solution)/shard_map/ppermute | solution.py:369
  180.4 21.2 %all-to-all-start.4 = ((f32[16,16,128]{2,1,0:T(8,128)}), f32[16,16,128]{2,1,0:T(8,128)S(1)}, u32[]{:S(2)}, u32[]{:S(2)}) async-start(f32[16,16,128]{2,1,0:T(8,128)} %broadcast_in_dim.7), calls=%async_computation.4 | async-start | bytes 262144 | tf_op jit(solution)/shard_map/all_to_all | solution.py:412
  199.4 0.6 copy-start.7

commit v4 on v3

--- a/solution.py
+++ b/solution.py
@@ -13,6 +13,7 @@
 WIDE = 256
 SUMS = FEAT
 
+TOGETHER = {"first": 4, "local": 2, "middle": 2, "inner": 4, "last": 4, "finish": 2}
 SEQ = ("x", "z", "core")
 HIGHEST = lax.Precision.HIGHEST
 F32 = jnp.float32
@@ -49,13 +50,22 @@
     return pair[:, :VD] + pair[:, VD:]
 
 
+def when(condition):
+    if isinstance(condition, bool):
+        return (lambda f: f()) if condition else (lambda f: None)
+    return pl.when(condition)
+
+
 def selectors(places, head):
-    row = lax.broadcasted_iota(jnp.int32, (WIDE, WIDE), 0)
-    own = (((row >> 4) & 3) == head) & (row < 192)
-    channel = row & 15
-    first = jnp.where(own & (channel == places[0:1, :]), 1.0, 0.0).astype(BF16)
-    second = jnp.where(own & (channel == places[1:2, :]), 1.0, 0.0).astype(BF16)
-    return first, second
+    row = lax.broadcasted_iota(jnp.int32, (64, WIDE), 0)
+    channel = jnp.where((row >> 4) == head, row & 15, -2)
+    return tuple(
+        jnp.where(channel == places[i : i + 1, :], 1.0, 0.0).astype(BF16) for i in (0, 1)
+    )
+
+
+def tall(select):
+    return jnp.concatenate([select, select, select, jnp.zeros_like(select)], axis=0)
 
 
 def head_lanes(head, width):
@@ -65,14 +75,14 @@
 
 def expand(pieces, select, factors):
     return (
-        mm(pieces, select[0], 1, 0) + factors[1:2, :],
-        mm(pieces, select[1], 1, 0) + factors[2:3, :],
+        mm(pieces, tall(select[0]), 1, 0) + factors[1:2, :],
+        mm(pieces, tall(select[1]), 1, 0) + factors[2:3, :],
     )
 
 
 def pull(grad_first, grad_second, select):
-    return mm(grad_first.astype(BF16), select[0][:64, :], 1, 1) + mm(
-        grad_second.astype(BF16), select[1][:64, :], 1, 1
+    return mm(grad_first.astype(BF16), select[0], 1, 1) + mm(
+        grad_second.astype(BF16), select[1], 1, 1
     )
 
 
@@ -136,58 +146,30 @@
 
 
 def first_kernel(
-    q_in, k_in, v_in, taps_q, taps_k, taps_v, places, factors,
+    head, q_in, k_in, v_in, rim_qk, rim_v, taps_q, taps_k, taps_v, places, factors,
     q4, k4, k5, vb, state, narrow, broad,
 ):
-    head = pl.program_id(0)
     length = q_in.shape[1]
-    none = jnp.zeros((8, 1), F32)
-
-    @pl.when(head == 0)
-    def _():
-        extend(narrow, q_in[...].astype(F32).T, jnp.broadcast_to(none, (8, 64)))
+
+    @when(head == 0)
+    def _():
+        rim = rim_qk[8:, :].astype(F32)
+        extend(narrow, q_in[...].astype(F32).T, rim[:, :64])
         split_query(convolve(narrow, taps_q[...], length), q4)
-        extend(narrow, k_in[...].astype(F32).T, jnp.broadcast_to(none, (8, 64)))
+        extend(narrow, k_in[...].astype(F32).T, rim[:, 64:])
         split_key(convolve(narrow, taps_k[...], length), k4, k5)
 
-    extend(broad, v_in[...], jnp.broadcast_to(none, (8, VD)))
+    extend(broad, v_in[...], rim_v[8:, :].astype(F32))
     value = jnp.concatenate(halves(convolve(broad, taps_v[...], length)), axis=1)
     vb[...] = value
     first, second = expand(k4[...], selectors(places[...], head), factors[...])
-    known = lax.broadcasted_iota(jnp.int32, (length, WIDE), 0) >= 2
-    phi = jnp.where(known, first * second, 0.0).astype(BF16)
+    phi = (first * second).astype(BF16)
     state[...] = pack(
         fold(mm(phi, value, 0, 0)), jnp.sum(phi.astype(F32), axis=0, keepdims=True)
     )
 
 
-def mend_kernel(
-    q_in, k_in, v_in, rim_qk, rim_v, taps_q, taps_k, taps_v, places, factors,
-    q4_in, k4_in, k5_in, vb_in, state_in, q4, k4, k5, vb, state, narrow, broad,
-):
-    head = pl.program_id(0)
-
-    @pl.when(head == 0)
-    def _():
-        rim = rim_qk[8:, :].astype(F32)
-        extend(narrow, q_in[...].astype(F32).T[:16, :], rim[:, :64])
-        split_query(convolve(narrow, taps_q[...], 16), q4)
-        extend(narrow, k_in[...].astype(F32).T[:16, :], rim[:, 64:])
-        split_key(convolve(narrow, taps_k[...], 16), k4, k5)
-
-    extend(broad, v_in[...], rim_v[8:, :].astype(F32))
-    value = jnp.concatenate(halves(convolve(broad, taps_v[...], 16)), axis=1)
-    vb[...] = value
-    first, second = expand(k4[...], selectors(places[...], head), factors[...])
-    missing = lax.broadcasted_iota(jnp.int32, (16, WIDE), 0) < 2
-    phi = jnp.where(missing, first * second, 0.0).astype(BF16)
-    state[...] = state_in[...] + pack(
-        fold(mm(phi, value, 0, 0)), jnp.sum(phi.astype(F32), axis=0, keepdims=True)
-    )
-
-
-def local_kernel(q4, k5, vb, numer, denom):
-    head = pl.program_id(0)
+def local_kernel(head, q4, k5, vb, numer, denom):
     a = similar(q4[...], k5[...], head)
     length = a.shape[0]
     weight = jnp.where(causal_mask(length), 1.0 + a + 0.5 * a * a, 0.0)
@@ -197,8 +179,7 @@
     denom[...] = jnp.broadcast_to(jnp.sum(weight, axis=1, keepdims=True), (length, VD))
 
 
-def middle_kernel(q4, before, numer, denom, up, places, factors, att, ng, dg, state):
-    head = pl.program_id(0)
+def middle_kernel(head, q4, before, numer, denom, up, places, factors, att, ng, dg, state):
     scale = factors[...]
     first, second = expand(q4[...], selectors(places[...], head), scale)
     phi = first * second * scale[0:1, :]
@@ -220,8 +201,7 @@
     )
 
 
-def inner_kernel(q4, k4, k5, vb, before, ng, dg, places, factors, gq, kd, gv):
-    head = pl.program_id(0)
+def inner_kernel(head, q4, k4, k5, vb, before, ng, dg, places, factors, gq, kd, gv):
     scale = factors[...]
     query, value = q4[...], vb[...]
     a = similar(query, k5[...], head)
@@ -254,25 +234,39 @@
     ) * scale[0:1, :]
     query_grad = query_direct + pull(phi_grad * second, phi_grad * first, select)
 
-    @pl.when(head == 0)
+    @when(head == 0)
     def _():
         gq[...] = query_grad
         kd[...] = key_direct
 
-    @pl.when(head > 0)
+    @when(head > 0)
     def _():
         gq[...] += query_grad
         kd[...] += key_direct
 
 
-def conv_back(scratch, grad, taps, length):
+def conv_back(scratch, grad, tail, taps):
+    length, width = grad.shape
     scratch[0:length, :] = grad
-    scratch[length : length + 8, :] = jnp.zeros((8, grad.shape[1]), F32)
+    scratch[length : length + 8, :] = jnp.concatenate([tail, jnp.zeros((6, width), F32)], axis=0)
     return (
         taps[0:1, :] * grad
         + taps[1:2, :] * scratch[1 : length + 1, :]
         + taps[2:3, :] * scratch[2 : length + 2, :]
     )
+
+
+def finish_kernel(
+    head, tail_qk, tail_v, taps_q, taps_k, taps_v, gq, gk, gv, grad_q, grad_k, grad_v,
+    narrow, broad,
+):
+    @when(head == 0)
+    def _():
+        tail = tail_qk[...]
+        grad_q[...] = conv_back(narrow, gq[...], tail[:, :64], taps_q[...]).T
+        grad_k[...] = conv_back(narrow, gk[...], tail[:, 64:], taps_k[...]).T
+
+    grad_v[...] = conv_back(broad, gv[...], tail_v[...], taps_v[...])
 
 
 def tap_sums(scratch, grad, length):
@@ -286,10 +280,9 @@
 
 
 def last_kernel(
-    q_in, k_in, v_in, rim_qk, rim_v, taps_q, taps_k, taps_v, places, factors,
-    k4, vb, after, gq, kd, gv_in, grad_q, grad_k, grad_v, taps_out, heads_first, narrow, broad, gk,
+    head, q_in, k_in, v_in, rim_qk, rim_v, places, factors,
+    k4, vb, after, gq, kd, gv_in, gk, gv, taps_out, heads_first, narrow, broad,
 ):
-    head = pl.program_id(0)
     length = q_in.shape[1]
     later, total = unpack(after[...])
     later_high, later_low = halves(later)
@@ -309,58 +302,39 @@
     )
     key_grad = pull(phi_grad * second, phi_grad * first, select)
 
-    @pl.when(head == 0)
+    @when(head == 0)
     def _():
         gk[...] = kd[...] + key_grad
 
-    @pl.when(head > 0)
+    @when(head > 0)
     def _():
         gk[...] += key_grad
 
     value_grad = gv_in[...] + mm((first * second).astype(BF16), later_high, 1, 0)
-    grad_v[...] = conv_back(broad, value_grad, taps_v[...], length)
+    gv[...] = value_grad
     extend(broad, v_in[...], rim_v[8:, :].astype(F32))
     sums = tap_sums(broad, value_grad, length)
     heads = heads_first.shape[1] // VD - 1
     for index in range(heads):
 
-        @pl.when(head == index)
+        @when(head == index)
         def _(index=index):
             taps_out[3 * index : 3 * index + 3, :] = sums
             heads_first[:, (index + 1) * VD : (index + 2) * VD] = value_grad[0:2, :]
 
-    @pl.when(head == pl.num_programs(0) - 1)
+    @when(head == heads - 1)
     def _():
         rim = rim_qk[8:, :].astype(F32)
         found = []
-        for source, taps, edge, grad, target in (
-            (q_in, taps_q, rim[:, :64], gq[...], grad_q),
-            (k_in, taps_k, rim[:, 64:], gk[...], grad_k),
+        for source, edge, grad in (
+            (q_in, rim[:, :64], gq[...]),
+            (k_in, rim[:, 64:], gk[...]),
         ):
-            target[...] = conv_back(narrow, grad, taps[...], length).T
             extend(narrow, source[...].astype(F32).T, edge)
             found.append(tap_sums(narrow, grad, length))
         taps_out[3 * heads : 3 * heads + 3, :] = jnp.concatenate(found, axis=1)
         taps_out[3 * heads + 3 :, :] = jnp.zeros((13 - 3 * heads, VD), F32)
         heads_first[:, :VD] = jnp.concatenate([gq[0:2, :], gk[0:2, :]], axis=1)
-
-
-def rim_kernel(tail, taps_q, taps_k, taps_v, q_in, k_in, v_in, grad_q, grad_k, grad_v):
-    tails = tail[...]
-    for start, taps, source, target in (
-        (0, taps_q, q_in, grad_q),
-        (64, taps_k, k_in, grad_k),
-        (128, taps_v, v_in, grad_v),
-    ):
-        width = taps.shape[1]
-        row = lax.broadcasted_iota(jnp.int32, (8, width), 0)
-        one, two = tails[0:1, start : start + width], tails[1:2, start : start + width]
-        weights = taps[...]
-        extra = jnp.where(row == 6, weights[2:3, :] * one, 0.0)
-        extra = extra + jnp.where(row == 7, weights[1:2, :] * one + weights[2:3, :] * two, 0.0)
-        if start < 128:
-            extra = jnp.concatenate([jnp.zeros((120, width), F32), extra], axis=0).T
-        target[...] = source[...] + extra
 
 
 def from_behind(block, axis, distance):
@@ -402,8 +376,8 @@
     total = lax.dynamic_slice_in_dim(whole, index * rows, rows, 0)
     for distance in range(1, size):
         target = (index + distance) % size
-        part = lax.dynamic_slice_in_dim(whole, target * rows, rows, 0)
-        total = total + turned(part, axis, distance)
+        part = lax.dynamic_slice_in_dim(whole, target * rows, rows, 0).astype(BF16)
+        total = total + turned(part, axis, distance).astype(F32)
     return total
 
 
@@ -426,11 +400,11 @@
     def whole(*shape):
         return pl.BlockSpec(shape, lambda h: (0,) * len(shape))
 
-    def per_head(rows):
-        return pl.BlockSpec((rows, VD), lambda h: (0, h))
-
-    pairs = pl.BlockSpec((length, 2 * VD), lambda h: (0, h))
-    packs = pl.BlockSpec((ROWS, VD), lambda h: (h, 0))
+    def per_head(rows, width=VD):
+        return ("lanes", rows, width)
+
+    pairs = per_head(length, 2 * VD)
+    packs = ("rows", ROWS, VD)
     table = whole(8, WIDE)
     pieces = whole(length, WIDE)
     narrow = whole(length, keys)
@@ -438,15 +412,45 @@
     def arr(rows, cols, dtype=F32):
         return jax.ShapeDtypeStruct((rows, cols), dtype)
 
-    def call(kernel, name, ins, outs, shapes, flops, scratch=()):
+    def call(kernel, name, together, ins, outs, shapes, flops, scratch=(), aliases=None):
+        kinds = [spec[0] if isinstance(spec, tuple) else "whole" for spec in ins + outs]
+
+        def spec_of(spec):
+            if not isinstance(spec, tuple):
+                return spec
+            kind, rows, width = spec
+            if kind == "lanes":
+                return pl.BlockSpec((rows, together * width), lambda h: (0, h))
+            if kind == "rows":
+                return pl.BlockSpec((together * rows, width), lambda h: (h, 0))
+            return whole(rows, width)
+
+        def step(*refs):
+            for sub in range(together):
+                head = sub if together == heads else pl.program_id(0) * together + sub
+                views = []
+                for kind, spec, ref in zip(kinds, ins + outs, refs):
+                    if kind == "lanes":
+                        ref = ref.at[:, sub * spec[2] : (sub + 1) * spec[2]]
+                    elif kind == "rows":
+                        ref = ref.at[sub * spec[1] : (sub + 1) * spec[1], :]
+                    elif kind == "rim":
+                        start = (head + 1) * VD
+                        if together < heads:
+                            start = pl.multiple_of(start, VD)
+                        ref = ref.at[:, pl.ds(start, VD)]
+                    views.append(ref)
+                kernel(head, *views, *refs[len(kinds) :])
+
         return pl.pallas_call(
-            kernel,
+            step,
             name=name,
-            grid=(heads,),
-            in_specs=ins,
-            out_specs=outs,
+            grid=(heads // together,),
+            in_specs=[spec_of(spec) for spec in ins],
+            out_specs=[spec_of(spec) for spec in outs],
             out_shape=shapes,
             scratch_shapes=list(scratch),
+            input_output_aliases=aliases or {},
             cost_estimate=pl.CostEstimate(
                 flops=flops, bytes_accessed=4 << 20, transcendentals=0
             ),
@@ -473,7 +477,7 @@
     weight_args = (conv_query, conv_key, conv_value, places, factors)
     inputs = (query_cols, key_cols, value_in)
     input_specs = [upright, upright, per_head(length)]
-    rim_specs = [whole(16, 2 * keys), pl.BlockSpec((16, VD), lambda h: (0, h + 1))]
+    rim_specs = [whole(16, 2 * keys), ("rim", 16, 2 * keys + values)]
     conv_ins = input_specs + rim_specs + weights
     conv_args = inputs + (rim, rim) + weight_args
     buffers = [pltpu.VMEM((length + 8, keys), F32), pltpu.VMEM((length + 8, VD), F32)]
@@ -481,33 +485,20 @@
     shapes_of = [arr(length, WIDE, BF16)] * 3 + [
         arr(length, 2 * values, BF16), arr(heads * ROWS, VD),
     ]
-    begun = call(
-        first_kernel, "first", input_specs + weights, pairs_of, shapes_of, 2 << 30, buffers
-    )(*inputs, *weight_args)
-    top = whole(16, WIDE)
-    corner = whole(keys, VD)
-    untouched = pl.BlockSpec(memory_space=pl.ANY)
-    q4, k4, k5, vb, local_state = pl.pallas_call(
-        mend_kernel,
-        name="mend",
-        grid=(heads,),
-        in_specs=[corner, corner, per_head(16)] + rim_specs + weights + [untouched] * 4 + [packs],
-        out_specs=[top, top, top, pl.BlockSpec((16, 2 * VD), lambda h: (0, h)), packs],
-        out_shape=shapes_of,
-        scratch_shapes=[pltpu.VMEM((24, keys), F32), pltpu.VMEM((24, VD), F32)],
-        input_output_aliases={10: 0, 11: 1, 12: 2, 13: 3, 14: 4},
-    )(*conv_args, *begun)
+    q4, k4, k5, vb, local_state = call(
+        first_kernel, "first", TOGETHER["first"], conv_ins, pairs_of, shapes_of, 2 << 30, buffers
+    )(*conv_args)
     cotangent = gathered(out_grad, "head")
     upstream = lax.dot_general(
         cotangent, out_proj, (((1,), (1,)), ((), ())), preferred_element_type=F32
     )
     numer, denom = call(
-        local_kernel, "local", [pieces, pieces, pairs],
+        local_kernel, "local", TOGETHER["local"], [pieces, pieces, pairs],
         [per_head(length)] * 2, [arr(length, values)] * 2, 4 << 30,
     )(q4, k5, vb)
     before, _ = carried_in(local_state, False)
     att, ng, dg, grad_state = call(
-        middle_kernel, "middle",
+        middle_kernel, "middle", TOGETHER["middle"],
         [pieces, packs] + [per_head(length)] * 3 + [table, table],
         [per_head(length)] * 3 + [packs],
         [arr(length, values, BF16), arr(length, values), arr(length, values)]
@@ -515,7 +506,7 @@
         4 << 30,
     )(q4, before, numer, denom, upstream, places, factors)
     gq, kd, gv = call(
-        inner_kernel, "inner",
+        inner_kernel, "inner", TOGETHER["inner"],
         [pieces] * 3 + [pairs, packs] + [per_head(length)] * 2 + [table, table],
         [narrow, narrow, per_head(length)],
         [arr(length, keys)] * 2 + [arr(length, values)],
@@ -524,34 +515,26 @@
     after, (gq, kd, gv) = carried_in(grad_state, True, (gq, kd, gv))
     partial = jnp.dot(att, out_proj, preferred_element_type=F32)
     mixed = scattered(partial, "head").astype(BF16)
-    grad_query, grad_key, grad_value, taps, first_rows = call(
-        last_kernel, "last",
-        conv_ins + [pieces, pairs, packs, narrow, narrow, per_head(length)],
-        [upright, upright, per_head(length), whole(16, VD), whole(2, 2 * keys + values)],
-        [arr(keys, length)] * 2
-        + [arr(length, values), arr(16, VD), arr(2, 2 * keys + values)],
-        4 << 30, buffers + [pltpu.VMEM((length, keys), F32)],
-    )(*conv_args, k4, vb, after, gq, kd, gv)
+    gk, gv, taps, first_rows = call(
+        last_kernel, "last", TOGETHER["last"],
+        input_specs + rim_specs + [table, table]
+        + [pieces, pairs, packs, narrow, narrow, per_head(length)],
+        [narrow, per_head(length), whole(16, VD), whole(2, 2 * keys + values)],
+        [arr(length, keys), arr(length, values), arr(16, VD), arr(2, 2 * keys + values)],
+        4 << 30, buffers,
+    )(*inputs, rim, rim, places, factors, k4, vb, after, gq, kd, gv)
+    first_rows, mixed = lax.optimization_barrier((first_rows, mixed))
     tail = from_behind(first_rows, SEQ, -1)
     taps = total_over(taps, "z")
-    rims = [
-        pl.BlockSpec((keys, VD), lambda i: (0, length // VD - 1)),
-        pl.BlockSpec((keys, VD), lambda i: (0, length // VD - 1)),
-        pl.BlockSpec((8, values), lambda i: (length // 8 - 1, 0)),
-    ]
-    grad_query, grad_key, grad_value = pl.pallas_call(
-        rim_kernel,
-        name="rims",
-        grid=(1,),
-        in_specs=[whole(2, 2 * keys + values), whole(3, keys), whole(3, keys), whole(3, values)]
-        + rims,
-        out_specs=rims,
-        out_shape=[arr(keys, length)] * 2 + [arr(length, values)],
-        input_output_aliases={4: 0, 5: 1, 6: 2},
-    )(tail, conv_query, conv_key, conv_value, grad_query, grad_key, grad_value)
-    taps, mixed, grad_query, grad_key, grad_value = lax.optimization_barrier(
-        (taps, mixed, grad_query, grad_key, grad_value)
-    )
+    taps, tail = lax.optimization_barrier((taps, tail))
+    grad_query, grad_key, grad_value = call(
+        finish_kernel, "finish", TOGETHER["finish"],
+        [whole(2, 2 * keys), ("rim", 2, 2 * keys + values)] + weights[:3]
+        + [narrow, narrow, per_head(length)],
+        [upright, upright, per_head(length)],
+        [arr(keys, length)] * 2 + [arr(length, values)],
+        1 << 24, buffers,
+    )(tail, tail, conv_query, conv_key, conv_value, gq, gk, gv)
     taps = total_over(taps, ("x", "core"))
     value_taps = taps[: 3 * heads].reshape(heads, 3, VD).transpose(1, 0, 2).reshape(3, values)
     other_taps = taps[3 * heads : 3 * heads + 3]

time: 216 us -> 204 us (0.944)
  blocking collectives: 11.4 us -> 0 us
  starting transfers between devices: 71.5 us -> 78.9 us
  Pallas kernels: 41.4 us -> 34.3 us
    ppermute x6, waiting for transfers between devices: 12.6 us -> 0.02 us  [turned(): lax.ppermute(block, axis, [(i, (i + distance) % size) for i in range(size)])]
    all_to_all x1 -> x0, blocking collectives: 11.4 us -> none  [to_all(): return lax.all_to_all(copies, axis, 0, 0, tiled=True)]
    all_to_all x1 -> x2, waiting for transfers between devices: 0.01 us -> 7.58 us  [to_all(): return lax.all_to_all(copies, axis, 0, 0, tiled=True)]
    all_to_all x1 -> x2, starting transfers between devices: 3.51 us -> 10.7 us  [to_all(): return lax.all_to_all(copies, axis, 0, 0, tiled=True)]
    pallas_call x7 -> x6, Pallas kernels: 39.8 us -> 32.6 us  [the longest x1 10 us: body(): call(inner_kernel, 'inner', TOGETHER['inner'], [pieces] * 3 + [pairs, pac...]
    ppermute x2, waiting for transfers between devices: 0.01 us -> 4.08 us  [from_behind(): return lax.ppermute(block, axis, route)]
  transfers between devices with their start and end apart: 13 -> 14, of which waited for: 5 -> 7; matrix products, arithmetic and copies ran while one was open for 9% -> 9% of each run, Pallas kernels for 14% -> 11%
where the time goes in v4:
time: 204 us; the launch traced here: 203 us
  starting transfers between devices  78.9 us (39%)
  waiting for transfers between devices  63.2 us (31%)
  Pallas kernels  34.3 us (17%)
  local copies, waits for them, and re-layouts  17.6 us (9%)
  matrix products  5.78 us (3%)
  other arithmetic  2.82 us (1%)
    all_to_all x2, waiting for transfers between devices, carried_in(): everyone = lax.all_to_all(packed.reshape(ranks, -1), SEQ, 0, 0, tiled=True)  28.2 us
    all_to_all x2, starting transfers between devices, carried_in(): everyone = lax.all_to_all(packed.reshape(ranks, -1), SEQ, 0, 0, tiled=True)  25.1 us
    all_to_all x2, waiting for transfers between devices, carried_in(): lax.all_to_all(sums, SEQ, 0, 0, tiled=True).reshape(packed.shape)  23.3 us
    ppermute x6, starting transfers between devices, turned(): lax.ppermute(block, axis, [(i, (i + distance) % size) for i in range(size)])  20.4 us
    all_to_all x2, starting transfers between devices, carried_in(): lax.all_to_all(sums, SEQ, 0, 0, tiled=True).reshape(packed.shape)  14 us
    all_to_all x2, starting transfers between devices, to_all(): return lax.all_to_all(copies, axis, 0, 0, tiled=True)  10.7 us
    pallas_call x1, Pallas kernels, body(): call(inner_kernel, 'inner', TOGETHER['inner'], [pieces] * 3 + [pairs, pac...  10 us
    ppermute x2, starting transfers between devices, from_behind(): return lax.ppermute(block, axis, route)  8.66 us
  transfers between devices with their start and end apart: 14, of which 7 were waited for; matrix products, arithmetic and copies ran while one was open for 9% of the time, Pallas kernels for 11%

profile of v4, /device:TPU:1, one launch (start us, length us, event | category | flops | bytes accessed | tf_op | source)
XLA Modules:
  0.0 203.4 jit_solution(128027244823770198)
XLA Ops:
  0.6 0.0 copy-start
  0.6 1.6 edge.1
  2.3 5.0 %collective-permute-start = (bf16[16,640]{1,0:T(8,128)(2,1)}, bf16[16,640]{1,0:T(8,128)(2,1)S(1)}, u32[]{:S(2)}, u32[]{:S(2)}) collective-permute-start(bf16[16,640]{1,0:T(8,128)(2,1)} %edge.1), channel_id=1, source_target_pairs={{0,4},{4,8},{8,12},{12,16},{16,20},{20,24},{24,28},{28,32},{32,36}... | collective-permute-start | bytes 61448 | tf_op jit(solution)/shard_map/ppermute | solution.py:343
  7.3 4.1 %collective-permute-done.refs_3_.refs_4_ = bf16[16,640]{1,0:T(8,128)(2,1)S(1)} collective-permute-done((bf16[16,640]{1,0:T(8,128)(2,1)}, bf16[16,640]{1,0:T(8,128)(2,1)S(1)}, u32[]{:S(2)}, u32[]{:S(2)}) %collective-permute-start) | collective-permute-done | bytes 20512 | tf_op jit(solution)/shard_map/ppermute | solution.py:343
  11.4 0.6 copy-done.7
  12.0 4.4 %first.1 = (bf16[512,256]{1,0:T(8,128)(2,1)}, bf16[512,256]{1,0:T(8,128)(2,1)}, bf16[512,256]{1,0:T(8,128)(2,1)}, bf16[512,1024]{1,0:T(8,128)(2,1)}, f32[640,128]{1,0:T(8,128)}) custom-call(bf16[64,512]{1,0:T(8,128)(2,1)} %bitcast.32, bf16[64,512]{1,0:T(8,128)(2,1)} %bitcast.35, bf16[512,512]{1,0:T(8,128)(2,1)} %refs_2_.4, bf16[16,640]{1,0:T(8,128)(2,1)} %copy-done.7, ...), custom_call_target="tpu_custom_call" | custom-call | flops 2147483648 | bytes 4194304 | tf_op jit(solution)/shard_map/first/pallas_call | solution.py:488
  16.4 17.9 %all-to-all-start = ((f32[128,1,640]{2,1,0:T(1,128)}), f32[128,1,640]{2,1,0:T(1,128)S(1)}, u32[]{:S(2)}, u32[]{:S(2)}) async-start(f32[128,1,640]{2,1,0:T(1,128)} %bitcast.26), calls=%async_computation | async-start | bytes 655360 | tf_op jit(solution)/shard_map/all_to_all | solution.py:348
  34.3 0.0 copy-done.2
  34.3 3.2 %collective-permute-start.1 = (bf16[128,2048]{1,0:T(8,128)(2,1)S(1)}, bf16[128,2048]{1,0:T(8,128)(2,1)}, u32[]{:S(2)}, u32[]{:S(2)}) collective-permute-start(bf16[128,2048]{1,0:T(8,128)(2,1)S(1)} %copy-done.2), channel_id=1, source_target_pairs={{0,1},{1,2},{2,3},{3,0},{4,5},{5,6},{6,7},{7,4},{8,9},{9,10},{10,1... | collective-permute-start | bytes 1572872 | tf_op jit(solution)/shard_map/ppermute | solution.py:360
  37.5 3.4 %collective-permute-start.3 = (bf16[128,2048]{1,0:T(8,128)(2,1)S(1)}, bf16[128,2048]{1,0:T(8,128)(2,1)S(1)}, u32[]{:S(2)}, u32[]{:S(2)}) collective-permute-start(bf16[128,2048]{1,0:T(8,128)(2,1)S(1)} %copy-done.2), channel_id=1, source_target_pairs={{0,3},{1,0},{2,1},{3,2},{4,7},{5,4},{6,5},{7,6},{8,11},{9,8},{10,9... | collective-permute-start | bytes 1572872 | tf_op jit(solution)/shard_map/ppermute | solution.py:360
  40.9 3.5 %collective-permute-start.2 = (bf16[128,2048]{1,0:T(8,128)(2,1)S(1)}, bf16[128,2048]{1,0:T(8,128)(2,1)}, u32[]{:S(2)}, u32[]{:S(2)}) collective-permute-start(bf16[128,2048]{1,0:T(8,128)(2,1)S(1)} %copy-done.2), channel_id=1, source_target_pairs={{0,2},{1,3},{2,0},{3,1},{4,6},{5,7},{6,4},{7,5},{8,10},{9,11},{10,... | collective-permute-start | bytes 1572872 | tf_op jit(solution)/shard_map/ppermute | solution.py:360
  44.5 1.6 broadcast_in_dim.6
  46.1 0.8 constant_dynamic-update-slice_fusion.3
  47.0 12.7 %all-to-all-done = f32[128,1,640]{2,1,0:T(1,128)S(1)} async-done(((f32[128,1,640]{2,1,0:T(1,128)}), f32[128,1,640]{2,1,0:T(1,128)S(1)}, u32[]{:S(2)}, u32[]{:S(2)}) %all-to-all-start) | async-done | bytes 327712 | tf_op jit(solution)/shard_map/all_to_all | solution.py:348
  59.7 0.3 convolution_bitcast_fusion
  60.0 1.1 copy.23
  61.1 7.0 %all-to-all-start.1 = ((f32[128,1,640]{2,1,0:T(1,128)}), f32[128,1,640]{2,1,0:T(1,128)S(1)}, u32[]{:S(2)}, u32[]{:S(2)}) async-start(f32[128,1,640]{2,1,0:T(1,128)} %copy.23), calls=%async_computation.1 | async-start | bytes 655360 | tf_op jit(solution)/shard_map/all_to_all | solution.py:355
  68.1 4.5 %local.1 = (f32[512,512]{1,0:T(8,128)}, f32[512,512]{1,0:T(8,128)}) custom-call(bf16[512,256]{1,0:T(8,128)(2,1)} %get-tuple-element.38.refs_0_, bf16[512,256]{1,0:T(8,128)(2,1)} %get-tuple-element.40.refs_1_.refs_2_, bf16[512,1024]{1,0:T(8,128)(2,1)} %get-tuple-element.37.refs_2_.refs_3_.refs_8_), custom_call_target="tpu_custom_call" | custom-call | flops 4294967296 | bytes 4194304 | tf_op jit(solution)/shard_map/local/pallas_call | solution.py:495
  72.5 0.0 collective-permute-done.1
  72.5 1.9 constant_dynamic-update-slice_fusion.2
  74.4 0.0 collective-permute-done.2
  74.4 1.9 constant_dynamic-update-slice_fusion.1
  76.3 0.0 collective-permute-done.3
  76.3 0.9 constant_dynamic-update-slice_fusion
  77.2 0.0 copy-done
  77.2 3.9 %fusion.6.refs_4_ = f32[512,512]{1,0:T(8,128)} fusion(bf16[512,2048]{1,0:T(8,128)(2,1)} %constant_dynamic-update-slice_fusion, bf16[512,2048]{1,0:T(8,128)(2,1)S(1)} %copy-done), kind=kOutput, calls=%fused_computation.17 | convolution fusion | flops 1073741824 | bytes 5242880 | tf_op jit(solution)/shard_map/dot_general | solution.py:492
  81.1 12.5 %all-to-all-done.1 = f32[128,1,640]{2,1,0:T(1,128)S(1)} async-done(((f32[128,1,640]{2,1,0:T(1,128)}), f32[128,1,640]{2,1,0:T(1,128)S(1)}, u32[]{:S(2)}, u32[]{:S(2)}) %all-to-all-start.1) | async-done | bytes 327712 | tf_op jit(solution)/shard_map/all_to_all | solution.py:355
  93.6 0.7 copy-done.5
  94.3 5.0 %middle.1 = (bf16[512,512]{1,0:T(8,128)(2,1)}, f32[512,512]{1,0:T(8,128)}, f32[512,512]{1,0:T(8,128)}, f32[640,128]{1,0:T(8,128)}) custom-call(bf16[512,256]{1,0:T(8,128)(2,1)} %get-tuple-element.38.refs_0_, f32[640,128]{1,0:T(8,128)} %bitcast.28, f32[512,512]{1,0:T(8,128)} %get-tuple-element.41.refs_2_, f32[512,512]{1,0:T(8,128)} %get-tuple-element.42.refs_3_, ...), custom_call_target="tpu_custom_call" | custom-call | flops 4294967296 | bytes 4194304 | tf_op jit(solution)/shard_map/middle/pallas_call | solution.py:500
  99.3 7.2 %all-to-all-start.2 = ((f32[128,1,640]{2,1,0:T(1,128)}), f32[128,1,640]{2,1,0:T(1,128)S(1)}, u32[]{:S(2)}, u32[]{:S(2)}) async-start(f32[128,1,640]{2,1,0:T(1,128)} %bitcast.30), calls=%async_computation.2 | async-start | bytes 655360 | tf_op jit(solution)/shard_map/all_to_all | solution.py:348
  106.4 10.0 %inner.1 = (f32[512,64]{1,0:T(8,128)}, f32[512,64]{1,0:T(8,128)}, f32[512,512]{1,0:T(8,128)}) custom-call(bf16[512,256]{1,0:T(8,128)(2,1)} %get-tuple-element.38.refs_0_, bf16[512,256]{1,0:T(8,128)(2,1)} %get-tuple-element.36.refs_1_.refs_7_, bf16[512,256]{1,0:T(8,128)(2,1)} %get-tuple-element.40.refs_1_.refs_2_, ...), custom_call_target="tpu_custom_call" | custom-call | flops 8589934592 | bytes 4194304 | tf_op jit(solution)/shard_map/inner/pallas_call | solution.py:508
  116.5 15.5 %all-to-all-done.2 = f32[128,1,640]{2,1,0:T(1,128)S(1)} async-done(((f32[128,1,640]{2,1,0:T(1,128)}), f32[128,1,640]{2,1,0:T(1,128)S(1)}, u32[]{:S(2)}, u32[]{:S(2)}) %all-to-all-start.2) | async-done | bytes 327712 | tf_op jit(solution)/shard_map/all_to_all | solution.py:348
  131.9 0.3 fusion
  132.2 1.1 copy.25
  133.3 7.0 %all-to-all-start.3 = ((f32[128,1,640]{2,1,0:T(1,128)}), f32[128,1,640]{2,1,0:T(1,128)S(1)}, u32[]{:S(2)}, u32[]{:S(2)}) async-start(f32[128,1,640]{2,1,0:T(1,128)} %copy.25), calls=%async_computation.3 | async-start | bytes 655360 | tf_op jit(solution)/shard_map/all_to_all | solution.py:355
  140.4 0.0 copy-done.3
  140.4 1.3 fusion.7
  141.6 0.0 copy-start.1
  141.6 2.0 copy-done.1
  143.6 1.0 dynamic-slice_convert_fusion.2
  144.6 3.2 %collective-permute-start.4 = (bf16[128,2048]{1,0:T(8,128)(2,1)}, bf16[128,2048]{1,0:T(8,128)(2,1)}, u32[]{:S(2)}, u32[]{:S(2)}) collective-permute-start(bf16[128,2048]{1,0:T(8,128)(2,1)} %get-tuple-element.65), channel_id=1, source_target_pairs={{0,1},{1,2},{2,3},{3,0},{4,5},{5,6},{6,7},{7,4},{8,9},{9,10},{10,1... | collective-permute-start | bytes 1572872 | tf_op jit(solution)/shard_map/ppermute | solution.py:360
  147.8 3.4 %collective-permute-start.6 = (bf16[128,2048]{1,0:T(8,128)(2,1)S(1)}, bf16[128,2048]{1,0:T(8,128)(2,1)}, u32[]{:S(2)}, u32[]{:S(2)}) collective-permute-start(bf16[128,2048]{1,0:T(8,128)(2,1)S(1)} %get-tuple-element.66), channel_id=1, source_target_pairs={{0,3},{1,0},{2,1},{3,2},{4,7},{5,4},{6,5},{7,6},{8,11},{9,8},{10,9... | collective-permute-start | bytes 1572872 | tf_op jit(solution)/shard_map/ppermute | solution.py:360
  151.2 3.8 %collective-permute-start.5 = (bf16[128,2048]{1,0:T(8,128)(2,1)S(1)}, bf16[128,2048]{1,0:T(8,128)(2,1)}, u32[]{:S(2)}, u32[]{:S(2)}) collective-permute-start(bf16[128,2048]{1,0:T(8,128)(2,1)S(1)} %get-tuple-element.67), channel_id=1, source_target_pairs={{0,2},{1,3},{2,0},{3,1},{4,6},{5,7},{6,4},{7,5},{8,10},{9,11},{10,... | collective-permute-start | bytes 1572872 | tf_op jit(solution)/shard_map/ppermute | solution.py:360
  155.0 10.8 %all-to-all-done.3 = f32[128,1,640]{2,1,0:T(1,128)S(1)} async-done(((f32[128,1,640]{2,1,0:T(1,128)}), f32[128,1,640]{2,1,0:T(1,128)S(1)}, u32[]{:S(2)}, u32[]{:S(2)}) %all-to-all-start.3) | async-done | bytes 327712 | tf_op jit(solution)/shard_map/all_to_all | solution.py:355
  165.8 0.8 copy-done.4
  166.6 6.0 %last.1 = (f32[512,64]{1,0:T(8,128)}, f32[512,512]{1,0:T(8,128)}, f32[16,128]{1,0:T(8,128)}, f32[2,640]{1,0:T(2,128)}) custom-call(bf16[64,512]{1,0:T(8,128)(2,1)} %bitcast.33, bf16[64,512]{1,0:T(8,128)(2,1)} %bitcast.36, bf16[512,512]{1,0:T(8,128)(2,1)} %refs_2_.4, bf16[16,640]{1,0:T(8,128)(2,1)} %copy-done.7, bf16[16,640]{1,0:T(8,128)(2,1)} %copy-done.7, ...), custom_call_target="tpu_custom_call" | custom-call | flops 4294967296 | bytes 4194304 | tf_op jit(solution)/shard_map/last/pallas_call | solution.py:518
  172.6 1.4 broadcast_in_dim.7
  173.9 3.6 %all-to-all-start.4 = ((f32[16,16,128]{2,1,0:T(8,128)}), f32[16,16,128]{2,1,0:T(8,128)S(1)}, u32[]{:S(2)}, u32[]{:S(2)}) async-start(f32[16,16,128]{2,1,0:T(8,128)} %broadcast_in_dim.7), calls=%async_computation.4 | async-start | bytes 262144 | tf_op jit(solution)/shard_map/all_to_all | solution.py:386
  177.6 0.0 collective-permute-done.4
  177.6 0.0 collective-permute-done.6
  177.6 0.0 collective-permute-done.5
  177.6 2.8 %add_convert_fusion = bf16[128,2048]{1,0:T(8,128)(2,1)} fusion(bf16[128,2048]{1,0:T(8,128)(2,1)} %collective-permute-done.6, bf16[128,2048]{1,0:T(8,128)(2,1)} %collective-permute-done.5, bf16[128,2048]{1,0:T(8,128)(2,1)} %collective-permute-done.4, f32[512,2048]{1,0:T(8,128)} %copy-done.1, s32[]{:T(128)S(6)} %select_n.63), kind=kLoop, calls=%fused_computation.1 | loop fusion | flops 1835008 | bytes 3145732 | tf_op jit(solution)/shard_map/convert_element_type | solution.py:517
  180.4 0.0 copy-done.8
  180.4 3.6 %collective-permute-start.7 = (f32[2,640]{1,0:T(2,128)S(1)}, f32[2,640]{1,0:T(2,128)S(1)}, u32[]{:S(2)}, u32[]{:S(2)}) collective-permute-start(f32[2,640]{1,0:T(2,128)S(1)} %copy-done.8), channel_id=1, source_target_pairs={{4,0},{8,4},{12,8},{16,12},{20,16},{24,20},{28,24},{32,28},{36,32}... | collective-permute-start | bytes 15368 | tf_op jit(solution)/shard_map/ppermute | solution.py:343
  184.0 5.5 %all-to-all-done.4 = f32[16,16,128]{2,1,0:T(8,128)S(1)} async-done(((f32[16,16,128]{2,1,0:T(8,128)}), f32[16,16,128]{2,1,0:T(8,128)S(1)}, u32[]{:S(2)}, u32[]{:S(2)}) %all-to-all-start.4) | async-done | bytes 131104 | tf_op jit(solution)/shard_map/all_to_all | solution.py:386
  189.6 0.0 collective-permute-done.7.refs_0_.refs_1_
  189.6 0.0 copy-start.6
  189.6 0.6 broadcast_in_dim.8
  190.2 7.1 %all-to-all-start.5 = ((f32[8,16,128]{2,1,0:T(8,128)}), f32[8,16,128]{2,1,0:T(8,128)S(1)}, u32[]{:S(2)}, u32[]{:S(2)}) async-start(f32[8,16,128]{2,1,0:T(8,128)} %broadcast_in_dim.8), calls=%async_computation.5 | async-start | bytes 131072 | tf_op jit(solution)/shard_map/all_to_all | solution.py:386
  197.3 0.0 copy-done.6
  197.3 2.8 %finish.1 = (f32[64,512]{1,0:T(8,128)}, f32[64,512]{1,0:T(8,128)}, f32[512,512]{1,0:T(8,128)}) custom-call(f32[2,640]{1,0:T(2,128)} %copy-done.6, f32[2,640]{1,0:T(2,128)} %copy-done.6, f32[3,64]{1,0:T(4,128)} %refs_2_.5, f32[3,64]{1,0:T(4,128)} %refs_3_.1, f32[3,512]{1,0:T(4,128)} %refs_4_.1, f32[512,64]{1,0:T(8,128)} %get-tuple-element.50.refs_10_.refs_5_, ...), custom_call_target="tpu_custom_call" | custom-call | flops 16777216 | bytes 4194304 | tf_op jit(solution)/shard_map/finish/pallas_call | solution.py:530
  200.1 2.1 %all-to-all-done.5 = f32[8,16,128]{2,1,0:T(8,128)S(1)} async-done(((f32[8,16,128]{2,1,0:T(8,128)}), f32[8,16,128]{2,1,0:T(8,128)S(1)}, u32[]{:S(2)}, u32[]{:S(2)}) %all-to-all-start.5) | async-done | bytes 65568 | tf_op jit(solution)/shard_map/all_to_all | solution.py:386
  202.2 0.7 fusion.5
  202.8 0.6 reshape.44
  (8 shorter events, 0.0 us)
Async XLA Ops:
  0.6 76.6 %copy-start = (bf16[512,2048]{1,0:T(8,128)(2,1)S(1)}, bf16[512,2048]{1,0:T(8,128)(2,1)}, u32[]{:S(2)}) copy-start(bf16[512,2048]{1,0:T(8,128)(2,1)} %param.16) | copy-start | bytes 6291460
  2.3 32.1 %copy-start.2 = (bf16[128,2048]{1,0:T(8,128)(2,1)S(1)}, bf16[128,2048]{1,0:T(8,128)(2,1)}, u32[]{:S(2)}) copy-start(bf16[128,2048]{1,0:T(8,128)(2,1)} %param.17) | copy-start | bytes 1572868
  2.3 9.1 %collective-permute-start = (bf16[16,640]{1,0:T(8,128)(2,1)}, bf16[16,640]{1,0:T(8,128)(2,1)S(1)}, u32[]{:S(2)}, u32[]{:S(2)}) collective-permute-start(bf16[16,640]{1,0:T(8,128)(2,1)} %edge.1), channel_id=1, source_target_pairs={{0,4},{4,8},{8,12},{12,16},{16,20},{20,24},{24,28},{28,32},{32,36}... | collective-permute-start | bytes 61448 | tf_op jit(solution)/shard_map/ppermute | solution.py:343
  11.4 0.6 copy-start.7
  16.4 43.3 %all-to-all-start = ((f32[128,1,640]{2,1,0:T(1,128)}), f32[128,1,640]{2,1,0:T(1,128)S(1)}, u32[]{:S(2)}, u32[]{:S(2)}) async-start(f32[128,1,640]{2,1,0:T(1,128)} %bitcast.26), calls=%async_computation | async-start | bytes 655360 | tf_op jit(solution)/shard_map/all_to_all | solution.py:348
  34.3 38.2 %collective-permute-start.1 = (bf16[128,2048]{1,0:T(8,128)(2,1)S(1)}, bf16[128,2048]{1,0:T(8,128)(2,1)}, u32[]{:S(2)}, u32[]{:S(2)}) collective-permute-start(bf16[128,2048]{1,0:T(8,128)(2,1)S(1)} %copy-done.2), channel_id=1, source_target_pairs={{0,1},{1,2},{2,3},{3,0},{4,5},{5,6},{6,7},{7,4},{8,9},{9,10},{10,1... | collective-permute-start | bytes 1572872 | tf_op jit(solution)/shard_map/ppermute | solution.py:360
  37.5 38.8 %collective-permute-start.3 = (bf16[128,2048]{1,0:T(8,128)(2,1)S(1)}, bf16[128,2048]{1,0:T(8,128)(2,1)S(1)}, u32[]{:S(2)}, u32[]{:S(2)}) collective-permute-start(bf16[128,2048]{1,0:T(8,128)(2,1)S(1)} %copy-done.2), channel_id=1, source_target_pairs={{0,3},{1,0},{2,1},{3,2},{4,7},{5,4},{6,5},{7,6},{8,11},{9,8},{10,9... | collective-permute-start | bytes 1572872 | tf_op jit(solution)/shard_map/ppermute | solution.py:360
  40.9 33.5 %collective-permute-start.2 = (bf16[128,2048]{1,0:T(8,128)(2,1)S(1)}, bf16[128,2048]{1,0:T(8,128)(2,1)}, u32[]{:S(2)}, u32[]{:S(2)}) collective-permute-start(bf16[128,2048]{1,0:T(8,128)(2,1)S(1)} %copy-done.2), channel_id=1, source_target_pairs={{0,2},{1,3},{2,0},{3,1},{4,6},{5,7},{6,4},{7,5},{8,10},{9,11},{10,... | collective-permute-start | bytes 1572872 | tf_op jit(solution)/shard_map/ppermute | solution.py:360
  61.1 32.5 %all-to-all-start.1 = ((f32[128,1,640]{2,1,0:T(1,128)}), f32[128,1,640]{2,1,0:T(1,128)S(1)}, u32[]{:S(2)}, u32[]{:S(2)}) async-start(f32[128,1,640]{2,1,0:T(1,128)} %copy.23), calls=%async_computation.1 | async-start | bytes 655360 | tf_op jit(solution)/shard_map/all_to_all | solution.py:355
  93.6 0.7 copy-start.5
  99.3 32.7 %all-to-all-start.2 = ((f32[128,1,640]{2,1,0:T(1,128)}), f32[128,1,640]{2,1,0:T(1,128)S(1)}, u32[]{:S(2)}, u32[]{:S(2)}) async-start(f32[128,1,640]{2,1,0:T(1,128)} %bitcast.30), calls=%async_computation.2 | async-start | bytes 655360 | tf_op jit(solution)/shard_map/all_to_all | solution.py:348
  116.4 23.9 %copy-start.3 = (bf16[512,512]{1,0:T(8,128)(2,1)S(1)}, bf16[512,512]{1,0:T(8,128)(2,1)}, u32[]{:S(2)}) copy-start(bf16[512,512]{1,0:T(8,128)(2,1)} %get-tuple-element.54) | copy-start | bytes 1572868
  133.3 32.5 %all-to-all-start.3 = ((f32[128,1,640]{2,1,0:T(1,128)}), f32[128,1,640]{2,1,0:T(1,128)S(1)}, u32[]{:S(2)}, u32[]{:S(2)}) async-start(f32[128,1,640]{2,1,0:T(1,128)} %copy.25), calls=%async_computation.3 | async-start | bytes 655360 | tf_op jit(solution)/shard_map/all_to_all | solution.py:355
  141.6 2.0 copy-start.1
  144.6 33.0 %collective-permute-start.4 = (bf16[128,2048]{1,0:T(8,128)(2,1)}, bf16[128,2048]{1,0:T(8,128)(2,1)}, u32[]{:S(2)}, u32[]{:S(2)}) collective-permute-start(bf16[128,2048]{1,0:T(8,128)(2,1)} %get-tuple-element.65), channel_id=1, source_target_pairs={{0,1},{1,2},{2,3},{3,0},{4,5},{5,6},{6,7},{7,4},{8,9},{9,10},{10,1... | collective-permute-start | bytes 1572872 | tf_op jit(solution)/shard_map/ppermute | solution.py:360
  147.8 29.8 %collective-permute-start.6 = (bf16[128,2048]{1,0:T(8,128)(2,1)S(1)}, bf16[128,2048]{1,0:T(8,128)(2,1)}, u32[]{:S(2)}, u32[]{:S(2)}) collective-permute-start(bf16[128,2048]{1,0:T(8,128)(2,1)S(1)} %get-tuple-element.66), channel_id=1, source_target_pairs={{0,3},{1,0},{2,1},{3,2},{4,7},{5,4},{6,5},{7,6},{8,11},{9,8},{10,9... | collective-permute-start | bytes 1572872 | tf_op jit(solution)/shard_map/ppermute | solution.py:360
  151.2 26.4 %collective-permute-start.5 = (bf16[128,2048]{1,0:T(8,128)(2,1)S(1)}, bf16[128,2048]{1,0:T(8,128)(2,1)}, u32[]{:S(2)}, u32[]{:S(2)}) collective-permute-start(bf16[128,2048]{1,0:T(8,128)(2,1)S(1)} %get-tuple-element.67), channel_id=1, source_target_pairs={{0,2},{1,3},{2,0},{3,1},{4,6},{5,7},{6,4},{7,5},{8,10},{9,11},{10,... | collective-permute-start | bytes 1572872 | tf_op jit(solution)/shard_map/ppermute | solution.py:360
  165.8 0.8 copy-start.4
  172.6 7.8 %copy-start.8 = (f32[2,640]{1,0:T(2,128)S(1)}, f32[2,640]{1,0:T(2,128)}, u32[]{:S(2)}) copy-start(f32[2,640]{1,0:T(2,128)} %get-tuple-element.57) | copy-start | bytes 15364
  173.9 15.6 %all-to-all-start.4 = ((f32[16,16,128]{2,1,0:T(8,128)}), f32[16,16,128]{2,1,0:T(8,128)S(1)}, u32[]{:S(2)}, u32[]{:S(2)}) async-start(f32[16,16,128]{2,1,0:T(8,128)} %broadcast_in_dim.7), calls=%async_computation.4 | async-start | bytes 262144 | tf_op jit(solution)/shard_map/all_to_all | solution.py:386
  180.4 9.2 %collective-permute-start.7 = (f32[2,640]{1,0:T(2,128)S(1)}, f32[2,640]{1,0:T(2,128)S(1)}, u32[]{:S(2)}, u32[]{:S(2)}) collective-permute-start(f32[2,640]{1,0:T(2,128)S(1)} %copy-done.8), channel_id=1, source_target_pairs={{4,0},{8,4},{12,8},{16,12},{20,16},{24,20},{28,24},{32,28},{36,32}... | collective-permute-start | bytes 15368 | tf_op jit(solution)/shard_map/ppermute | solution.py:343
  189.6 7.7 %copy-start.6 = (f32[2,640]{1,0:T(2,128)}, f32[2,640]{1,0:T(2,128)S(1)}, u32[]{:S(2)}) copy-start(f32[2,640]{1,0:T(2,128)S(1)} %collective-permute-done.7.refs_0_.refs_1_) | copy-start | bytes 15364
  190.2 11.9 %all-to-all-start.5 = ((f32[8,16,128]{2,1,0:T(8,128)}), f32[8,16,128]{2,1,0:T(8,128)S(1)}, u32[]{:S(2)}, u32[]{:S(2)}) async-start(f32[8,16,128]{2,1,0:T(8,128)} %broadcast_in_dim.8), calls=%async_computation.5 | async-start | bytes 131072 | tf_op jit(solution)/shard_map/all_to_all | solution.py:386

commit v5 on v4

--- a/solution.py
+++ b/solution.py
@@ -333,7 +333,10 @@
             extend(narrow, source[...].astype(F32).T, edge)
             found.append(tap_sums(narrow, grad, length))
         taps_out[3 * heads : 3 * heads + 3, :] = jnp.concatenate(found, axis=1)
-        taps_out[3 * heads + 3 :, :] = jnp.zeros((13 - 3 * heads, VD), F32)
+        taps_out[3 * heads + 3 : 16, :] = jnp.zeros((13 - 3 * heads, VD), F32)
+        block = taps_out[0:16, :]
+        for copy in range(1, taps_out.shape[0] // 16):
+            taps_out[16 * copy : 16 * copy + 16, :] = block
         heads_first[:, :VD] = jnp.concatenate([gq[0:2, :], gk[0:2, :]], axis=1)
 
 
@@ -515,17 +518,19 @@
     after, (gq, kd, gv) = carried_in(grad_state, True, (gq, kd, gv))
     partial = jnp.dot(att, out_proj, preferred_element_type=F32)
     mixed = scattered(partial, "head").astype(BF16)
+    along = lax.axis_size("z")
     gk, gv, taps, first_rows = call(
         last_kernel, "last", TOGETHER["last"],
         input_specs + rim_specs + [table, table]
         + [pieces, pairs, packs, narrow, narrow, per_head(length)],
-        [narrow, per_head(length), whole(16, VD), whole(2, 2 * keys + values)],
-        [arr(length, keys), arr(length, values), arr(16, VD), arr(2, 2 * keys + values)],
+        [narrow, per_head(length), whole(16 * along, VD), whole(2, 2 * keys + values)],
+        [arr(length, keys), arr(length, values), arr(16 * along, VD), arr(2, 2 * keys + values)],
         4 << 30, buffers,
     )(*inputs, rim, rim, places, factors, k4, vb, after, gq, kd, gv)
     first_rows, mixed = lax.optimization_barrier((first_rows, mixed))
     tail = from_behind(first_rows, SEQ, -1)
-    taps = total_over(taps, "z")
+    taps = lax.all_to_all(taps.reshape(along, 16, VD), "z", 0, 0, tiled=True)
+    taps = jnp.sum(taps, axis=0)
     taps, tail = lax.optimization_barrier((taps, tail))
     grad_query, grad_key, grad_value = call(
         finish_kernel, "finish", TOGETHER["finish"],

time: 204 us -> 203 us (level)
    all_to_all x0 -> x1, waiting for transfers between devices: none -> 5.51 us  [body(): taps = lax.all_to_all(taps.reshape(along, 16, VD), 'z', 0, 0, tiled=True)]
    all_to_all x2 -> x1, waiting for transfers between devices: 7.58 us -> 2.07 us  [to_all(): return lax.all_to_all(copies, axis, 0, 0, tiled=True)]
    all_to_all x0 -> x1, starting transfers between devices: none -> 3.76 us  [body(): taps = lax.all_to_all(taps.reshape(along, 16, VD), 'z', 0, 0, tiled=True)]
    all_to_all x2 -> x1, starting transfers between devices: 10.7 us -> 7.09 us  [to_all(): return lax.all_to_all(copies, axis, 0, 0, tiled=True)]
  transfers between devices with their start and end apart: 14 -> 14, of which waited for: 7 -> 7; matrix products, arithmetic and copies ran while one was open for 9% -> 9% of each run, Pallas kernels for 11% -> 12%
where the time goes in v5:
time: 203 us; the launch traced here: 202 us
  starting transfers between devices  79 us (39%)
  waiting for transfers between devices  63.2 us (31%)
  Pallas kernels  34.3 us (17%)
  local copies, waits for them, and re-layouts  16.2 us (8%)
  matrix products  5.78 us (3%)
  other arithmetic  2.82 us (1%)
    all_to_all x2, waiting for transfers between devices, carried_in(): everyone = lax.all_to_all(packed.reshape(ranks, -1), SEQ, 0, 0, tiled=True)  28.2 us
    all_to_all x2, starting transfers between devices, carried_in(): everyone = lax.all_to_all(packed.reshape(ranks, -1), SEQ, 0, 0, tiled=True)  25.1 us
    all_to_all x2, waiting for transfers between devices, carried_in(): lax.all_to_all(sums, SEQ, 0, 0, tiled=True).reshape(packed.shape)  23.3 us
    ppermute x6, starting transfers between devices, turned(): lax.ppermute(block, axis, [(i, (i + distance) % size) for i in range(size)])  20.4 us
    all_to_all x2, starting transfers between devices, carried_in(): lax.all_to_all(sums, SEQ, 0, 0, tiled=True).reshape(packed.shape)  14 us
    pallas_call x1, Pallas kernels, body(): call(inner_kernel, 'inner', TOGETHER['inner'], [pieces] * 3 + [pairs, pac...  10 us
    ppermute x2, starting transfers between devices, from_behind(): return lax.ppermute(block, axis, route)  8.66 us
    all_to_all x1, starting transfers between devices, to_all(): return lax.all_to_all(copies, axis, 0, 0, tiled=True)  7.09 us
  transfers between devices with their start and end apart: 14, of which 7 were waited for; matrix products, arithmetic and copies ran while one was open for 9% of the time, Pallas kernels for 12%

profile of v5, /device:TPU:1, one launch (start us, length us, event | category | flops | bytes accessed | tf_op | source)
XLA Modules:
  0.0 202.3 jit_solution(5506024584422779591)
XLA Ops:
  0.6 0.0 copy-start
  0.6 1.6 edge.1
  2.3 0.0 copy-start.2
  2.3 5.0 %collective-permute-start = (bf16[16,640]{1,0:T(8,128)(2,1)}, bf16[16,640]{1,0:T(8,128)(2,1)S(1)}, u32[]{:S(2)}, u32[]{:S(2)}) collective-permute-start(bf16[16,640]{1,0:T(8,128)(2,1)} %edge.1), channel_id=1, source_target_pairs={{0,4},{4,8},{8,12},{12,16},{16,20},{20,24},{24,28},{28,32},{32,36}... | collective-permute-start | bytes 61448 | tf_op jit(solution)/shard_map/ppermute | solution.py:346
  7.3 4.1 %collective-permute-done.refs_3_.refs_4_ = bf16[16,640]{1,0:T(8,128)(2,1)S(1)} collective-permute-done((bf16[16,640]{1,0:T(8,128)(2,1)}, bf16[16,640]{1,0:T(8,128)(2,1)S(1)}, u32[]{:S(2)}, u32[]{:S(2)}) %collective-permute-start) | collective-permute-done | bytes 20512 | tf_op jit(solution)/shard_map/ppermute | solution.py:346
  11.4 0.6 copy-done.7
  12.0 4.4 %first.1 = (bf16[512,256]{1,0:T(8,128)(2,1)}, bf16[512,256]{1,0:T(8,128)(2,1)}, bf16[512,256]{1,0:T(8,128)(2,1)}, bf16[512,1024]{1,0:T(8,128)(2,1)}, f32[640,128]{1,0:T(8,128)}) custom-call(bf16[64,512]{1,0:T(8,128)(2,1)} %bitcast.34, bf16[64,512]{1,0:T(8,128)(2,1)} %bitcast.37, bf16[512,512]{1,0:T(8,128)(2,1)} %refs_2_.4, bf16[16,640]{1,0:T(8,128)(2,1)} %copy-done.7, ...), custom_call_target="tpu_custom_call" | custom-call | flops 2147483648 | bytes 4194304 | tf_op jit(solution)/shard_map/first/pallas_call | solution.py:491
  16.4 17.9 %all-to-all-start = ((f32[128,1,640]{2,1,0:T(1,128)}), f32[128,1,640]{2,1,0:T(1,128)S(1)}, u32[]{:S(2)}, u32[]{:S(2)}) async-start(f32[128,1,640]{2,1,0:T(1,128)} %bitcast.27), calls=%async_computation | async-start | bytes 655360 | tf_op jit(solution)/shard_map/all_to_all | solution.py:351
  34.3 0.0 copy-done.2
  34.3 3.2 %collective-permute-start.1 = (bf16[128,2048]{1,0:T(8,128)(2,1)S(1)}, bf16[128,2048]{1,0:T(8,128)(2,1)}, u32[]{:S(2)}, u32[]{:S(2)}) collective-permute-start(bf16[128,2048]{1,0:T(8,128)(2,1)S(1)} %copy-done.2), channel_id=1, source_target_pairs={{0,1},{1,2},{2,3},{3,0},{4,5},{5,6},{6,7},{7,4},{8,9},{9,10},{10,1... | collective-permute-start | bytes 1572872 | tf_op jit(solution)/shard_map/ppermute | solution.py:363
  37.5 3.4 %collective-permute-start.3 = (bf16[128,2048]{1,0:T(8,128)(2,1)S(1)}, bf16[128,2048]{1,0:T(8,128)(2,1)S(1)}, u32[]{:S(2)}, u32[]{:S(2)}) collective-permute-start(bf16[128,2048]{1,0:T(8,128)(2,1)S(1)} %copy-done.2), channel_id=1, source_target_pairs={{0,3},{1,0},{2,1},{3,2},{4,7},{5,4},{6,5},{7,6},{8,11},{9,8},{10,9... | collective-permute-start | bytes 1572872 | tf_op jit(solution)/shard_map/ppermute | solution.py:363
  40.9 3.5 %collective-permute-start.2 = (bf16[128,2048]{1,0:T(8,128)(2,1)S(1)}, bf16[128,2048]{1,0:T(8,128)(2,1)}, u32[]{:S(2)}, u32[]{:S(2)}) collective-permute-start(bf16[128,2048]{1,0:T(8,128)(2,1)S(1)} %copy-done.2), channel_id=1, source_target_pairs={{0,2},{1,3},{2,0},{3,1},{4,6},{5,7},{6,4},{7,5},{8,10},{9,11},{10,... | collective-permute-start | bytes 1572872 | tf_op jit(solution)/shard_map/ppermute | solution.py:363
  44.5 1.6 broadcast_in_dim.4
  46.1 0.8 constant_dynamic-update-slice_fusion.3
  47.0 12.7 %all-to-all-done = f32[128,1,640]{2,1,0:T(1,128)S(1)} async-done(((f32[128,1,640]{2,1,0:T(1,128)}), f32[128,1,640]{2,1,0:T(1,128)S(1)}, u32[]{:S(2)}, u32[]{:S(2)}) %all-to-all-start) | async-done | bytes 327712 | tf_op jit(solution)/shard_map/all_to_all | solution.py:351
  59.7 0.3 convolution_bitcast_fusion
  60.0 1.1 copy.23
  61.1 7.0 %all-to-all-start.1 = ((f32[128,1,640]{2,1,0:T(1,128)}), f32[128,1,640]{2,1,0:T(1,128)S(1)}, u32[]{:S(2)}, u32[]{:S(2)}) async-start(f32[128,1,640]{2,1,0:T(1,128)} %copy.23), calls=%async_computation.1 | async-start | bytes 655360 | tf_op jit(solution)/shard_map/all_to_all | solution.py:358
  68.1 4.5 %local.1 = (f32[512,512]{1,0:T(8,128)}, f32[512,512]{1,0:T(8,128)}) custom-call(bf16[512,256]{1,0:T(8,128)(2,1)} %get-tuple-element.38.refs_0_, bf16[512,256]{1,0:T(8,128)(2,1)} %get-tuple-element.40.refs_1_.refs_2_, bf16[512,1024]{1,0:T(8,128)(2,1)} %get-tuple-element.37.refs_2_.refs_3_.refs_8_), custom_call_target="tpu_custom_call" | custom-call | flops 4294967296 | bytes 4194304 | tf_op jit(solution)/shard_map/local/pallas_call | solution.py:498
  72.5 0.0 collective-permute-done.1
  72.5 1.9 constant_dynamic-update-slice_fusion.2
  74.4 0.0 collective-permute-done.2
  74.4 1.9 constant_dynamic-update-slice_fusion.1
  76.3 0.0 collective-permute-done.3
  76.3 0.9 constant_dynamic-update-slice_fusion
  77.2 0.0 copy-done
  77.2 3.9 %fusion.6.refs_4_ = f32[512,512]{1,0:T(8,128)} fusion(bf16[512,2048]{1,0:T(8,128)(2,1)} %constant_dynamic-update-slice_fusion, bf16[512,2048]{1,0:T(8,128)(2,1)S(1)} %copy-done), kind=kOutput, calls=%fused_computation.17 | convolution fusion | flops 1073741824 | bytes 5242880 | tf_op jit(solution)/shard_map/dot_general | solution.py:495
  81.1 12.5 %all-to-all-done.1 = f32[128,1,640]{2,1,0:T(1,128)S(1)} async-done(((f32[128,1,640]{2,1,0:T(1,128)}), f32[128,1,640]{2,1,0:T(1,128)S(1)}, u32[]{:S(2)}, u32[]{:S(2)}) %all-to-all-start.1) | async-done | bytes 327712 | tf_op jit(solution)/shard_map/all_to_all | solution.py:358
  93.6 0.7 copy-done.5
  94.3 5.0 %middle.1 = (bf16[512,512]{1,0:T(8,128)(2,1)}, f32[512,512]{1,0:T(8,128)}, f32[512,512]{1,0:T(8,128)}, f32[640,128]{1,0:T(8,128)}) custom-call(bf16[512,256]{1,0:T(8,128)(2,1)} %get-tuple-element.38.refs_0_, f32[640,128]{1,0:T(8,128)} %bitcast.29, f32[512,512]{1,0:T(8,128)} %get-tuple-element.41.refs_2_, f32[512,512]{1,0:T(8,128)} %get-tuple-element.42.refs_3_, ...), custom_call_target="tpu_custom_call" | custom-call | flops 4294967296 | bytes 4194304 | tf_op jit(solution)/shard_map/middle/pallas_call | solution.py:503
  99.3 7.2 %all-to-all-start.2 = ((f32[128,1,640]{2,1,0:T(1,128)}), f32[128,1,640]{2,1,0:T(1,128)S(1)}, u32[]{:S(2)}, u32[]{:S(2)}) async-start(f32[128,1,640]{2,1,0:T(1,128)} %bitcast.31), calls=%async_computation.2 | async-start | bytes 655360 | tf_op jit(solution)/shard_map/all_to_all | solution.py:351
  106.4 10.0 %inner.1 = (f32[512,64]{1,0:T(8,128)}, f32[512,64]{1,0:T(8,128)}, f32[512,512]{1,0:T(8,128)}) custom-call(bf16[512,256]{1,0:T(8,128)(2,1)} %get-tuple-element.38.refs_0_, bf16[512,256]{1,0:T(8,128)(2,1)} %get-tuple-element.36.refs_1_.refs_7_, bf16[512,256]{1,0:T(8,128)(2,1)} %get-tuple-element.40.refs_1_.refs_2_, ...), custom_call_target="tpu_custom_call" | custom-call | flops 8589934592 | bytes 4194304 | tf_op jit(solution)/shard_map/inner/pallas_call | solution.py:511
  116.5 15.5 %all-to-all-done.2 = f32[128,1,640]{2,1,0:T(1,128)S(1)} async-done(((f32[128,1,640]{2,1,0:T(1,128)}), f32[128,1,640]{2,1,0:T(1,128)S(1)}, u32[]{:S(2)}, u32[]{:S(2)}) %all-to-all-start.2) | async-done | bytes 327712 | tf_op jit(solution)/shard_map/all_to_all | solution.py:351
  131.9 0.3 fusion
  132.2 1.1 copy.25
  133.3 7.0 %all-to-all-start.3 = ((f32[128,1,640]{2,1,0:T(1,128)}), f32[128,1,640]{2,1,0:T(1,128)S(1)}, u32[]{:S(2)}, u32[]{:S(2)}) async-start(f32[128,1,640]{2,1,0:T(1,128)} %copy.25), calls=%async_computation.3 | async-start | bytes 655360 | tf_op jit(solution)/shard_map/all_to_all | solution.py:358
  140.4 0.0 copy-done.3
  140.4 1.3 fusion.7
  141.6 0.0 copy-start.1
  141.6 2.0 copy-done.1
  143.6 1.0 dynamic-slice_convert_fusion.2
  144.6 3.2 %collective-permute-start.4 = (bf16[128,2048]{1,0:T(8,128)(2,1)}, bf16[128,2048]{1,0:T(8,128)(2,1)}, u32[]{:S(2)}, u32[]{:S(2)}) collective-permute-start(bf16[128,2048]{1,0:T(8,128)(2,1)} %get-tuple-element.65), channel_id=1, source_target_pairs={{0,1},{1,2},{2,3},{3,0},{4,5},{5,6},{6,7},{7,4},{8,9},{9,10},{10,1... | collective-permute-start | bytes 1572872 | tf_op jit(solution)/shard_map/ppermute | solution.py:363
  147.8 3.4 %collective-permute-start.6 = (bf16[128,2048]{1,0:T(8,128)(2,1)S(1)}, bf16[128,2048]{1,0:T(8,128)(2,1)}, u32[]{:S(2)}, u32[]{:S(2)}) collective-permute-start(bf16[128,2048]{1,0:T(8,128)(2,1)S(1)} %get-tuple-element.66), channel_id=1, source_target_pairs={{0,3},{1,0},{2,1},{3,2},{4,7},{5,4},{6,5},{7,6},{8,11},{9,8},{10,9... | collective-permute-start | bytes 1572872 | tf_op jit(solution)/shard_map/ppermute | solution.py:363
  151.2 3.8 %collective-permute-start.5 = (bf16[128,2048]{1,0:T(8,128)(2,1)S(1)}, bf16[128,2048]{1,0:T(8,128)(2,1)}, u32[]{:S(2)}, u32[]{:S(2)}) collective-permute-start(bf16[128,2048]{1,0:T(8,128)(2,1)S(1)} %get-tuple-element.67), channel_id=1, source_target_pairs={{0,2},{1,3},{2,0},{3,1},{4,6},{5,7},{6,4},{7,5},{8,10},{9,11},{10,... | collective-permute-start | bytes 1572872 | tf_op jit(solution)/shard_map/ppermute | solution.py:363
  155.0 10.8 %all-to-all-done.3 = f32[128,1,640]{2,1,0:T(1,128)S(1)} async-done(((f32[128,1,640]{2,1,0:T(1,128)}), f32[128,1,640]{2,1,0:T(1,128)S(1)}, u32[]{:S(2)}, u32[]{:S(2)}) %all-to-all-start.3) | async-done | bytes 327712 | tf_op jit(solution)/shard_map/all_to_all | solution.py:358
  165.8 0.8 copy-done.4
  166.6 6.1 %last.1 = (f32[512,64]{1,0:T(8,128)}, f32[512,512]{1,0:T(8,128)}, f32[256,128]{1,0:T(8,128)}, f32[2,640]{1,0:T(2,128)}) custom-call(bf16[64,512]{1,0:T(8,128)(2,1)} %bitcast.35, bf16[64,512]{1,0:T(8,128)(2,1)} %bitcast.38, bf16[512,512]{1,0:T(8,128)(2,1)} %refs_2_.4, bf16[16,640]{1,0:T(8,128)(2,1)} %copy-done.7, bf16[16,640]{1,0:T(8,128)(2,1)} %copy-done.7, ...), custom_call_target="tpu_custom_call" | custom-call | flops 4294967296 | bytes 4194304 | tf_op jit(solution)/shard_map/last/pallas_call | solution.py:522
  172.7 3.8 %all-to-all-start.4 = ((f32[16,16,128]{2,1,0:T(8,128)}), f32[16,16,128]{2,1,0:T(8,128)S(1)}, u32[]{:S(2)}, u32[]{:S(2)}) async-start(f32[16,16,128]{2,1,0:T(8,128)} %bitcast.32), calls=%async_computation.4 | async-start | bytes 262144 | tf_op jit(solution)/shard_map/all_to_all | solution.py:532
  176.4 0.0 collective-permute-done.4
  176.4 0.0 collective-permute-done.6
  176.4 0.0 collective-permute-done.5
  176.5 2.8 %add_convert_fusion = bf16[128,2048]{1,0:T(8,128)(2,1)} fusion(bf16[128,2048]{1,0:T(8,128)(2,1)} %collective-permute-done.6, bf16[128,2048]{1,0:T(8,128)(2,1)} %collective-permute-done.5, bf16[128,2048]{1,0:T(8,128)(2,1)} %collective-permute-done.4, f32[512,2048]{1,0:T(8,128)} %copy-done.1, s32[]{:T(128)S(6)} %select_n.63), kind=kLoop, calls=%fused_computation.1 | loop fusion | flops 1835008 | bytes 3145732 | tf_op jit(solution)/shard_map/convert_element_type | solution.py:520
  179.2 0.0 copy-done.8
  179.3 3.6 %collective-permute-start.7 = (f32[2,640]{1,0:T(2,128)S(1)}, f32[2,640]{1,0:T(2,128)S(1)}, u32[]{:S(2)}, u32[]{:S(2)}) collective-permute-start(f32[2,640]{1,0:T(2,128)S(1)} %copy-done.8), channel_id=1, source_target_pairs={{4,0},{8,4},{12,8},{16,12},{20,16},{24,20},{28,24},{32,28},{36,32}... | collective-permute-start | bytes 15368 | tf_op jit(solution)/shard_map/ppermute | solution.py:346
  182.9 5.5 %all-to-all-done.4 = f32[16,16,128]{2,1,0:T(8,128)S(1)} async-done(((f32[16,16,128]{2,1,0:T(8,128)}), f32[16,16,128]{2,1,0:T(8,128)S(1)}, u32[]{:S(2)}, u32[]{:S(2)}) %all-to-all-start.4) | async-done | bytes 131104 | tf_op jit(solution)/shard_map/all_to_all | solution.py:532
  188.4 0.0 collective-permute-done.7.refs_0_.refs_1_
  188.4 0.0 copy-start.6
  188.4 0.6 broadcast_in_dim.10
  189.1 7.1 %all-to-all-start.5 = ((f32[8,16,128]{2,1,0:T(8,128)}), f32[8,16,128]{2,1,0:T(8,128)S(1)}, u32[]{:S(2)}, u32[]{:S(2)}) async-start(f32[8,16,128]{2,1,0:T(8,128)} %broadcast_in_dim.10), calls=%async_computation.5 | async-start | bytes 131072 | tf_op jit(solution)/shard_map/all_to_all | solution.py:389
  196.2 0.0 copy-done.6
  196.2 2.8 %finish.1 = (f32[64,512]{1,0:T(8,128)}, f32[64,512]{1,0:T(8,128)}, f32[512,512]{1,0:T(8,128)}) custom-call(f32[2,640]{1,0:T(2,128)} %copy-done.6, f32[2,640]{1,0:T(2,128)} %copy-done.6, f32[3,64]{1,0:T(4,128)} %refs_2_.5, f32[3,64]{1,0:T(4,128)} %refs_3_.1, f32[3,512]{1,0:T(4,128)} %refs_4_.1, f32[512,64]{1,0:T(8,128)} %get-tuple-element.50.refs_10_.refs_5_, ...), custom_call_target="tpu_custom_call" | custom-call | flops 16777216 | bytes 4194304 | tf_op jit(solution)/shard_map/finish/pallas_call | solution.py:535
  198.9 2.1 %all-to-all-done.5 = f32[8,16,128]{2,1,0:T(8,128)S(1)} async-done(((f32[8,16,128]{2,1,0:T(8,128)}), f32[8,16,128]{2,1,0:T(8,128)S(1)}, u32[]{:S(2)}, u32[]{:S(2)}) %all-to-all-start.5) | async-done | bytes 65568 | tf_op jit(solution)/shard_map/all_to_all | solution.py:389
  201.0 0.7 fusion.5
  201.7 0.6 reshape.47
  (7 shorter events, 0.0 us)
Async XLA Ops:
  0.6 76.6 %copy-start = (bf16[512,2048]{1,0:T(8,128)(2,1)S(1)}, bf16[512,2048]{1,0:T(8,128)(2,1)}, u32[]{:S(2)}) copy-start(bf16[512,2048]{1,0:T(8,128)(2,1)} %param.16) | copy-start | bytes 6291460
  2.3 32.1 %copy-start.2 = (bf16[128,2048]{1,0:T(8,128)(2,1)S(1)}, bf16[128,2048]{1,0:T(8,128)(2,1)}, u32[]{:S(2)}) copy-start(bf16[128,2048]{1,0:T(8,128)(2,1)} %param.17) | copy-start | bytes 1572868
  2.3 9.1 %collective-permute-start = (bf16[16,640]{1,0:T(8,128)(2,1)}, bf16[16,640]{1,0:T(8,128)(2,1)S(1)}, u32[]{:S(2)}, u32[]{:S(2)}) collective-permute-start(bf16[16,640]{1,0:T(8,128)(2,1)} %edge.1), channel_id=1, source_target_pairs={{0,4},{4,8},{8,12},{12,16},{16,20},{20,24},{24,28},{28,32},{32,36}... | collective-permute-start | bytes 61448 | tf_op jit(solution)/shard_map/ppermute | solution.py:346
  11.4 0.6 copy-start.7
  16.4 43.3 %all-to-all-start = ((f32[128,1,640]{2,1,0:T(1,128)}), f32[128,1,640]{2,1,0:T(1,128)S(1)}, u32[]{:S(2)}, u32[]{:S(2)}) async-start(f32[128,1,640]{2,1,0:T(1,128)} %bitcast.27), calls=%async_computation | async-start | bytes 655360 | tf_op jit(solution)/shard_map/all_to_all | solution.py:351
  34.3 38.2 %collective-permute-start.1 = (bf16[128,2048]{1,0:T(8,128)(2,1)S(1)}, bf16[128,2048]{1,0:T(8,128)(2,1)}, u32[]{:S(2)}, u32[]{:S(2)}) collective-permute-start(bf16[128,2048]{1,0:T(8,128)(2,1)S(1)} %copy-done.2), channel_id=1, source_target_pairs={{0,1},{1,2},{2,3},{3,0},{4,5},{5,6},{6,7},{7,4},{8,9},{9,10},{10,1... | collective-permute-start | bytes 1572872 | tf_op jit(solution)/shard_map/ppermute | solution.py:363
  37.5 38.8 %collective-permute-start.3 = (bf16[128,2048]{1,0:T(8,128)(2,1)S(1)}, bf16[128,2048]{1,0:T(8,128)(2,1)S(1)}, u32[]{:S(2)}, u32[]{:S(2)}) collective-permute-start(bf16[128,2048]{1,0:T(8,128)(2,1)S(1)} %copy-done.2), channel_id=1, source_target_pairs={{0,3},{1,0},{2,1},{3,2},{4,7},{5,4},{6,5},{7,6},{8,11},{9,8},{10,9... | collective-permute-start | bytes 1572872 | tf_op jit(solution)/shard_map/ppermute | solution.py:363
  40.9 33.5 %collective-permute-start.2 = (bf16[128,2048]{1,0:T(8,128)(2,1)S(1)}, bf16[128,2048]{1,0:T(8,128)(2,1)}, u32[]{:S(2)}, u32[]{:S(2)}) collective-permute-start(bf16[128,2048]{1,0:T(8,128)(2,1)S(1)} %copy-done.2), channel_id=1, source_target_pairs={{0,2},{1,3},{2,0},{3,1},{4,6},{5,7},{6,4},{7,5},{8,10},{9,11},{10,... | collective-permute-start | bytes 1572872 | tf_op jit(solution)/shard_map/ppermute | solution.py:363
  61.1 32.5 %all-to-all-start.1 = ((f32[128,1,640]{2,1,0:T(1,128)}), f32[128,1,640]{2,1,0:T(1,128)S(1)}, u32[]{:S(2)}, u32[]{:S(2)}) async-start(f32[128,1,640]{2,1,0:T(1,128)} %copy.23), calls=%async_computation.1 | async-start | bytes 655360 | tf_op jit(solution)/shard_map/all_to_all | solution.py:358
  93.6 0.7 copy-start.5
  99.3 32.7 %all-to-all-start.2 = ((f32[128,1,640]{2,1,0:T(1,128)}), f32[128,1,640]{2,1,0:T(1,128)S(1)}, u32[]{:S(2)}, u32[]{:S(2)}) async-start(f32[128,1,640]{2,1,0:T(1,128)} %bitcast.31), calls=%async_computation.2 | async-start | bytes 655360 | tf_op jit(solution)/shard_map/all_to_all | solution.py:351
  116.4 23.9 %copy-start.3 = (bf16[512,512]{1,0:T(8,128)(2,1)S(1)}, bf16[512,512]{1,0:T(8,128)(2,1)}, u32[]{:S(2)}) copy-start(bf16[512,512]{1,0:T(8,128)(2,1)} %get-tuple-element.54) | copy-start | bytes 1572868
  133.3 32.5 %all-to-all-start.3 = ((f32[128,1,640]{2,1,0:T(1,128)}), f32[128,1,640]{2,1,0:T(1,128)S(1)}, u32[]{:S(2)}, u32[]{:S(2)}) async-start(f32[128,1,640]{2,1,0:T(1,128)} %copy.25), calls=%async_computation.3 | async-start | bytes 655360 | tf_op jit(solution)/shard_map/all_to_all | solution.py:358
  141.6 2.0 copy-start.1
  144.6 31.8 %collective-permute-start.4 = (bf16[128,2048]{1,0:T(8,128)(2,1)}, bf16[128,2048]{1,0:T(8,128)(2,1)}, u32[]{:S(2)}, u32[]{:S(2)}) collective-permute-start(bf16[128,2048]{1,0:T(8,128)(2,1)} %get-tuple-element.65), channel_id=1, source_target_pairs={{0,1},{1,2},{2,3},{3,0},{4,5},{5,6},{6,7},{7,4},{8,9},{9,10},{10,1... | collective-permute-start | bytes 1572872 | tf_op jit(solution)/shard_map/ppermute | solution.py:363
  147.8 28.6 %collective-permute-start.6 = (bf16[128,2048]{1,0:T(8,128)(2,1)S(1)}, bf16[128,2048]{1,0:T(8,128)(2,1)}, u32[]{:S(2)}, u32[]{:S(2)}) collective-permute-start(bf16[128,2048]{1,0:T(8,128)(2,1)S(1)} %get-tuple-element.66), channel_id=1, source_target_pairs={{0,3},{1,0},{2,1},{3,2},{4,7},{5,4},{6,5},{7,6},{8,11},{9,8},{10,9... | collective-permute-start | bytes 1572872 | tf_op jit(solution)/shard_map/ppermute | solution.py:363
  151.2 25.3 %collective-permute-start.5 = (bf16[128,2048]{1,0:T(8,128)(2,1)S(1)}, bf16[128,2048]{1,0:T(8,128)(2,1)}, u32[]{:S(2)}, u32[]{:S(2)}) collective-permute-start(bf16[128,2048]{1,0:T(8,128)(2,1)S(1)} %get-tuple-element.67), channel_id=1, source_target_pairs={{0,2},{1,3},{2,0},{3,1},{4,6},{5,7},{6,4},{7,5},{8,10},{9,11},{10,... | collective-permute-start | bytes 1572872 | tf_op jit(solution)/shard_map/ppermute | solution.py:363
  165.8 0.8 copy-start.4
  172.7 6.6 %copy-start.8 = (f32[2,640]{1,0:T(2,128)S(1)}, f32[2,640]{1,0:T(2,128)}, u32[]{:S(2)}) copy-start(f32[2,640]{1,0:T(2,128)} %get-tuple-element.57) | copy-start | bytes 15364
  172.7 15.7 %all-to-all-start.4 = ((f32[16,16,128]{2,1,0:T(8,128)}), f32[16,16,128]{2,1,0:T(8,128)S(1)}, u32[]{:S(2)}, u32[]{:S(2)}) async-start(f32[16,16,128]{2,1,0:T(8,128)} %bitcast.32), calls=%async_computation.4 | async-start | bytes 262144 | tf_op jit(solution)/shard_map/all_to_all | solution.py:532
  179.3 9.2 %collective-permute-start.7 = (f32[2,640]{1,0:T(2,128)S(1)}, f32[2,640]{1,0:T(2,128)S(1)}, u32[]{:S(2)}, u32[]{:S(2)}) collective-permute-start(f32[2,640]{1,0:T(2,128)S(1)} %copy-done.8), channel_id=1, source_target_pairs={{4,0},{8,4},{12,8},{16,12},{20,16},{24,20},{28,24},{32,28},{36,32}... | collective-permute-start | bytes 15368 | tf_op jit(solution)/shard_map/ppermute | solution.py:346
  188.4 7.7 %copy-start.6 = (f32[2,640]{1,0:T(2,128)}, f32[2,640]{1,0:T(2,128)S(1)}, u32[]{:S(2)}) copy-start(f32[2,640]{1,0:T(2,128)S(1)} %collective-permute-done.7.refs_0_.refs_1_) | copy-start | bytes 15364
  189.1 11.9 %all-to-all-start.5 = ((f32[8,16,128]{2,1,0:T(8,128)}), f32[8,16,128]{2,1,0:T(8,128)S(1)}, u32[]{:S(2)}, u32[]{:S(2)}) async-start(f32[8,16,128]{2,1,0:T(8,128)} %broadcast_in_dim.10), calls=%async_computation.5 | async-start | bytes 131072 | tf_op jit(solution)/shard_map/all_to_all | solution.py:389
